TPU v7x, 32 devices: a whole 2x2x4 slice. The times are simulated.
32 devices in a mesh: parts: 2 (over y), tm: 8 (over z, x), band: 2 (over core).
Axes of the slice: x: 2, y: 2, z: 4, core: 2. Of those that a mesh axis runs over, the one named last changes fastest.
Arguments:
- query_tokens: bfloat16 [16, 8, 32, 2240], P(('parts', 'tm'), 'band'), parts along dimension 0, may hold values from -6 to 6
- key_tokens: bfloat16 [16, 8, 32, 2240], P(('parts', 'tm'), 'band'), parts along dimension 0, may hold values from -6 to 6
- value_tokens: bfloat16 [16, 8, 32, 2240], P(('parts', 'tm'), 'band'), parts along dimension 0, may hold values from -14 to 14
- norm_gain: float32 [2240], replicated, may hold values from 0.1 to 1.9
- out_weight: bfloat16 [2, 8, 313600], P('band', 'tm'), may hold values from -0.125 to 0.125
Outputs:
- block_out: bfloat16 [16, 8, 32, 2240], P(('parts', 'tm'), 'band'), parts along dimension 0
There are 2 independent parts, one for each index of `parts`. A program takes and returns all parts, laid end to end along the dimension named above; an argument that names none is the same for every part. Nothing has to cross between parts.
All inputs are finite; a program needn't handle non-finite values.
Results may differ from a plain program's by a relative error of at most 0.0049.
Values may be sent and summed in bfloat16 or wider, within the bound.
No kernel may reach another device: no remote copies, remote signals or barrier semaphores. Data moves between devices by JAX's collectives and lax.ppermute only.
A program may use at most 128 MiB of HBM per device.

v0:
```python
import functools

import jax
import jax.numpy as jnp
from jax import lax
from jax.experimental import pallas as pl
from jax.experimental.pallas import tpu as pltpu
from jax.sharding import PartitionSpec as P


HEADS = 70
HD = 32
LANES = 128

norm_epsilon = 1e-06
read_epsilon = 1e-06


def round_up(n, m):
    return -(-n // m) * m


def call(kernel, out, args, scratch=(), flops=0, smem=0, mib=16):
    whole = pl.BlockSpec(memory_space=pltpu.VMEM)
    scalar = pl.BlockSpec(memory_space=pltpu.SMEM)
    moved = sum(a.size * a.dtype.itemsize for a in jax.tree.leaves((args, out)))
    return pl.pallas_call(
        kernel,
        out_shape=out,
        in_specs=[scalar] * smem + [whole] * (len(args) - smem),
        out_specs=jax.tree.map(lambda _: whole, out),
        scratch_shapes=list(scratch),
        compiler_params=pltpu.CompilerParams(vmem_limit_bytes=mib * 1024 * 1024),
        cost_estimate=pl.CostEstimate(flops=flops, bytes_accessed=moved, transcendentals=0),
    )(*args)


def shape(dims, dtype):
    return jax.ShapeDtypeStruct(tuple(dims), dtype)


def unpack_weight(rows, depth, at_ref, w_ref, mine_ref, rest_ref, tall):
    half = mine_ref.shape[1]
    tall[pl.ds(rows // 8 * 8, tall.shape[0] - rows // 8 * 8), :] = jnp.zeros(
        (tall.shape[0] - rows // 8 * 8, tall.shape[1]), jnp.float32
    )
    edge = depth // LANES * LANES
    tall[:, pl.ds(edge, tall.shape[1] - edge)] = jnp.zeros(
        (tall.shape[0], tall.shape[1] - edge), jnp.float32
    )
    for r in range(rows):
        tall[r : r + 1, 0:depth] = w_ref[0, :, depth * r : depth * (r + 1)].astype(jnp.float32)
    y = at_ref[0]
    mine_ref[...] = tall[:, pl.ds(pl.multiple_of(y * half, LANES), half)].astype(jnp.bfloat16)
    rest_ref[...] = tall[:, pl.ds(pl.multiple_of((1 - y) * half, LANES), half)].astype(jnp.bfloat16)


def head_mask():
    row = lax.broadcasted_iota(jnp.int32, (LANES, LANES), 0) // HD
    lane = lax.broadcasted_iota(jnp.int32, (LANES, LANES), 1) // HD
    return row == lane


def state_sums(half, at_ref, k_ref, v_ref, own_ref, other_ref, sums):
    depth = k_ref.shape[1]
    mask = head_mask()
    sums[...] = jnp.zeros_like(sums)
    for start in range(0, depth, LANES):
        n = min(LANES, depth - start)
        keys = jnp.maximum(k_ref[:, start : start + n], 0)
        values = v_ref[:, start : start + n]
        outer = lax.dot_general(
            values, keys, (((0,), (0,)), ((), ())), preferred_element_type=jnp.float32
        )
        outer = jnp.where(mask[:n, :n], outer, 0.0)
        folded = sum(outer[i : i + HD] for i in range(0, n, HD))
        sums[0:HD, start : start + n] = folded
        sums[HD : HD + 1, start : start + n] = jnp.sum(
            keys.astype(jnp.float32), axis=0, keepdims=True
        )
    own_ref[...] = jnp.zeros_like(own_ref)
    other_ref[...] = jnp.zeros_like(other_ref)

    @pl.when(at_ref[1] == 0)
    def _():
        own_ref[:, 0:half] = sums[:, 0:half]
        other_ref[:, 0:half] = sums[:, half : 2 * half]

    @pl.when(at_ref[1] != 0)
    def _():
        own_ref[:, 0:half] = sums[:, half : 2 * half]
        other_ref[:, 0:half] = sums[:, 0:half]


def read_states(half, shard, slots, at_ref, q_ref, p_ref, s_ref, g_ref, left_ref, square_ref, qh, gh, flat, blocks):
    count = q_ref.shape[0]
    qh[...] = jnp.zeros_like(qh)
    gh[...] = jnp.zeros_like(gh)

    def take(first):
        qh[0:count, 0:half] = q_ref[:, first : first + half]
        qh[count : 2 * count, 0:half] = p_ref[:, first : first + half]
        gh[:, 0:half] = g_ref[:, first : first + half]

    @pl.when(at_ref[1] == 0)
    def _():
        take(0)

    @pl.when(at_ref[1] != 0)
    def _():
        take(half)

    mask = head_mask()
    square = jnp.zeros((2 * count, LANES), jnp.float32)
    for start in range(0, qh.shape[1], LANES):
        query = jnp.maximum(qh[:, start : start + LANES], 0)
        state = s_ref[0:HD, start : start + LANES]
        total = s_ref[HD : HD + 1, start : start + LANES]
        spread = jnp.concatenate(
            [
                jnp.where(mask, jnp.concatenate([state] * (LANES // HD), axis=0), 0.0),
                jnp.where(mask, jnp.broadcast_to(total, (LANES, LANES)), 0.0),
            ],
            axis=0,
        )
        high = spread.astype(jnp.bfloat16)
        low = (spread - high.astype(jnp.float32)).astype(jnp.bfloat16)
        both = lax.dot_general(
            jnp.concatenate([query, query], axis=1),
            jnp.concatenate([high, low], axis=1),
            (((1,), (1,)), ((), ())),
            preferred_element_type=jnp.float32,
        )
        reads = both[:, 0:LANES] / (both[:, LANES : 2 * LANES] + read_epsilon)
        square += reads * reads
        flat[:, start : start + LANES] = (reads * gh[:, start : start + LANES]).astype(jnp.bfloat16)
    square_ref[...] = jnp.broadcast_to(
        jnp.sum(square, axis=1, keepdims=True), square_ref.shape
    )
    wide = left_ref.shape[1] // slots
    blocks[...] = jnp.zeros_like(blocks)
    for t in range(slots):
        blocks[t, :, 0:shard] = flat[:, shard * t : shard * (t + 1)]
    me = at_ref[2]
    for m in range(slots):
        left_ref[:, wide * m : wide * (m + 1)] = blocks[me ^ m]


def project(first, last, sides, spare, at_ref, left_ref, square_ref, *refs):
    refs = list(refs)
    out_ref = refs.pop()
    pieces = [[refs.pop(0) for _ in slots] for slots in sides]
    base = refs.pop(0) if refs else None
    wide = pieces[0][0].shape[0] if pieces[0] else pieces[1][0].shape[0]
    for i, slots in enumerate(sides):
        weight = jnp.concatenate([p[...] for p in pieces[i]], axis=0)
        left = jnp.concatenate(
            [left_ref[first:last, wide * m : wide * (m + 1)] for m in slots], axis=1
        )
        total = jnp.dot(left, weight, preferred_element_type=jnp.float32)
        out_ref[i] = total if base is None else total + base[i, first:last]
    if base is not None:
        tail = 1 - at_ref[0]
        lane = lax.broadcasted_iota(jnp.int32, (last - first, LANES), 1)
        cut = spare // LANES * LANES
        out_ref[tail, :, cut : cut + LANES] = jnp.where(
            lane == spare % LANES, square_ref[first:last], out_ref[tail, :, cut : cut + LANES]
        )


def finish(depth, spare, at_ref, own_ref, got_ref, out_ref):
    half = own_ref.shape[2]
    first, last = at_ref[0], 1 - at_ref[0]
    right = own_ref[last] + got_ref[last]
    scale = lax.rsqrt(right[:, spare : spare + 1] / depth + norm_epsilon)
    out_ref[:, half:depth] = (right[:, : depth - half] * scale).astype(jnp.bfloat16)
    out_ref[:, 0:half] = ((own_ref[first] + got_ref[first]) * scale).astype(jnp.bfloat16)


def fast(query_tokens, key_tokens, value_tokens, norm_gain, out_weight):
    frames, rows, width, depth = query_tokens.shape
    count = rows * width
    bands, peers = lax.axis_size("band"), lax.axis_size("tm")
    half = depth // bands
    wide = round_up(half, LANES)
    shard = out_weight.shape[-1] // depth
    tall = round_up(shard, 16)
    cols = round_up(depth, 2 * LANES) // 2
    spare = depth - cols
    swap = [(0, 1), (1, 0)]

    def flip(x, mask):
        return lax.ppermute(x, "tm", [(i, i ^ mask) for i in range(peers)])

    def across(x, axis):
        return lax.ppermute(x, axis, swap)

    at = jnp.stack(
        [lax.axis_index("parts"), lax.axis_index("band"), lax.axis_index("tm")]
    ).astype(jnp.int32)
    bf16, f32 = jnp.bfloat16, jnp.float32

    mine, rest = {}, {}
    mine[0], rest[0] = call(
        functools.partial(unpack_weight, shard, depth),
        (shape((tall, cols), bf16), shape((tall, cols), bf16)),
        (at, out_weight),
        scratch=[pltpu.VMEM((tall, 2 * cols), f32)],
        smem=1,
    )
    far = range(2, peers, 2)
    for m in far:
        mine[m] = flip(mine[0], m)
    mine[1], rest[1] = flip(mine[0], 1), flip(rest[0], 1)
    for m in far:
        mine[m + 1] = flip(mine[m], 1)
        rest[m] = across(mine[m], "parts")
    for m in far:
        if m == 2:
            rest[m + 1] = flip(rest[m], 1)
        else:
            rest[m + 1] = across(mine[m + 1], "parts")

    queries = query_tokens.reshape(count, depth)
    partner = across(query_tokens, "band").reshape(count, depth)
    own, other = call(
        functools.partial(state_sums, half),
        (shape((HD + 8, wide), f32), shape((HD + 8, wide), f32)),
        (at, key_tokens.reshape(count, depth), value_tokens.reshape(count, depth)),
        scratch=[pltpu.VMEM((HD + 8, round_up(depth, LANES)), f32)],
        smem=1,
        flops=2 * count * LANES * depth,
    )
    total = own + across(other, "band")
    prefix = total
    step = 0
    while 1 << step < peers:
        got = flip(total, 1 << step)
        prefix = prefix + jnp.where((at[2] & (1 << step)) != 0, got, 0.0)
        total = total + got
        step += 1
    left, square = call(
        functools.partial(read_states, half, shard, peers),
        (shape((2 * count, peers * tall), bf16), shape((2 * count, LANES), f32)),
        (at, queries, partner, prefix, norm_gain.reshape(1, depth)),
        scratch=[
            pltpu.VMEM((2 * count, wide), bf16),
            pltpu.VMEM((1, wide), f32),
            pltpu.VMEM((2 * count, wide), bf16),
            pltpu.VMEM((peers, 2 * count, tall), bf16),
        ],
        smem=1,
        flops=8 * count * LANES * wide,
    )

    def partial_sums(first, last, slots, base):
        sides = ((slots[0], mine), (slots[1], rest))
        pieces = [held[m] for chosen, held in sides for m in chosen]
        return call(
            functools.partial(project, first, last, slots, spare),
            shape((2, last - first, cols), f32),
            (at, left, square, *pieces, *base),
            smem=1,
            flops=2 * (last - first) * cols * tall * len(pieces),
        )

    late = ((peers - 1,), (peers - 2, peers - 1))
    soon = tuple(tuple(m for m in range(peers) if m not in side) for side in late)
    base = partial_sums(0, 2 * count, soon, ())
    other = partial_sums(count, 2 * count, late, (base,))
    own = partial_sums(0, count, late, (base,))
    out = call(
        functools.partial(finish, depth, spare),
        shape((count, depth), bf16),
        (at, own, across(other, "band")),
        smem=1,
    )
    return out.reshape(frames, rows, width, depth)


def entering(x, axis, combine, identity):
    peers, place = (lax.axis_size(axis), lax.axis_index(axis))
    everything = jax.tree.map(lambda part: lax.all_gather(part, axis), x)
    start = jax.tree.map(
        lambda part, zero: jnp.broadcast_to(jnp.asarray(zero, part.dtype), part.shape), x, identity
    )

    def hop(k, before):
        reached = k < place
        new = combine(before, jax.tree.map(lambda part: part[k], everything))
        return jax.tree.map(lambda a, b: jnp.where(reached, a, b), new, before)

    return lax.fori_loop(0, peers, hop, start)


def add_pair(earlier, later):
    return (earlier[0] + later[0], earlier[1] + later[1])


def general(query_tokens, key_tokens, value_tokens, norm_gain, out_weight):
    frames, rows, width, depth = query_tokens.shape
    key_relu = jax.nn.relu(key_tokens).reshape(frames, rows * width, HEADS, HD)
    value_heads = value_tokens.reshape(frames, rows * width, HEADS, HD)
    part_state = jnp.einsum(
        "fthd,fthe->fhde", key_relu, value_heads, preferred_element_type=jnp.float32
    ).reshape(frames, HEADS, HD * HD)
    part_norm = jnp.sum(key_relu, axis=1, dtype=jnp.float32)
    state_sum, norm_sum = lax.psum((part_state, part_norm), "band")
    local_state = jnp.cumsum(state_sum, axis=0)
    local_norm = jnp.cumsum(norm_sum, axis=0)
    before = entering(
        (local_state[-1], local_norm[-1]),
        "tm",
        add_pair,
        (jnp.zeros_like(local_state[-1]), jnp.zeros_like(local_norm[-1])),
    )
    prefix_state = local_state + before[0]
    prefix_norm = local_norm + before[1]
    query_relu = jax.nn.relu(query_tokens.astype(jnp.float32)).reshape(
        frames, rows * width, HEADS, HD
    )
    numer = jnp.einsum(
        "fthd,fhde->fthe",
        query_relu,
        prefix_state.reshape(frames, HEADS, HD, HD),
        precision=lax.Precision.HIGHEST,
    )
    denom = (
        jnp.einsum("fthd,fhd->fth", query_relu, prefix_norm, precision=lax.Precision.HIGHEST)
        + read_epsilon
    )
    reads = (numer / denom[:, :, :, None]).reshape(frames * rows * width, depth)
    square = jnp.mean(reads * reads, axis=-1, keepdims=True)
    normed = (reads * lax.rsqrt(square + norm_epsilon) * norm_gain).astype(jnp.bfloat16)
    gathered = lax.all_gather(out_weight, "tm", axis=1, tiled=True)
    rows_half = gathered.reshape(-1, depth)
    result = jnp.dot(
        normed,
        lax.all_gather(rows_half, "band", axis=0, tiled=True),
        preferred_element_type=jnp.float32,
    )
    return result.astype(jnp.bfloat16).reshape(frames, rows, width, depth)


def body(query_tokens, key_tokens, value_tokens, norm_gain, out_weight):
    frames, depth = query_tokens.shape[0], query_tokens.shape[-1]
    peers = lax.axis_size("tm")
    whole_rows = (
        frames == 1
        and lax.axis_size("band") == 2
        and lax.axis_size("parts") == 2
        and peers > 1
        and peers & (peers - 1) == 0
        and out_weight.shape[-1] % depth == 0
        and depth % (2 * HD) == 0
        and round_up(depth, 2 * LANES) > depth
    )
    run = fast if whole_rows else general
    return run(query_tokens, key_tokens, value_tokens, norm_gain, out_weight)


def solution(mesh):
    in_specs = (
        P(("parts", "tm"), "band", None, None),
        P(("parts", "tm"), "band", None, None),
        P(("parts", "tm"), "band", None, None),
        P(),
        P("band", "tm", None),
    )
    out_specs = P(("parts", "tm"), "band", None, None)
    return jax.shard_map(body, mesh=mesh, in_specs=in_specs, out_specs=out_specs, check_vma=False)
```

profile of v0, /device:TPU:0, one launch (start us, length us, event | category | flops | bytes accessed | tf_op | source)
XLA Modules:
  0.0 76.8 jit_solution(1802646956510399531)
XLA Ops:
  0.1 1.1 %copy-done.1 = bf16[1,4,32,2240]{3,2,1,0:T(8,128)(2,1)S(1)} copy-done((bf16[1,4,32,2240]{3,2,1,0:T(8,128)(2,1)S(1)}, bf16[1,4,32,2240]{3,2,1,0:T(8,128)(2,1)}, u32[]{:S(2)}) %copy-start.1) | copy-done | bytes 573464
  1.1 1.1 %copy-done.2 = bf16[1,4,32,2240]{3,2,1,0:T(8,128)(2,1)S(1)} copy-done((bf16[1,4,32,2240]{3,2,1,0:T(8,128)(2,1)S(1)}, bf16[1,4,32,2240]{3,2,1,0:T(8,128)(2,1)}, u32[]{:S(2)}) %copy-start.2) | copy-done | bytes 573464
  2.2 1.0 %shard_map.55 = (f32[40,1152]{1,0:T(8,128)S(1)}, f32[40,1152]{1,0:T(8,128)S(1)}) custom-call(s32[3]{0:T(128)S(1)} %pad_add_fusion.at_ref, bf16[128,2240]{1,0:T(8,128)(2,1)S(1)} %bitcast.8, bf16[128,2240]{1,0:T(8,128)(2,1)S(1)} %bitcast.9), custom_call_target="tpu_custom_call" | custom-call | flops 73400320 | bytes 1515532 | tf_op jit(solution)/shard_map/pallas_call | solution.py:27
  3.8 1.3 %copy-done = bf16[1,1,313600]{2,1,0:T(2,128)(2,1)S(1)} copy-done((bf16[1,1,313600]{2,1,0:T(2,128)(2,1)S(1)}, bf16[1,1,313600]{2,1,0:T(2,128)(2,1)}, u32[]{:S(2)}) %copy-start) | copy-done | bytes 627224
  5.1 1.0 %shard_map.57 = (bf16[144,1152]{1,0:T(8,128)(2,1)S(1)}, bf16[144,1152]{1,0:T(8,128)(2,1)S(1)}) custom-call(s32[3]{0:T(128)S(1)} %pad_add_fusion.at_ref, bf16[1,1,313600]{2,1,0:T(2,128)(2,1)S(1)} %copy-done), custom_call_target="tpu_custom_call" | custom-call | bytes 1290764 | tf_op jit(solution)/shard_map/pallas_call | solution.py:27
  6.1 2.6 %collective-permute-start.14 = (bf16[144,1152]{1,0:T(8,128)(2,1)S(1)}, bf16[144,1152]{1,0:T(8,128)(2,1)S(1)}, u32[]{:S(2)}, u32[]{:S(2)}) collective-permute-start(bf16[144,1152]{1,0:T(8,128)(2,1)S(1)} %get-tuple-element.16.refs_7_), channel_id=1, source_target_pairs={{0,2},{2,0},{4,6},{6,4},{8,10},{10,8},{12,14},{14,12},{1,3},{3,1},... | collective-permute-start | bytes 995336 | tf_op jit(solution)/shard_map/ppermute | solution.py:193
  8.7 3.1 %collective-permute-start.12 = (bf16[144,1152]{1,0:T(8,128)(2,1)S(1)}, bf16[144,1152]{1,0:T(8,128)(2,1)S(1)}, u32[]{:S(2)}, u32[]{:S(2)}) collective-permute-start(bf16[144,1152]{1,0:T(8,128)(2,1)S(1)} %get-tuple-element.15.refs_0_), channel_id=1, source_target_pairs={{0,8},{2,10},{4,12},{6,14},{8,0},{10,2},{12,4},{14,6},{1,9},{3,11}... | collective-permute-start | bytes 995336 | tf_op jit(solution)/shard_map/ppermute | solution.py:193
  11.9 1.6 %collective-permute-start.10 = (bf16[144,1152]{1,0:T(8,128)(2,1)S(1)}, bf16[144,1152]{1,0:T(8,128)(2,1)S(1)}, u32[]{:S(2)}, u32[]{:S(2)}) collective-permute-start(bf16[144,1152]{1,0:T(8,128)(2,1)S(1)} %get-tuple-element.15.refs_0_), channel_id=1, source_target_pairs={{0,4},{2,6},{4,0},{6,2},{8,12},{10,14},{12,8},{14,10},{1,5},{3,7},... | collective-permute-start | bytes 995336 | tf_op jit(solution)/shard_map/ppermute | solution.py:193
  13.4 3.8 %collective-permute-done.14.refs_8_ = bf16[144,1152]{1,0:T(8,128)(2,1)S(1)} collective-permute-done((bf16[144,1152]{1,0:T(8,128)(2,1)S(1)}, bf16[144,1152]{1,0:T(8,128)(2,1)S(1)}, u32[]{:S(2)}, u32[]{:S(2)}) %collective-permute-start.14) | collective-permute-done | bytes 331808 | tf_op jit(solution)/shard_map/ppermute | solution.py:193
  17.3 2.0 %collective-permute-start.9 = (bf16[144,1152]{1,0:T(8,128)(2,1)S(1)}, bf16[144,1152]{1,0:T(8,128)(2,1)S(1)}, u32[]{:S(2)}, u32[]{:S(2)}) collective-permute-start(bf16[144,1152]{1,0:T(8,128)(2,1)S(1)} %get-tuple-element.15.refs_0_), channel_id=1, source_target_pairs={{0,2},{2,0},{4,6},{6,4},{8,10},{10,8},{12,14},{14,12},{1,3},{3,1},... | collective-permute-start | bytes 995336 | tf_op jit(solution)/shard_map/ppermute | solution.py:193
  19.3 1.9 %collective-permute-done.2 = f32[40,1152]{1,0:T(8,128)S(1)} collective-permute-done((f32[40,1152]{1,0:T(8,128)S(1)}, f32[40,1152]{1,0:T(8,128)S(1)}, u32[]{:S(2)}, u32[]{:S(2)}) %collective-permute-start.2) | collective-permute-done | bytes 184352 | tf_op jit(solution)/shard_map/ppermute | solution.py:193
  21.2 4.1 %collective-permute-start.5 = (bf16[144,1152]{1,0:T(8,128)(2,1)S(1)}, bf16[144,1152]{1,0:T(8,128)(2,1)}, u32[]{:S(2)}, u32[]{:S(2)}) collective-permute-start(bf16[144,1152]{1,0:T(8,128)(2,1)S(1)} %get-tuple-element.15.refs_0_), channel_id=1, source_target_pairs={{0,12},{2,14},{4,8},{6,10},{8,4},{10,6},{12,0},{14,2},{1,13},{3,15... | collective-permute-start | bytes 995336 | tf_op jit(solution)/shard_map/ppermute | solution.py:193
  25.4 2.9 %collective-permute-done.12.refs_4_ = bf16[144,1152]{1,0:T(8,128)(2,1)S(1)} collective-permute-done((bf16[144,1152]{1,0:T(8,128)(2,1)S(1)}, bf16[144,1152]{1,0:T(8,128)(2,1)S(1)}, u32[]{:S(2)}, u32[]{:S(2)}) %collective-permute-start.12) | collective-permute-done | bytes 331808 | tf_op jit(solution)/shard_map/ppermute | solution.py:193
  29.1 6.9 %collective-permute-start.17 = (bf16[144,1152]{1,0:T(8,128)(2,1)S(1)}, bf16[144,1152]{1,0:T(8,128)(2,1)}, u32[]{:S(2)}, u32[]{:S(2)}) collective-permute-start(bf16[144,1152]{1,0:T(8,128)(2,1)S(1)} %collective-permute-done.12.refs_4_), channel_id=1, source_target_pairs={{0,16},{16,0},{1,17},{17,1},{2,18},{18,2},{3,19},{19,3},{4,20},{20... | collective-permute-start | bytes 995336 | tf_op jit(solution)/shard_map/ppermute | solution.py:196
  36.0 1.5 %collective-permute-start.13 = (bf16[144,1152]{1,0:T(8,128)(2,1)S(1)}, bf16[144,1152]{1,0:T(8,128)(2,1)}, u32[]{:S(2)}, u32[]{:S(2)}) collective-permute-start(bf16[144,1152]{1,0:T(8,128)(2,1)S(1)} %collective-permute-done.12.refs_4_), channel_id=1, source_target_pairs={{0,2},{2,0},{4,6},{6,4},{8,10},{10,8},{12,14},{14,12},{1,3},{3,1},... | collective-permute-start | bytes 995336 | tf_op jit(solution)/shard_map/ppermute | solution.py:193
  37.9 1.1 %collective-permute-done.3 = f32[40,1152]{1,0:T(8,128)S(1)} collective-permute-done((f32[40,1152]{1,0:T(8,128)S(1)}, f32[40,1152]{1,0:T(8,128)S(1)}, u32[]{:S(2)}, u32[]{:S(2)}) %collective-permute-start.3) | collective-permute-done | bytes 184352 | tf_op jit(solution)/shard_map/ppermute | solution.py:193
  39.1 1.5 %collective-permute-start.6 = (bf16[144,1152]{1,0:T(8,128)(2,1)}, bf16[144,1152]{1,0:T(8,128)(2,1)S(1)}, u32[]{:S(2)}, u32[]{:S(2)}) collective-permute-start(bf16[144,1152]{1,0:T(8,128)(2,1)} %collective-permute-done.5.refs_6_), channel_id=1, source_target_pairs={{0,2},{2,0},{4,6},{6,4},{8,10},{10,8},{12,14},{14,12},{1,3},{3,1},... | collective-permute-start | bytes 995336 | tf_op jit(solution)/shard_map/ppermute | solution.py:193
  40.6 0.7 add.22
  41.3 6.3 %collective-permute-start.4 = (f32[40,1152]{1,0:T(8,128)}, f32[40,1152]{1,0:T(8,128)}, u32[]{:S(2)}, u32[]{:S(2)}) collective-permute-start(f32[40,1152]{1,0:T(8,128)} %add.22), channel_id=1, source_target_pairs={{0,8},{2,10},{4,12},{6,14},{8,0},{10,2},{12,4},{14,6},{1,9},{3,11}... | collective-permute-start | bytes 552968 | tf_op jit(solution)/shard_map/ppermute | solution.py:193
  47.7 0.6 collective-permute-start.11
  48.8 1.5 %collective-permute-start.18 = (bf16[144,1152]{1,0:T(8,128)(2,1)}, bf16[144,1152]{1,0:T(8,128)(2,1)S(1)}, u32[]{:S(2)}, u32[]{:S(2)}) collective-permute-start(bf16[144,1152]{1,0:T(8,128)(2,1)} %collective-permute-done.13.refs_5_), channel_id=1, source_target_pairs={{0,16},{16,0},{1,17},{17,1},{2,18},{18,2},{3,19},{19,3},{4,20},{20... | collective-permute-start | bytes 995336 | tf_op jit(solution)/shard_map/ppermute | solution.py:196
  50.8 1.8 %collective-permute-start.16 = (bf16[144,1152]{1,0:T(8,128)(2,1)}, bf16[144,1152]{1,0:T(8,128)(2,1)S(1)}, u32[]{:S(2)}, u32[]{:S(2)}) collective-permute-start(bf16[144,1152]{1,0:T(8,128)(2,1)} %collective-permute-done.15.refs_9_), channel_id=1, source_target_pairs={{0,2},{2,0},{4,6},{6,4},{8,10},{10,8},{12,14},{14,12},{1,3},{3,1},... | collective-permute-start | bytes 995336 | tf_op jit(solution)/shard_map/ppermute | solution.py:193
  52.7 3.5 %collective-permute-done.4 = f32[40,1152]{1,0:T(8,128)} collective-permute-done((f32[40,1152]{1,0:T(8,128)}, f32[40,1152]{1,0:T(8,128)}, u32[]{:S(2)}, u32[]{:S(2)}) %collective-permute-start.4) | collective-permute-done | bytes 184352 | tf_op jit(solution)/shard_map/ppermute | solution.py:193
  56.7 1.0 %select_add_fusion.s_ref = f32[40,1152]{1,0:T(8,128)S(1)} fusion(f32[40,1152]{1,0:T(8,128)} %collective-permute-done.4, f32[40,1152]{1,0:T(8,128)} %copy-done.6, f32[40,1152]{1,0:T(8,128)} %copy-done.4, f32[40,1152]{1,0:T(8,128)} %copy-done.5, pred[]{:T(512)S(6)} %ne.11, pred[]{:T(512)S(6)} %ne.10, pred[]{:T(512)S(6)} %ne.9), kind=kLoop, calls=%fused_computation | loop fusion | flops 276480 | bytes 921603 | tf_op jit(solution)/shard_map/add | solution.py:239
  57.7 1.9 %shard_map.56 = (bf16[256,1152]{1,0:T(8,128)(2,1)S(1)}, f32[256,128]{1,0:T(8,128)S(1)}) custom-call(s32[3]{0:T(128)S(1)} %pad_add_fusion.at_ref, bf16[128,2240]{1,0:T(8,128)(2,1)S(1)} %bitcast.10, bf16[128,2240]{1,0:T(8,128)(2,1)S(1)} %bitcast.11, f32[40,1152]{1,0:T(8,128)S(1)} %select_add_fusion.s_ref, f32[1,2240]{1,0:T(1,128)S(1)} %reshape.22.g_ref), custom_call_target="tpu_custom_call" | custom-call | flops 150994944 | bytes 2061068 | tf_op jit(solution)/shard_map/pallas_call | solution.py:27
  59.6 6.7 %collective-permute-done.18.refs_12_ = bf16[144,1152]{1,0:T(8,128)(2,1)S(1)} collective-permute-done((bf16[144,1152]{1,0:T(8,128)(2,1)}, bf16[144,1152]{1,0:T(8,128)(2,1)S(1)}, u32[]{:S(2)}, u32[]{:S(2)}) %collective-permute-start.18) | collective-permute-done | bytes 331808 | tf_op jit(solution)/shard_map/ppermute | solution.py:196
  66.3 2.8 %shard_map.58.refs_3_ = f32[2,256,1152]{2,1,0:T(8,128)S(1)} custom-call(s32[3]{0:T(128)S(1)} %pad_add_fusion.at_ref, bf16[256,1152]{1,0:T(8,128)(2,1)S(1)} %get-tuple-element.13.left_ref, f32[256,128]{1,0:T(8,128)S(1)} %get-tuple-element.14.square_ref, bf16[144,1152]{1,0:T(8,128)(2,1)S(1)} %get-tuple-element.15.refs_0_, ...), custom_call_target="tpu_custom_call" | custom-call | flops 1104150528 | bytes 7393292 | tf_op jit(solution)/shard_map/pallas_call | solution.py:27
  69.1 2.2 %collective-permute-done.8.refs_2_ = bf16[144,1152]{1,0:T(8,128)(2,1)S(1)} collective-permute-done((bf16[144,1152]{1,0:T(8,128)(2,1)S(1)}, bf16[144,1152]{1,0:T(8,128)(2,1)S(1)}, u32[]{:S(2)}, u32[]{:S(2)}) %collective-permute-start.8) | collective-permute-done | bytes 331808 | tf_op jit(solution)/shard_map/ppermute | solution.py:196
  71.3 1.0 %shard_map.60 = f32[2,128,1152]{2,1,0:T(8,128)S(1)} custom-call(s32[3]{0:T(128)S(1)} %pad_add_fusion.at_ref, bf16[256,1152]{1,0:T(8,128)(2,1)S(1)} %get-tuple-element.13.left_ref, f32[256,128]{1,0:T(8,128)S(1)} %get-tuple-element.14.square_ref, bf16[144,1152]{1,0:T(8,128)(2,1)S(1)} %collective-permute-done.6.refs_0_, ...), custom_call_target="tpu_custom_call" | custom-call | flops 127401984 | bytes 5255180 | tf_op jit(solution)/shard_map/pallas_call | solution.py:27
  72.4 1.0 %shard_map.59.own_ref = f32[2,128,1152]{2,1,0:T(8,128)S(1)} custom-call(s32[3]{0:T(128)S(1)} %pad_add_fusion.at_ref, bf16[256,1152]{1,0:T(8,128)(2,1)S(1)} %get-tuple-element.13.left_ref, f32[256,128]{1,0:T(8,128)S(1)} %get-tuple-element.14.square_ref, bf16[144,1152]{1,0:T(8,128)(2,1)S(1)} %collective-permute-done.6.refs_0_, ...), custom_call_target="tpu_custom_call" | custom-call | flops 127401984 | bytes 5255180 | tf_op jit(solution)/shard_map/pallas_call | solution.py:27
  73.4 1.8 %collective-permute-done.19.got_ref = f32[2,128,1152]{2,1,0:T(8,128)S(1)} collective-permute-done((f32[2,128,1152]{2,1,0:T(8,128)S(1)}, f32[2,128,1152]{2,1,0:T(8,128)S(1)}, u32[]{:S(2)}, u32[]{:S(2)}) %collective-permute-start.19) | collective-permute-done | bytes 1179680 | tf_op jit(solution)/shard_map/ppermute | solution.py:196
  75.2 1.5 %shard_map.61 = bf16[128,2240]{1,0:T(8,128)(2,1)} custom-call(s32[3]{0:T(128)S(1)} %pad_add_fusion.at_ref, f32[2,128,1152]{2,1,0:T(8,128)S(1)} %shard_map.59.own_ref, f32[2,128,1152]{2,1,0:T(8,128)S(1)} %collective-permute-done.19.got_ref), custom_call_target="tpu_custom_call" | custom-call | bytes 2932748 | tf_op jit(solution)/shard_map/pallas_call | solution.py:27
  (37 shorter events, 3.7 us)
Async XLA Ops:
  0.1 1.1 %copy-start.1 = (bf16[1,4,32,2240]{3,2,1,0:T(8,128)(2,1)S(1)}, bf16[1,4,32,2240]{3,2,1,0:T(8,128)(2,1)}, u32[]{:S(2)}) copy-start(bf16[1,4,32,2240]{3,2,1,0:T(8,128)(2,1)} %param.6) | copy-start | bytes 1720324
  1.1 1.1 %copy-start.2 = (bf16[1,4,32,2240]{3,2,1,0:T(8,128)(2,1)S(1)}, bf16[1,4,32,2240]{3,2,1,0:T(8,128)(2,1)}, u32[]{:S(2)}) copy-start(bf16[1,4,32,2240]{3,2,1,0:T(8,128)(2,1)} %param.7) | copy-start | bytes 1720324
  2.2 9.6 %copy-start.3 = (bf16[1,4,32,2240]{3,2,1,0:T(8,128)(2,1)S(1)}, bf16[1,4,32,2240]{3,2,1,0:T(8,128)(2,1)}, u32[]{:S(2)}) copy-start(bf16[1,4,32,2240]{3,2,1,0:T(8,128)(2,1)} %param.5) | copy-start | bytes 1720324
  3.2 5.4 %collective-permute-start.1 = (f32[40,1152]{1,0:T(8,128)S(1)}, f32[40,1152]{1,0:T(8,128)S(1)}, u32[]{:S(2)}, u32[]{:S(2)}) collective-permute-start(f32[40,1152]{1,0:T(8,128)S(1)} %get-tuple-element.12), channel_id=1, source_target_pairs={{0,1},{1,0},{2,3},{3,2},{4,5},{5,4},{6,7},{7,6},{8,9},{9,8},{10,11... | collective-permute-start | bytes 552968 | tf_op jit(solution)/shard_map/ppermute | solution.py:196
  3.8 1.3 %copy-start = (bf16[1,1,313600]{2,1,0:T(2,128)(2,1)S(1)}, bf16[1,1,313600]{2,1,0:T(2,128)(2,1)}, u32[]{:S(2)}) copy-start(bf16[1,1,313600]{2,1,0:T(2,128)(2,1)} %w_ref.1) | copy-start | bytes 1881604
  5.1 42.6 %copy-start.7 = (f32[2240]{0:T(1024)S(1)}, f32[2240]{0:T(1024)}, u32[]{:S(2)}) copy-start(f32[2240]{0:T(1024)} %param.8) | copy-start | bytes 26884
  6.1 11.2 %collective-permute-start.14 = (bf16[144,1152]{1,0:T(8,128)(2,1)S(1)}, bf16[144,1152]{1,0:T(8,128)(2,1)S(1)}, u32[]{:S(2)}, u32[]{:S(2)}) collective-permute-start(bf16[144,1152]{1,0:T(8,128)(2,1)S(1)} %get-tuple-element.16.refs_7_), channel_id=1, source_target_pairs={{0,2},{2,0},{4,6},{6,4},{8,10},{10,8},{12,14},{14,12},{1,3},{3,1},... | collective-permute-start | bytes 995336 | tf_op jit(solution)/shard_map/ppermute | solution.py:193
  8.7 32.7 %copy-start.4 = (f32[40,1152]{1,0:T(8,128)}, f32[40,1152]{1,0:T(8,128)S(1)}, u32[]{:S(2)}) copy-start(f32[40,1152]{1,0:T(8,128)S(1)} %add.18) | copy-start | bytes 552964
  8.7 12.6 %collective-permute-start.2 = (f32[40,1152]{1,0:T(8,128)S(1)}, f32[40,1152]{1,0:T(8,128)S(1)}, u32[]{:S(2)}, u32[]{:S(2)}) collective-permute-start(f32[40,1152]{1,0:T(8,128)S(1)} %add.18), channel_id=1, source_target_pairs={{0,2},{2,0},{4,6},{6,4},{8,10},{10,8},{12,14},{14,12},{1,3},{3,1},... | collective-permute-start | bytes 552968 | tf_op jit(solution)/shard_map/ppermute | solution.py:193
  8.7 19.6 %collective-permute-start.12 = (bf16[144,1152]{1,0:T(8,128)(2,1)S(1)}, bf16[144,1152]{1,0:T(8,128)(2,1)S(1)}, u32[]{:S(2)}, u32[]{:S(2)}) collective-permute-start(bf16[144,1152]{1,0:T(8,128)(2,1)S(1)} %get-tuple-element.15.refs_0_), channel_id=1, source_target_pairs={{0,8},{2,10},{4,12},{6,14},{8,0},{10,2},{12,4},{14,6},{1,9},{3,11}... | collective-permute-start | bytes 995336 | tf_op jit(solution)/shard_map/ppermute | solution.py:193
  11.9 29.5 %collective-permute-start = (bf16[1,4,32,2240]{3,2,1,0:T(8,128)(2,1)S(1)}, bf16[1,4,32,2240]{3,2,1,0:T(8,128)(2,1)S(1)}, u32[]{:S(2)}, u32[]{:S(2)}) collective-permute-start(bf16[1,4,32,2240]{3,2,1,0:T(8,128)(2,1)S(1)} %copy-done.3), channel_id=1, source_target_pairs={{0,1},{1,0},{2,3},{3,2},{4,5},{5,4},{6,7},{7,6},{8,9},{9,8},{10,11... | collective-permute-start | bytes 1720328 | tf_op jit(solution)/shard_map/ppermute | solution.py:196
  11.9 17.2 %collective-permute-start.10 = (bf16[144,1152]{1,0:T(8,128)(2,1)S(1)}, bf16[144,1152]{1,0:T(8,128)(2,1)S(1)}, u32[]{:S(2)}, u32[]{:S(2)}) collective-permute-start(bf16[144,1152]{1,0:T(8,128)(2,1)S(1)} %get-tuple-element.15.refs_0_), channel_id=1, source_target_pairs={{0,4},{2,6},{4,0},{6,2},{8,12},{10,14},{12,8},{14,10},{1,5},{3,7},... | collective-permute-start | bytes 995336 | tf_op jit(solution)/shard_map/ppermute | solution.py:193
  17.3 18.7 %collective-permute-start.9 = (bf16[144,1152]{1,0:T(8,128)(2,1)S(1)}, bf16[144,1152]{1,0:T(8,128)(2,1)S(1)}, u32[]{:S(2)}, u32[]{:S(2)}) collective-permute-start(bf16[144,1152]{1,0:T(8,128)(2,1)S(1)} %get-tuple-element.15.refs_0_), channel_id=1, source_target_pairs={{0,2},{2,0},{4,6},{6,4},{8,10},{10,8},{12,14},{14,12},{1,3},{3,1},... | collective-permute-start | bytes 995336 | tf_op jit(solution)/shard_map/ppermute | solution.py:193
  21.2 20.1 %copy-start.5 = (f32[40,1152]{1,0:T(8,128)}, f32[40,1152]{1,0:T(8,128)S(1)}, u32[]{:S(2)}) copy-start(f32[40,1152]{1,0:T(8,128)S(1)} %collective-permute-done.2) | copy-start | bytes 552964
  21.2 16.2 %collective-permute-start.5 = (bf16[144,1152]{1,0:T(8,128)(2,1)S(1)}, bf16[144,1152]{1,0:T(8,128)(2,1)}, u32[]{:S(2)}, u32[]{:S(2)}) collective-permute-start(bf16[144,1152]{1,0:T(8,128)(2,1)S(1)} %get-tuple-element.15.refs_0_), channel_id=1, source_target_pairs={{0,12},{2,14},{4,8},{6,10},{8,4},{10,6},{12,0},{14,2},{1,13},{3,15... | collective-permute-start | bytes 995336 | tf_op jit(solution)/shard_map/ppermute | solution.py:193
  28.3 10.7 %collective-permute-start.3 = (f32[40,1152]{1,0:T(8,128)S(1)}, f32[40,1152]{1,0:T(8,128)S(1)}, u32[]{:S(2)}, u32[]{:S(2)}) collective-permute-start(f32[40,1152]{1,0:T(8,128)S(1)} %add.20), channel_id=1, source_target_pairs={{0,4},{2,6},{4,0},{6,2},{8,12},{10,14},{12,8},{14,10},{1,5},{3,7},... | collective-permute-start | bytes 552968 | tf_op jit(solution)/shard_map/ppermute | solution.py:193
  29.1 18.6 %collective-permute-start.17 = (bf16[144,1152]{1,0:T(8,128)(2,1)S(1)}, bf16[144,1152]{1,0:T(8,128)(2,1)}, u32[]{:S(2)}, u32[]{:S(2)}) collective-permute-start(bf16[144,1152]{1,0:T(8,128)(2,1)S(1)} %collective-permute-done.12.refs_4_), channel_id=1, source_target_pairs={{0,16},{16,0},{1,17},{17,1},{2,18},{18,2},{3,19},{19,3},{4,20},{20... | collective-permute-start | bytes 995336 | tf_op jit(solution)/shard_map/ppermute | solution.py:196
  36.0 12.3 %collective-permute-start.13 = (bf16[144,1152]{1,0:T(8,128)(2,1)S(1)}, bf16[144,1152]{1,0:T(8,128)(2,1)}, u32[]{:S(2)}, u32[]{:S(2)}) collective-permute-start(bf16[144,1152]{1,0:T(8,128)(2,1)S(1)} %collective-permute-done.12.refs_4_), channel_id=1, source_target_pairs={{0,2},{2,0},{4,6},{6,4},{8,10},{10,8},{12,14},{14,12},{1,3},{3,1},... | collective-permute-start | bytes 995336 | tf_op jit(solution)/shard_map/ppermute | solution.py:193
  37.4 11.4 %collective-permute-start.15 = (bf16[144,1152]{1,0:T(8,128)(2,1)S(1)}, bf16[144,1152]{1,0:T(8,128)(2,1)}, u32[]{:S(2)}, u32[]{:S(2)}) collective-permute-start(bf16[144,1152]{1,0:T(8,128)(2,1)S(1)} %collective-permute-done.10.refs_2_), channel_id=1, source_target_pairs={{0,16},{16,0},{1,17},{17,1},{2,18},{18,2},{3,19},{19,3},{4,20},{20... | collective-permute-start | bytes 995336 | tf_op jit(solution)/shard_map/ppermute | solution.py:196
  39.1 2.3 %copy-start.6 = (f32[40,1152]{1,0:T(8,128)}, f32[40,1152]{1,0:T(8,128)S(1)}, u32[]{:S(2)}) copy-start(f32[40,1152]{1,0:T(8,128)S(1)} %collective-permute-done.3) | copy-start | bytes 552964
  39.1 11.8 %collective-permute-start.6 = (bf16[144,1152]{1,0:T(8,128)(2,1)}, bf16[144,1152]{1,0:T(8,128)(2,1)S(1)}, u32[]{:S(2)}, u32[]{:S(2)}) collective-permute-start(bf16[144,1152]{1,0:T(8,128)(2,1)} %collective-permute-done.5.refs_6_), channel_id=1, source_target_pairs={{0,2},{2,0},{4,6},{6,4},{8,10},{10,8},{12,14},{14,12},{1,3},{3,1},... | collective-permute-start | bytes 995336 | tf_op jit(solution)/shard_map/ppermute | solution.py:193
  41.3 14.9 %collective-permute-start.4 = (f32[40,1152]{1,0:T(8,128)}, f32[40,1152]{1,0:T(8,128)}, u32[]{:S(2)}, u32[]{:S(2)}) collective-permute-start(f32[40,1152]{1,0:T(8,128)} %add.22), channel_id=1, source_target_pairs={{0,8},{2,10},{4,12},{6,14},{8,0},{10,2},{12,4},{14,6},{1,9},{3,11}... | collective-permute-start | bytes 552968 | tf_op jit(solution)/shard_map/ppermute | solution.py:193
  47.7 11.9 %collective-permute-start.11 = (bf16[144,1152]{1,0:T(8,128)(2,1)S(1)}, bf16[144,1152]{1,0:T(8,128)(2,1)S(1)}, u32[]{:S(2)}, u32[]{:S(2)}) collective-permute-start(bf16[144,1152]{1,0:T(8,128)(2,1)S(1)} %collective-permute-done.10.refs_2_), channel_id=1, source_target_pairs={{0,2},{2,0},{4,6},{6,4},{8,10},{10,8},{12,14},{14,12},{1,3},{3,1},... | collective-permute-start | bytes 995336 | tf_op jit(solution)/shard_map/ppermute | solution.py:193
  48.3 20.8 %collective-permute-start.7 = (bf16[144,1152]{1,0:T(8,128)(2,1)}, bf16[144,1152]{1,0:T(8,128)(2,1)S(1)}, u32[]{:S(2)}, u32[]{:S(2)}) collective-permute-start(bf16[144,1152]{1,0:T(8,128)(2,1)} %collective-permute-done.5.refs_6_), channel_id=1, source_target_pairs={{0,16},{16,0},{1,17},{17,1},{2,18},{18,2},{3,19},{19,3},{4,20},{20... | collective-permute-start | bytes 995336 | tf_op jit(solution)/shard_map/ppermute | solution.py:196
  48.8 17.5 %collective-permute-start.18 = (bf16[144,1152]{1,0:T(8,128)(2,1)}, bf16[144,1152]{1,0:T(8,128)(2,1)S(1)}, u32[]{:S(2)}, u32[]{:S(2)}) collective-permute-start(bf16[144,1152]{1,0:T(8,128)(2,1)} %collective-permute-done.13.refs_5_), channel_id=1, source_target_pairs={{0,16},{16,0},{1,17},{17,1},{2,18},{18,2},{3,19},{19,3},{4,20},{20... | collective-permute-start | bytes 995336 | tf_op jit(solution)/shard_map/ppermute | solution.py:196
  50.8 15.5 %collective-permute-start.16 = (bf16[144,1152]{1,0:T(8,128)(2,1)}, bf16[144,1152]{1,0:T(8,128)(2,1)S(1)}, u32[]{:S(2)}, u32[]{:S(2)}) collective-permute-start(bf16[144,1152]{1,0:T(8,128)(2,1)} %collective-permute-done.15.refs_9_), channel_id=1, source_target_pairs={{0,2},{2,0},{4,6},{6,4},{8,10},{10,8},{12,14},{14,12},{1,3},{3,1},... | collective-permute-start | bytes 995336 | tf_op jit(solution)/shard_map/ppermute | solution.py:193
  56.2 15.1 %collective-permute-start.8 = (bf16[144,1152]{1,0:T(8,128)(2,1)S(1)}, bf16[144,1152]{1,0:T(8,128)(2,1)S(1)}, u32[]{:S(2)}, u32[]{:S(2)}) collective-permute-start(bf16[144,1152]{1,0:T(8,128)(2,1)S(1)} %collective-permute-done.6.refs_0_), channel_id=1, source_target_pairs={{0,16},{16,0},{1,17},{17,1},{2,18},{18,2},{3,19},{19,3},{4,20},{20... | collective-permute-start | bytes 995336 | tf_op jit(solution)/shard_map/ppermute | solution.py:196
  72.3 2.9 %collective-permute-start.19 = (f32[2,128,1152]{2,1,0:T(8,128)S(1)}, f32[2,128,1152]{2,1,0:T(8,128)S(1)}, u32[]{:S(2)}, u32[]{:S(2)}) collective-permute-start(f32[2,128,1152]{2,1,0:T(8,128)S(1)} %shard_map.60), channel_id=1, source_target_pairs={{0,1},{1,0},{2,3},{3,2},{4,5},{5,4},{6,7},{7,6},{8,9},{9,8},{10,11... | collective-permute-start | bytes 3538952 | tf_op jit(solution)/shard_map/ppermute | solution.py:196
where the time goes:
time: 77.1 us; the launch traced here: 76.8 us
  starting transfers between devices  36 us (47%)
  waiting for transfers between devices  25.1 us (33%)
  Pallas kernels  10.3 us (13%)
  local copies, waits for them, and re-layouts  3.45 us (4%)
  other arithmetic  1.8 us (2%)
    ppermute x12, starting transfers between devices, flip(): return lax.ppermute(x, 'tm', [(i, i ^ mask) for i in range(peers)])  25.5 us
    ppermute x12, waiting for transfers between devices, flip(): return lax.ppermute(x, 'tm', [(i, i ^ mask) for i in range(peers)])  14.4 us
    ppermute x8, waiting for transfers between devices, across(): return lax.ppermute(x, axis, swap)  10.7 us
    ppermute x8, starting transfers between devices, across(): return lax.ppermute(x, axis, swap)  10.6 us
    pallas_call x7, Pallas kernels, call(): pl.pallas_call(kernel, out_shape=out, in_specs=[scalar] * smem + [whole]...  10.3 us
    unnamed x16, local copies, waits for them, and re-layouts  3.44 us
  transfers between devices with their start and end apart: 20, of which 10 were waited for; matrix products, arithmetic and copies ran while one was open for 2% of the time, Pallas kernels for 9%

commit v1 on v0

--- a/solution.py
+++ b/solution.py
@@ -35,11 +35,23 @@
     )(*args)
 
 
+def line_ring(length):
+    return [0, *range(1, length, 2), *reversed(range(2, length, 2))]
+
+
+def ring_place(z, length):
+    return jnp.where(z % 2 == 1, (z + 1) // 2, jnp.where(z == 0, 0, length - z // 2))
+
+
+def at_ring_place(p, length):
+    return jnp.where(p == 0, 0, jnp.where(p <= length // 2, 2 * p - 1, 2 * (length - p)))
+
+
 def shape(dims, dtype):
     return jax.ShapeDtypeStruct(tuple(dims), dtype)
 
 
-def unpack_weight(rows, depth, at_ref, w_ref, mine_ref, rest_ref, tall):
+def unpack_weight(rows, depth, at_ref, w_ref, mine_ref, both_ref, tall):
     half = mine_ref.shape[1]
     tall[pl.ds(rows // 8 * 8, tall.shape[0] - rows // 8 * 8), :] = jnp.zeros(
         (tall.shape[0] - rows // 8 * 8, tall.shape[1]), jnp.float32
@@ -51,8 +63,10 @@
     for r in range(rows):
         tall[r : r + 1, 0:depth] = w_ref[0, :, depth * r : depth * (r + 1)].astype(jnp.float32)
     y = at_ref[0]
-    mine_ref[...] = tall[:, pl.ds(pl.multiple_of(y * half, LANES), half)].astype(jnp.bfloat16)
-    rest_ref[...] = tall[:, pl.ds(pl.multiple_of((1 - y) * half, LANES), half)].astype(jnp.bfloat16)
+    first = tall[:, pl.ds(pl.multiple_of(y * half, LANES), half)].astype(jnp.bfloat16)
+    mine_ref[...] = first
+    both_ref[0] = first
+    both_ref[1] = tall[:, pl.ds(pl.multiple_of((1 - y) * half, LANES), half)].astype(jnp.bfloat16)
 
 
 def head_mask():
@@ -141,19 +155,25 @@
     blocks[...] = jnp.zeros_like(blocks)
     for t in range(slots):
         blocks[t, :, 0:shard] = flat[:, shard * t : shard * (t + 1)]
-    me = at_ref[2]
+    length = slots // 2
+    z, x = at_ref[2] // 2, at_ref[2] % 2
+    place = ring_place(z, length)
     for m in range(slots):
-        left_ref[:, wide * m : wide * (m + 1)] = blocks[me ^ m]
-
-
-def project(first, last, sides, spare, at_ref, left_ref, square_ref, *refs):
+        source = at_ring_place((place + length - m // 2) % length, length)
+        left_ref[:, wide * m : wide * (m + 1)] = blocks[2 * source + (x ^ (m % 2))]
+
+
+def project(first, last, sides, plan, spare, at_ref, left_ref, square_ref, *refs):
     refs = list(refs)
     out_ref = refs.pop()
-    pieces = [[refs.pop(0) for _ in slots] for slots in sides]
-    base = refs.pop(0) if refs else None
-    wide = pieces[0][0].shape[0] if pieces[0] else pieces[1][0].shape[0]
+    count = 1 + max(at for pieces in plan for at, _ in pieces)
+    base = refs[count] if len(refs) > count else None
+    pieces = [
+        [refs[at][...] if part is None else refs[at][part] for at, part in side] for side in plan
+    ]
+    wide = (pieces[0] + pieces[1])[0].shape[0]
     for i, slots in enumerate(sides):
-        weight = jnp.concatenate([p[...] for p in pieces[i]], axis=0)
+        weight = jnp.concatenate(pieces[i], axis=0)
         left = jnp.concatenate(
             [left_ref[first:last, wide * m : wide * (m + 1)] for m in slots], axis=1
         )
@@ -201,24 +221,31 @@
     bf16, f32 = jnp.bfloat16, jnp.float32
 
     mine, rest = {}, {}
-    mine[0], rest[0] = call(
+    mine[0], both = call(
         functools.partial(unpack_weight, shard, depth),
-        (shape((tall, cols), bf16), shape((tall, cols), bf16)),
+        (shape((tall, cols), bf16), shape((2, tall, cols), bf16)),
         (at, out_weight),
         scratch=[pltpu.VMEM((tall, 2 * cols), f32)],
         smem=1,
     )
-    far = range(2, peers, 2)
-    for m in far:
-        mine[m] = flip(mine[0], m)
-    mine[1], rest[1] = flip(mine[0], 1), flip(rest[0], 1)
-    for m in far:
-        mine[m + 1] = flip(mine[m], 1)
+    length = peers // 2
+    order = line_ring(length)
+    onward = [
+        (2 * a + x, 2 * b + x) for a, b in zip(order, order[1:] + order[:1]) for x in range(2)
+    ]
+    beside = flip(both, 1)
+    rest[0] = (both, 1)
+    mine[1], rest[1] = (beside, 0), (beside, 1)
+    for k in range(1, length):
+        m = 2 * k
+        mine[m] = lax.ppermute(mine[m - 2], "tm", onward)
         rest[m] = across(mine[m], "parts")
-    for m in far:
-        if m == 2:
+        if k < length - 1:
+            last = beside[0] if k == 1 else mine[m - 1]
+            mine[m + 1] = lax.ppermute(last, "tm", onward)
             rest[m + 1] = flip(rest[m], 1)
         else:
+            mine[m + 1] = flip(mine[m], 1)
             rest[m + 1] = across(mine[m + 1], "parts")
 
     queries = query_tokens.reshape(count, depth)
@@ -232,12 +259,14 @@
         flops=2 * count * LANES * depth,
     )
     total = own + across(other, "band")
+    sent = total.astype(bf16)
     prefix = total
     step = 0
     while 1 << step < peers:
-        got = flip(total, 1 << step)
-        prefix = prefix + jnp.where((at[2] & (1 << step)) != 0, got, 0.0)
-        total = total + got
+        got = flip(sent, 1 << step)
+        prefix = prefix + jnp.where((at[2] & (1 << step)) != 0, got.astype(f32), 0.0)
+        total = total + got.astype(f32)
+        sent = total.astype(bf16)
         step += 1
     left, square = call(
         functools.partial(read_states, half, shard, peers),
@@ -254,17 +283,23 @@
     )
 
     def partial_sums(first, last, slots, base):
-        sides = ((slots[0], mine), (slots[1], rest))
-        pieces = [held[m] for chosen, held in sides for m in chosen]
+        arrays, plan = [], []
+        for chosen, held in zip(slots, (mine, rest)):
+            plan.append([])
+            for m in chosen:
+                array, part = held[m] if isinstance(held[m], tuple) else (held[m], None)
+                if not any(array is a for a in arrays):
+                    arrays.append(array)
+                plan[-1].append(([array is a for a in arrays].index(True), part))
         return call(
-            functools.partial(project, first, last, slots, spare),
+            functools.partial(project, first, last, slots, plan, spare),
             shape((2, last - first, cols), f32),
-            (at, left, square, *pieces, *base),
+            (at, left, square, *arrays, *base),
             smem=1,
-            flops=2 * (last - first) * cols * tall * len(pieces),
-        )
-
-    late = ((peers - 1,), (peers - 2, peers - 1))
+            flops=2 * (last - first) * cols * tall * sum(map(len, plan)),
+        )
+
+    late = ((peers - 3,), (peers - 3, peers - 1))
     soon = tuple(tuple(m for m in range(peers) if m not in side) for side in late)
     base = partial_sums(0, 2 * count, soon, ())
     other = partial_sums(count, 2 * count, late, (base,))
@@ -349,7 +384,7 @@
         frames == 1
         and lax.axis_size("band") == 2
         and lax.axis_size("parts") == 2
-        and peers > 1
+        and peers > 2
         and peers & (peers - 1) == 0
         and out_weight.shape[-1] % depth == 0
         and depth % (2 * HD) == 0

time: 77.1 us -> 66.9 us (0.87)
  starting transfers between devices: 36 us -> 25 us
  waiting for transfers between devices: 25.1 us -> 26.8 us
    ppermute x0 -> x5, waiting for transfers between devices: none -> 19 us  [the longest x3 19 us: fast(): mine[m] = lax.ppermute(mine[m - 2], 'tm', onward)]
    ppermute x12 -> x7, starting transfers between devices: 25.5 us -> 10.2 us  [flip(): return lax.ppermute(x, 'tm', [(i, i ^ mask) for i in range(peers)])]
    ppermute x12 -> x7, waiting for transfers between devices: 14.4 us -> 4.99 us  [flip(): return lax.ppermute(x, 'tm', [(i, i ^ mask) for i in range(peers)])]
    ppermute x0 -> x5, starting transfers between devices: none -> 8.09 us  [the longest x2 4.11 us: fast(): mine[m + 1] = lax.ppermute(last, 'tm', onward)]
    ppermute x8 -> x7, waiting for transfers between devices: 10.7 us -> 2.88 us  [across(): return lax.ppermute(x, axis, swap)]
    ppermute x8 -> x7, starting transfers between devices: 10.6 us -> 6.71 us  [across(): return lax.ppermute(x, axis, swap)]
    unnamed x16 -> x18, local copies, waits for them, and re-layouts: 3.44 us -> 2.25 us
    add x4 -> x1, other arithmetic: 1.72 us -> 1.13 us  [fast(): prefix = prefix + jnp.where(at[2] & 1 << step != 0, got.astype(f32), 0.0)]
  transfers between devices with their start and end apart: 20 -> 19, of which waited for: 10 -> 6; matrix products, arithmetic and copies ran while one was open for 2% -> 3% of each run, Pallas kernels for 9% -> 10%
where the time goes in v1:
time: 66.9 us; the launch traced here: 66.7 us
  waiting for transfers between devices  26.8 us (40%)
  starting transfers between devices  25 us (37%)
  Pallas kernels  10.4 us (16%)
  local copies, waits for them, and re-layouts  3 us (4%)
  other arithmetic  1.29 us (2%)
    ppermute x3, waiting for transfers between devices, fast(): mine[m] = lax.ppermute(mine[m - 2], 'tm', onward)  19 us
    pallas_call x7, Pallas kernels, call(): pl.pallas_call(kernel, out_shape=out, in_specs=[scalar] * smem + [whole]...  10.4 us
    ppermute x7, starting transfers between devices, flip(): return lax.ppermute(x, 'tm', [(i, i ^ mask) for i in range(peers)])  10.2 us
    ppermute x7, starting transfers between devices, across(): return lax.ppermute(x, axis, swap)  6.71 us
    ppermute x7, waiting for transfers between devices, flip(): return lax.ppermute(x, 'tm', [(i, i ^ mask) for i in range(peers)])  4.99 us
    ppermute x2, starting transfers between devices, fast(): mine[m + 1] = lax.ppermute(last, 'tm', onward)  4.11 us
    ppermute x3, starting transfers between devices, fast(): mine[m] = lax.ppermute(mine[m - 2], 'tm', onward)  3.98 us
    ppermute x7, waiting for transfers between devices, across(): return lax.ppermute(x, axis, swap)  2.88 us
  transfers between devices with their start and end apart: 19, of which 6 were waited for; matrix products, arithmetic and copies ran while one was open for 3% of the time, Pallas kernels for 10%

profile of v1, /device:TPU:0, one launch (start us, length us, event | category | flops | bytes accessed | tf_op | source)
XLA Modules:
  0.0 66.7 jit_solution(16513465868268092047)
XLA Ops:
  0.1 1.1 %copy-done.1 = bf16[1,4,32,2240]{3,2,1,0:T(8,128)(2,1)S(1)} copy-done((bf16[1,4,32,2240]{3,2,1,0:T(8,128)(2,1)S(1)}, bf16[1,4,32,2240]{3,2,1,0:T(8,128)(2,1)}, u32[]{:S(2)}) %copy-start.1) | copy-done | bytes 573464
  1.2 1.1 %copy-done.2 = bf16[1,4,32,2240]{3,2,1,0:T(8,128)(2,1)S(1)} copy-done((bf16[1,4,32,2240]{3,2,1,0:T(8,128)(2,1)S(1)}, bf16[1,4,32,2240]{3,2,1,0:T(8,128)(2,1)}, u32[]{:S(2)}) %copy-start.2) | copy-done | bytes 573464
  2.3 1.0 %shard_map.55 = (f32[40,1152]{1,0:T(8,128)S(1)}, f32[40,1152]{1,0:T(8,128)S(1)}) custom-call(s32[3]{0:T(128)S(1)} %pad_add_fusion.at_ref, bf16[128,2240]{1,0:T(8,128)(2,1)S(1)} %bitcast.10, bf16[128,2240]{1,0:T(8,128)(2,1)S(1)} %bitcast.11), custom_call_target="tpu_custom_call" | custom-call | flops 73400320 | bytes 1515532 | tf_op jit(solution)/shard_map/pallas_call | solution.py:27
  3.3 0.6 collective-permute-start.1
  3.9 1.1 %collective-permute-done.1 = f32[40,1152]{1,0:T(8,128)S(1)} collective-permute-done((f32[40,1152]{1,0:T(8,128)S(1)}, f32[40,1152]{1,0:T(8,128)S(1)}, u32[]{:S(2)}, u32[]{:S(2)}) %collective-permute-start.1) | collective-permute-done | bytes 184352 | tf_op jit(solution)/shard_map/ppermute | solution.py:216
  5.0 2.9 %collective-permute-start.2 = (bf16[40,1152]{1,0:T(8,128)(2,1)S(1)}, bf16[40,1152]{1,0:T(8,128)(2,1)S(1)}, u32[]{:S(2)}, u32[]{:S(2)}) collective-permute-start(bf16[40,1152]{1,0:T(8,128)(2,1)S(1)} %get-tuple-element.17), channel_id=1, source_target_pairs={{0,2},{2,0},{4,6},{6,4},{8,10},{10,8},{12,14},{14,12},{1,3},{3,1},... | collective-permute-start | bytes 276488 | tf_op jit(solution)/shard_map/ppermute | solution.py:213
  7.9 1.0 %shard_map.57 = (bf16[144,1152]{1,0:T(8,128)(2,1)S(1)}, bf16[2,144,1152]{2,1,0:T(8,128)(2,1)S(1)}) custom-call(s32[3]{0:T(128)S(1)} %pad_add_fusion.at_ref, bf16[1,1,313600]{2,1,0:T(2,128)(2,1)S(1)} %copy-done), custom_call_target="tpu_custom_call" | custom-call | bytes 1622540 | tf_op jit(solution)/shard_map/pallas_call | solution.py:27
  8.9 1.6 %collective-permute-start.8 = (bf16[144,1152]{1,0:T(8,128)(2,1)S(1)}, bf16[144,1152]{1,0:T(8,128)(2,1)S(1)}, u32[]{:S(2)}, u32[]{:S(2)}) collective-permute-start(bf16[144,1152]{1,0:T(8,128)(2,1)S(1)} %get-tuple-element.16.refs_0_), channel_id=1, source_target_pairs={{0,4},{2,6},{4,12},{6,14},{12,8},{14,10},{8,0},{10,2},{1,5},{3,7},... | collective-permute-start | bytes 995336 | tf_op jit(solution)/shard_map/ppermute | solution.py:241
  11.1 2.7 %collective-permute-start.3 = (bf16[40,1152]{1,0:T(8,128)(2,1)S(1)}, bf16[40,1152]{1,0:T(8,128)(2,1)S(1)}, u32[]{:S(2)}, u32[]{:S(2)}) collective-permute-start(bf16[40,1152]{1,0:T(8,128)(2,1)S(1)} %fusion.4), channel_id=1, source_target_pairs={{0,4},{2,6},{4,0},{6,2},{8,12},{10,14},{12,8},{14,10},{1,5},{3,7},... | collective-permute-start | bytes 276488 | tf_op jit(solution)/shard_map/ppermute | solution.py:213
  13.7 5.8 %collective-permute-done.8.refs_2_ = bf16[144,1152]{1,0:T(8,128)(2,1)S(1)} collective-permute-done((bf16[144,1152]{1,0:T(8,128)(2,1)S(1)}, bf16[144,1152]{1,0:T(8,128)(2,1)S(1)}, u32[]{:S(2)}, u32[]{:S(2)}) %collective-permute-start.8) | collective-permute-done | bytes 331808 | tf_op jit(solution)/shard_map/ppermute | solution.py:241
  19.5 1.6 %collective-permute-start.9 = (bf16[144,1152]{1,0:T(8,128)(2,1)S(1)}, bf16[144,1152]{1,0:T(8,128)(2,1)S(1)}, u32[]{:S(2)}, u32[]{:S(2)}) collective-permute-start(bf16[144,1152]{1,0:T(8,128)(2,1)S(1)} %collective-permute-done.8.refs_2_), channel_id=1, source_target_pairs={{0,4},{2,6},{4,12},{6,14},{12,8},{14,10},{8,0},{10,2},{1,5},{3,7},... | collective-permute-start | bytes 995336 | tf_op jit(solution)/shard_map/ppermute | solution.py:241
  21.1 1.5 %collective-permute-start.15 = (bf16[144,1152]{1,0:T(8,128)(2,1)S(1)}, bf16[144,1152]{1,0:T(8,128)(2,1)}, u32[]{:S(2)}, u32[]{:S(2)}) collective-permute-start(bf16[144,1152]{1,0:T(8,128)(2,1)S(1)} %collective-permute-done.8.refs_2_), channel_id=1, source_target_pairs={{0,16},{16,0},{1,17},{17,1},{2,18},{18,2},{3,19},{19,3},{4,20},{20... | collective-permute-start | bytes 995336 | tf_op jit(solution)/shard_map/ppermute | solution.py:216
  22.6 1.4 %collective-permute-start.4 = (bf16[40,1152]{1,0:T(8,128)(2,1)S(1)}, bf16[40,1152]{1,0:T(8,128)(2,1)S(1)}, u32[]{:S(2)}, u32[]{:S(2)}) collective-permute-start(bf16[40,1152]{1,0:T(8,128)(2,1)S(1)} %fusion.3), channel_id=1, source_target_pairs={{0,8},{2,10},{4,12},{6,14},{8,0},{10,2},{12,4},{14,6},{1,9},{3,11}... | collective-permute-start | bytes 276488 | tf_op jit(solution)/shard_map/ppermute | solution.py:213
  24.1 8.3 %collective-permute-done.9.refs_4_ = bf16[144,1152]{1,0:T(8,128)(2,1)S(1)} collective-permute-done((bf16[144,1152]{1,0:T(8,128)(2,1)S(1)}, bf16[144,1152]{1,0:T(8,128)(2,1)S(1)}, u32[]{:S(2)}, u32[]{:S(2)}) %collective-permute-start.9) | collective-permute-done | bytes 331808 | tf_op jit(solution)/shard_map/ppermute | solution.py:241
  32.4 0.8 %collective-permute-start.12 = (bf16[144,1152]{1,0:T(8,128)(2,1)S(1)}, bf16[144,1152]{1,0:T(8,128)(2,1)}, u32[]{:S(2)}, u32[]{:S(2)}) collective-permute-start(bf16[144,1152]{1,0:T(8,128)(2,1)S(1)} %collective-permute-done.9.refs_4_), channel_id=1, source_target_pairs={{0,4},{2,6},{4,12},{6,14},{12,8},{14,10},{8,0},{10,2},{1,5},{3,7},... | collective-permute-start | bytes 995336 | tf_op jit(solution)/shard_map/ppermute | solution.py:241
  33.2 1.5 %collective-permute-start.10 = (bf16[144,1152]{1,0:T(8,128)(2,1)S(1)}, bf16[144,1152]{1,0:T(8,128)(2,1)}, u32[]{:S(2)}, u32[]{:S(2)}) collective-permute-start(bf16[144,1152]{1,0:T(8,128)(2,1)S(1)} %collective-permute-done.9.refs_4_), channel_id=1, source_target_pairs={{0,16},{16,0},{1,17},{17,1},{2,18},{18,2},{3,19},{19,3},{4,20},{20... | collective-permute-start | bytes 995336 | tf_op jit(solution)/shard_map/ppermute | solution.py:216
  34.7 0.8 %slice_bitcast_fusion = bf16[144,1152]{1,0:T(8,128)(2,1)} fusion(bf16[2,144,1152]{2,1,0:T(8,128)(2,1)S(1)} %collective-permute-done.5.refs_1_), kind=kLoop, calls=%fused_computation | loop fusion | bytes 663552 | tf_op jit(solution)/shard_map/squeeze | solution.py:244
  35.5 3.4 %collective-permute-start.6 = (bf16[144,1152]{1,0:T(8,128)(2,1)}, bf16[144,1152]{1,0:T(8,128)(2,1)}, u32[]{:S(2)}, u32[]{:S(2)}) collective-permute-start(bf16[144,1152]{1,0:T(8,128)(2,1)} %slice_bitcast_fusion), channel_id=1, source_target_pairs={{0,4},{2,6},{4,12},{6,14},{12,8},{14,10},{8,0},{10,2},{1,5},{3,7},... | collective-permute-start | bytes 995336 | tf_op jit(solution)/shard_map/ppermute | solution.py:245
  38.9 4.9 %collective-permute-done.12.refs_5_ = bf16[144,1152]{1,0:T(8,128)(2,1)} collective-permute-done((bf16[144,1152]{1,0:T(8,128)(2,1)S(1)}, bf16[144,1152]{1,0:T(8,128)(2,1)}, u32[]{:S(2)}, u32[]{:S(2)}) %collective-permute-start.12) | collective-permute-done | bytes 331808 | tf_op jit(solution)/shard_map/ppermute | solution.py:241
  43.8 0.8 %collective-permute-start.13 = (bf16[144,1152]{1,0:T(8,128)(2,1)}, bf16[144,1152]{1,0:T(8,128)(2,1)}, u32[]{:S(2)}, u32[]{:S(2)}) collective-permute-start(bf16[144,1152]{1,0:T(8,128)(2,1)} %collective-permute-done.12.refs_5_), channel_id=1, source_target_pairs={{0,2},{2,0},{4,6},{6,4},{8,10},{10,8},{12,14},{14,12},{1,3},{3,1},... | collective-permute-start | bytes 995336 | tf_op jit(solution)/shard_map/ppermute | solution.py:213
  44.6 1.3 %collective-permute-start.16 = (bf16[144,1152]{1,0:T(8,128)(2,1)}, bf16[144,1152]{1,0:T(8,128)(2,1)S(1)}, u32[]{:S(2)}, u32[]{:S(2)}) collective-permute-start(bf16[144,1152]{1,0:T(8,128)(2,1)} %collective-permute-done.15.refs_8_), channel_id=1, source_target_pairs={{0,2},{2,0},{4,6},{6,4},{8,10},{10,8},{12,14},{14,12},{1,3},{3,1},... | collective-permute-start | bytes 995336 | tf_op jit(solution)/shard_map/ppermute | solution.py:213
  45.9 1.5 %collective-permute-start.17 = (bf16[144,1152]{1,0:T(8,128)(2,1)}, bf16[144,1152]{1,0:T(8,128)(2,1)S(1)}, u32[]{:S(2)}, u32[]{:S(2)}) collective-permute-start(bf16[144,1152]{1,0:T(8,128)(2,1)} %collective-permute-done.12.refs_5_), channel_id=1, source_target_pairs={{0,16},{16,0},{1,17},{17,1},{2,18},{18,2},{3,19},{19,3},{4,20},{20... | collective-permute-start | bytes 995336 | tf_op jit(solution)/shard_map/ppermute | solution.py:216
  48.0 0.7 %collective-permute-start.7 = (bf16[144,1152]{1,0:T(8,128)(2,1)}, bf16[144,1152]{1,0:T(8,128)(2,1)S(1)}, u32[]{:S(2)}, u32[]{:S(2)}) collective-permute-start(bf16[144,1152]{1,0:T(8,128)(2,1)} %collective-permute-done.6.refs_3_), channel_id=1, source_target_pairs={{0,4},{2,6},{4,12},{6,14},{12,8},{14,10},{8,0},{10,2},{1,5},{3,7},... | collective-permute-start | bytes 995336 | tf_op jit(solution)/shard_map/ppermute | solution.py:245
  48.6 5.0 %collective-permute-done.13.refs_6_ = bf16[144,1152]{1,0:T(8,128)(2,1)} collective-permute-done((bf16[144,1152]{1,0:T(8,128)(2,1)}, bf16[144,1152]{1,0:T(8,128)(2,1)}, u32[]{:S(2)}, u32[]{:S(2)}) %collective-permute-start.13) | collective-permute-done | bytes 331808 | tf_op jit(solution)/shard_map/ppermute | solution.py:213
  53.6 1.5 %collective-permute-start.14 = (bf16[144,1152]{1,0:T(8,128)(2,1)}, bf16[144,1152]{1,0:T(8,128)(2,1)S(1)}, u32[]{:S(2)}, u32[]{:S(2)}) collective-permute-start(bf16[144,1152]{1,0:T(8,128)(2,1)} %collective-permute-done.13.refs_6_), channel_id=1, source_target_pairs={{0,16},{16,0},{1,17},{17,1},{2,18},{18,2},{3,19},{19,3},{4,20},{20... | collective-permute-start | bytes 995336 | tf_op jit(solution)/shard_map/ppermute | solution.py:216
  55.1 1.1 %fusion.2.s_ref = f32[40,1152]{1,0:T(8,128)S(1)} fusion(f32[40,1152]{1,0:T(8,128)} %copy-done.4, bf16[40,1152]{1,0:T(8,128)(2,1)} %copy-done.5, bf16[40,1152]{1,0:T(8,128)(2,1)} %copy-done.6, bf16[40,1152]{1,0:T(8,128)(2,1)} %copy-done.7, pred[]{:T(512)S(6)} %ne.11, pred[]{:T(512)S(6)} %ne.10, pred[]{:T(512)S(6)} %ne.9), kind=kLoop, calls=%fused_computation.7 | loop fusion | flops 414720 | bytes 645123 | tf_op jit(solution)/shard_map/add | solution.py:267
  56.3 1.9 %shard_map.56 = (bf16[256,1152]{1,0:T(8,128)(2,1)S(1)}, f32[256,128]{1,0:T(8,128)S(1)}) custom-call(s32[3]{0:T(128)S(1)} %pad_add_fusion.at_ref, bf16[128,2240]{1,0:T(8,128)(2,1)S(1)} %bitcast.12, bf16[128,2240]{1,0:T(8,128)(2,1)S(1)} %bitcast.13, f32[40,1152]{1,0:T(8,128)S(1)} %fusion.2.s_ref, f32[1,2240]{1,0:T(1,128)S(1)} %reshape.22.g_ref), custom_call_target="tpu_custom_call" | custom-call | flops 150994944 | bytes 2061068 | tf_op jit(solution)/shard_map/pallas_call | solution.py:27
  58.2 2.9 %shard_map.58.refs_3_ = f32[2,256,1152]{2,1,0:T(8,128)S(1)} custom-call(s32[3]{0:T(128)S(1)} %pad_add_fusion.at_ref, bf16[256,1152]{1,0:T(8,128)(2,1)S(1)} %get-tuple-element.13.left_ref, f32[256,128]{1,0:T(8,128)S(1)} %get-tuple-element.14.square_ref, bf16[144,1152]{1,0:T(8,128)(2,1)S(1)} %get-tuple-element.16.refs_0_, ...), custom_call_target="tpu_custom_call" | custom-call | flops 1104150528 | bytes 7725068 | tf_op jit(solution)/shard_map/pallas_call | solution.py:27
  61.2 1.0 %shard_map.60 = f32[2,128,1152]{2,1,0:T(8,128)S(1)} custom-call(s32[3]{0:T(128)S(1)} %pad_add_fusion.at_ref, bf16[256,1152]{1,0:T(8,128)(2,1)S(1)} %get-tuple-element.13.left_ref, f32[256,128]{1,0:T(8,128)S(1)} %get-tuple-element.14.square_ref, bf16[144,1152]{1,0:T(8,128)(2,1)S(1)} %collective-permute-done.7.refs_0_, ...), custom_call_target="tpu_custom_call" | custom-call | flops 127401984 | bytes 5255180 | tf_op jit(solution)/shard_map/pallas_call | solution.py:27
  62.3 1.0 %shard_map.59.own_ref = f32[2,128,1152]{2,1,0:T(8,128)S(1)} custom-call(s32[3]{0:T(128)S(1)} %pad_add_fusion.at_ref, bf16[256,1152]{1,0:T(8,128)(2,1)S(1)} %get-tuple-element.13.left_ref, f32[256,128]{1,0:T(8,128)S(1)} %get-tuple-element.14.square_ref, bf16[144,1152]{1,0:T(8,128)(2,1)S(1)} %collective-permute-done.7.refs_0_, ...), custom_call_target="tpu_custom_call" | custom-call | flops 127401984 | bytes 5255180 | tf_op jit(solution)/shard_map/pallas_call | solution.py:27
  63.3 1.8 %collective-permute-done.18.got_ref = f32[2,128,1152]{2,1,0:T(8,128)S(1)} collective-permute-done((f32[2,128,1152]{2,1,0:T(8,128)S(1)}, f32[2,128,1152]{2,1,0:T(8,128)S(1)}, u32[]{:S(2)}, u32[]{:S(2)}) %collective-permute-start.18) | collective-permute-done | bytes 1179680 | tf_op jit(solution)/shard_map/ppermute | solution.py:216
  65.1 1.5 %shard_map.61 = bf16[128,2240]{1,0:T(8,128)(2,1)} custom-call(s32[3]{0:T(128)S(1)} %pad_add_fusion.at_ref, f32[2,128,1152]{2,1,0:T(8,128)S(1)} %shard_map.59.own_ref, f32[2,128,1152]{2,1,0:T(8,128)S(1)} %collective-permute-done.18.got_ref), custom_call_target="tpu_custom_call" | custom-call | bytes 2932748 | tf_op jit(solution)/shard_map/pallas_call | solution.py:27
  (38 shorter events, 1.4 us)
Async XLA Ops:
  0.0 7.9 %copy-start = (bf16[1,1,313600]{2,1,0:T(2,128)(2,1)S(1)}, bf16[1,1,313600]{2,1,0:T(2,128)(2,1)}, u32[]{:S(2)}) copy-start(bf16[1,1,313600]{2,1,0:T(2,128)(2,1)} %w_ref.1) | copy-start | bytes 1881604
  0.1 1.2 %copy-start.1 = (bf16[1,4,32,2240]{3,2,1,0:T(8,128)(2,1)S(1)}, bf16[1,4,32,2240]{3,2,1,0:T(8,128)(2,1)}, u32[]{:S(2)}) copy-start(bf16[1,4,32,2240]{3,2,1,0:T(8,128)(2,1)} %param.6) | copy-start | bytes 1720324
  1.2 1.1 %copy-start.2 = (bf16[1,4,32,2240]{3,2,1,0:T(8,128)(2,1)S(1)}, bf16[1,4,32,2240]{3,2,1,0:T(8,128)(2,1)}, u32[]{:S(2)}) copy-start(bf16[1,4,32,2240]{3,2,1,0:T(8,128)(2,1)} %param.7) | copy-start | bytes 1720324
  3.3 10.4 %copy-start.3 = (bf16[1,4,32,2240]{3,2,1,0:T(8,128)(2,1)S(1)}, bf16[1,4,32,2240]{3,2,1,0:T(8,128)(2,1)}, u32[]{:S(2)}) copy-start(bf16[1,4,32,2240]{3,2,1,0:T(8,128)(2,1)} %param.5) | copy-start | bytes 1720324
  3.3 1.6 %collective-permute-start.1 = (f32[40,1152]{1,0:T(8,128)S(1)}, f32[40,1152]{1,0:T(8,128)S(1)}, u32[]{:S(2)}, u32[]{:S(2)}) collective-permute-start(f32[40,1152]{1,0:T(8,128)S(1)} %get-tuple-element.12), channel_id=1, source_target_pairs={{0,1},{1,0},{2,3},{3,2},{4,5},{5,4},{6,7},{7,6},{8,9},{9,8},{10,11... | collective-permute-start | bytes 552968 | tf_op jit(solution)/shard_map/ppermute | solution.py:216
  5.0 30.5 %copy-start.4 = (f32[40,1152]{1,0:T(8,128)}, f32[40,1152]{1,0:T(8,128)S(1)}, u32[]{:S(2)}) copy-start(f32[40,1152]{1,0:T(8,128)S(1)} %get-tuple-element.18) | copy-start | bytes 552964
  5.0 39.6 %copy-start.8 = (f32[2240]{0:T(1024)S(1)}, f32[2240]{0:T(1024)}, u32[]{:S(2)}) copy-start(f32[2240]{0:T(1024)} %param.8) | copy-start | bytes 26884
  5.0 6.1 %collective-permute-start.2 = (bf16[40,1152]{1,0:T(8,128)(2,1)S(1)}, bf16[40,1152]{1,0:T(8,128)(2,1)S(1)}, u32[]{:S(2)}, u32[]{:S(2)}) collective-permute-start(bf16[40,1152]{1,0:T(8,128)(2,1)S(1)} %get-tuple-element.17), channel_id=1, source_target_pairs={{0,2},{2,0},{4,6},{6,4},{8,10},{10,8},{12,14},{14,12},{1,3},{3,1},... | collective-permute-start | bytes 276488 | tf_op jit(solution)/shard_map/ppermute | solution.py:213
  8.9 10.6 %collective-permute-start.8 = (bf16[144,1152]{1,0:T(8,128)(2,1)S(1)}, bf16[144,1152]{1,0:T(8,128)(2,1)S(1)}, u32[]{:S(2)}, u32[]{:S(2)}) collective-permute-start(bf16[144,1152]{1,0:T(8,128)(2,1)S(1)} %get-tuple-element.16.refs_0_), channel_id=1, source_target_pairs={{0,4},{2,6},{4,12},{6,14},{12,8},{14,10},{8,0},{10,2},{1,5},{3,7},... | collective-permute-start | bytes 995336 | tf_op jit(solution)/shard_map/ppermute | solution.py:241
  10.5 22.7 %collective-permute-start.5 = (bf16[2,144,1152]{2,1,0:T(8,128)(2,1)S(1)}, bf16[2,144,1152]{2,1,0:T(8,128)(2,1)S(1)}, u32[]{:S(2)}, u32[]{:S(2)}) collective-permute-start(bf16[2,144,1152]{2,1,0:T(8,128)(2,1)S(1)} %get-tuple-element.15.refs_7_), channel_id=1, source_target_pairs={{0,2},{2,0},{4,6},{6,4},{8,10},{10,8},{12,14},{14,12},{1,3},{3,1},... | collective-permute-start | bytes 1990664 | tf_op jit(solution)/shard_map/ppermute | solution.py:213
  11.1 32.7 %copy-start.5 = (bf16[40,1152]{1,0:T(8,128)(2,1)}, bf16[40,1152]{1,0:T(8,128)(2,1)S(1)}, u32[]{:S(2)}) copy-start(bf16[40,1152]{1,0:T(8,128)(2,1)S(1)} %collective-permute-done.2) | copy-start | bytes 276484
  11.1 11.5 %collective-permute-start.3 = (bf16[40,1152]{1,0:T(8,128)(2,1)S(1)}, bf16[40,1152]{1,0:T(8,128)(2,1)S(1)}, u32[]{:S(2)}, u32[]{:S(2)}) collective-permute-start(bf16[40,1152]{1,0:T(8,128)(2,1)S(1)} %fusion.4), channel_id=1, source_target_pairs={{0,4},{2,6},{4,0},{6,2},{8,12},{10,14},{12,8},{14,10},{1,5},{3,7},... | collective-permute-start | bytes 276488 | tf_op jit(solution)/shard_map/ppermute | solution.py:213
  13.7 32.2 %collective-permute-start = (bf16[1,4,32,2240]{3,2,1,0:T(8,128)(2,1)S(1)}, bf16[1,4,32,2240]{3,2,1,0:T(8,128)(2,1)S(1)}, u32[]{:S(2)}, u32[]{:S(2)}) collective-permute-start(bf16[1,4,32,2240]{3,2,1,0:T(8,128)(2,1)S(1)} %copy-done.3), channel_id=1, source_target_pairs={{0,1},{1,0},{2,3},{3,2},{4,5},{5,4},{6,7},{7,6},{8,9},{9,8},{10,11... | collective-permute-start | bytes 1720328 | tf_op jit(solution)/shard_map/ppermute | solution.py:216
  19.5 12.9 %collective-permute-start.9 = (bf16[144,1152]{1,0:T(8,128)(2,1)S(1)}, bf16[144,1152]{1,0:T(8,128)(2,1)S(1)}, u32[]{:S(2)}, u32[]{:S(2)}) collective-permute-start(bf16[144,1152]{1,0:T(8,128)(2,1)S(1)} %collective-permute-done.8.refs_2_), channel_id=1, source_target_pairs={{0,4},{2,6},{4,12},{6,14},{12,8},{14,10},{8,0},{10,2},{1,5},{3,7},... | collective-permute-start | bytes 995336 | tf_op jit(solution)/shard_map/ppermute | solution.py:241
  21.1 23.5 %collective-permute-start.15 = (bf16[144,1152]{1,0:T(8,128)(2,1)S(1)}, bf16[144,1152]{1,0:T(8,128)(2,1)}, u32[]{:S(2)}, u32[]{:S(2)}) collective-permute-start(bf16[144,1152]{1,0:T(8,128)(2,1)S(1)} %collective-permute-done.8.refs_2_), channel_id=1, source_target_pairs={{0,16},{16,0},{1,17},{17,1},{2,18},{18,2},{3,19},{19,3},{4,20},{20... | collective-permute-start | bytes 995336 | tf_op jit(solution)/shard_map/ppermute | solution.py:216
  22.6 10.6 %copy-start.6 = (bf16[40,1152]{1,0:T(8,128)(2,1)}, bf16[40,1152]{1,0:T(8,128)(2,1)S(1)}, u32[]{:S(2)}) copy-start(bf16[40,1152]{1,0:T(8,128)(2,1)S(1)} %collective-permute-done.3) | copy-start | bytes 276484
  22.6 12.8 %collective-permute-start.4 = (bf16[40,1152]{1,0:T(8,128)(2,1)S(1)}, bf16[40,1152]{1,0:T(8,128)(2,1)S(1)}, u32[]{:S(2)}, u32[]{:S(2)}) collective-permute-start(bf16[40,1152]{1,0:T(8,128)(2,1)S(1)} %fusion.3), channel_id=1, source_target_pairs={{0,8},{2,10},{4,12},{6,14},{8,0},{10,2},{12,4},{14,6},{1,9},{3,11}... | collective-permute-start | bytes 276488 | tf_op jit(solution)/shard_map/ppermute | solution.py:213
  32.4 11.4 %collective-permute-start.12 = (bf16[144,1152]{1,0:T(8,128)(2,1)S(1)}, bf16[144,1152]{1,0:T(8,128)(2,1)}, u32[]{:S(2)}, u32[]{:S(2)}) collective-permute-start(bf16[144,1152]{1,0:T(8,128)(2,1)S(1)} %collective-permute-done.9.refs_4_), channel_id=1, source_target_pairs={{0,4},{2,6},{4,12},{6,14},{12,8},{14,10},{8,0},{10,2},{1,5},{3,7},... | collective-permute-start | bytes 995336 | tf_op jit(solution)/shard_map/ppermute | solution.py:241
  33.2 14.2 %collective-permute-start.10 = (bf16[144,1152]{1,0:T(8,128)(2,1)S(1)}, bf16[144,1152]{1,0:T(8,128)(2,1)}, u32[]{:S(2)}, u32[]{:S(2)}) collective-permute-start(bf16[144,1152]{1,0:T(8,128)(2,1)S(1)} %collective-permute-done.9.refs_4_), channel_id=1, source_target_pairs={{0,16},{16,0},{1,17},{17,1},{2,18},{18,2},{3,19},{19,3},{4,20},{20... | collective-permute-start | bytes 995336 | tf_op jit(solution)/shard_map/ppermute | solution.py:216
  35.5 8.3 %copy-start.7 = (bf16[40,1152]{1,0:T(8,128)(2,1)}, bf16[40,1152]{1,0:T(8,128)(2,1)S(1)}, u32[]{:S(2)}) copy-start(bf16[40,1152]{1,0:T(8,128)(2,1)S(1)} %collective-permute-done.4) | copy-start | bytes 276484
  35.5 12.5 %collective-permute-start.6 = (bf16[144,1152]{1,0:T(8,128)(2,1)}, bf16[144,1152]{1,0:T(8,128)(2,1)}, u32[]{:S(2)}, u32[]{:S(2)}) collective-permute-start(bf16[144,1152]{1,0:T(8,128)(2,1)} %slice_bitcast_fusion), channel_id=1, source_target_pairs={{0,4},{2,6},{4,12},{6,14},{12,8},{14,10},{8,0},{10,2},{1,5},{3,7},... | collective-permute-start | bytes 995336 | tf_op jit(solution)/shard_map/ppermute | solution.py:245
  43.8 9.8 %collective-permute-start.13 = (bf16[144,1152]{1,0:T(8,128)(2,1)}, bf16[144,1152]{1,0:T(8,128)(2,1)}, u32[]{:S(2)}, u32[]{:S(2)}) collective-permute-start(bf16[144,1152]{1,0:T(8,128)(2,1)} %collective-permute-done.12.refs_5_), channel_id=1, source_target_pairs={{0,2},{2,0},{4,6},{6,4},{8,10},{10,8},{12,14},{14,12},{1,3},{3,1},... | collective-permute-start | bytes 995336 | tf_op jit(solution)/shard_map/ppermute | solution.py:213
  44.6 13.6 %collective-permute-start.16 = (bf16[144,1152]{1,0:T(8,128)(2,1)}, bf16[144,1152]{1,0:T(8,128)(2,1)S(1)}, u32[]{:S(2)}, u32[]{:S(2)}) collective-permute-start(bf16[144,1152]{1,0:T(8,128)(2,1)} %collective-permute-done.15.refs_8_), channel_id=1, source_target_pairs={{0,2},{2,0},{4,6},{6,4},{8,10},{10,8},{12,14},{14,12},{1,3},{3,1},... | collective-permute-start | bytes 995336 | tf_op jit(solution)/shard_map/ppermute | solution.py:213
  45.9 12.3 %collective-permute-start.17 = (bf16[144,1152]{1,0:T(8,128)(2,1)}, bf16[144,1152]{1,0:T(8,128)(2,1)S(1)}, u32[]{:S(2)}, u32[]{:S(2)}) collective-permute-start(bf16[144,1152]{1,0:T(8,128)(2,1)} %collective-permute-done.12.refs_5_), channel_id=1, source_target_pairs={{0,16},{16,0},{1,17},{17,1},{2,18},{18,2},{3,19},{19,3},{4,20},{20... | collective-permute-start | bytes 995336 | tf_op jit(solution)/shard_map/ppermute | solution.py:216
  47.4 13.7 %collective-permute-start.11 = (bf16[144,1152]{1,0:T(8,128)(2,1)}, bf16[144,1152]{1,0:T(8,128)(2,1)S(1)}, u32[]{:S(2)}, u32[]{:S(2)}) collective-permute-start(bf16[144,1152]{1,0:T(8,128)(2,1)} %collective-permute-done.10.refs_10_), channel_id=1, source_target_pairs={{0,2},{2,0},{4,6},{6,4},{8,10},{10,8},{12,14},{14,12},{1,3},{3,1},... | collective-permute-start | bytes 995336 | tf_op jit(solution)/shard_map/ppermute | solution.py:213
  48.0 13.2 %collective-permute-start.7 = (bf16[144,1152]{1,0:T(8,128)(2,1)}, bf16[144,1152]{1,0:T(8,128)(2,1)S(1)}, u32[]{:S(2)}, u32[]{:S(2)}) collective-permute-start(bf16[144,1152]{1,0:T(8,128)(2,1)} %collective-permute-done.6.refs_3_), channel_id=1, source_target_pairs={{0,4},{2,6},{4,12},{6,14},{12,8},{14,10},{8,0},{10,2},{1,5},{3,7},... | collective-permute-start | bytes 995336 | tf_op jit(solution)/shard_map/ppermute | solution.py:245
  53.6 7.6 %collective-permute-start.14 = (bf16[144,1152]{1,0:T(8,128)(2,1)}, bf16[144,1152]{1,0:T(8,128)(2,1)S(1)}, u32[]{:S(2)}, u32[]{:S(2)}) collective-permute-start(bf16[144,1152]{1,0:T(8,128)(2,1)} %collective-permute-done.13.refs_6_), channel_id=1, source_target_pairs={{0,16},{16,0},{1,17},{17,1},{2,18},{18,2},{3,19},{19,3},{4,20},{20... | collective-permute-start | bytes 995336 | tf_op jit(solution)/shard_map/ppermute | solution.py:216
  62.2 2.9 %collective-permute-start.18 = (f32[2,128,1152]{2,1,0:T(8,128)S(1)}, f32[2,128,1152]{2,1,0:T(8,128)S(1)}, u32[]{:S(2)}, u32[]{:S(2)}) collective-permute-start(f32[2,128,1152]{2,1,0:T(8,128)S(1)} %shard_map.60), channel_id=1, source_target_pairs={{0,1},{1,0},{2,3},{3,2},{4,5},{5,4},{6,7},{7,6},{8,9},{9,8},{10,11... | collective-permute-start | bytes 3538952 | tf_op jit(solution)/shard_map/ppermute | solution.py:216

commit v2 on v1

--- a/solution.py
+++ b/solution.py
@@ -106,7 +106,14 @@
         other_ref[:, 0:half] = sums[:, 0:half]
 
 
-def read_states(half, shard, slots, at_ref, q_ref, p_ref, s_ref, g_ref, left_ref, square_ref, qh, gh, flat, blocks):
+def read_states(half, shard, slots, at_ref, q_ref, p_ref, g_ref, total_ref, *refs):
+    steps = slots.bit_length() - 1
+    scanned = refs[:steps]
+    left_ref, square_ref, qh, gh, flat, blocks, s_ref = refs[steps:]
+    s_ref[...] = total_ref[...]
+    for step, got in enumerate(scanned):
+        reached = (at_ref[2] >> step) % 2 == 1
+        s_ref[...] += jnp.where(reached, got[...].astype(jnp.float32), 0.0)
     count = q_ref.shape[0]
     qh[...] = jnp.zeros_like(qh)
     gh[...] = jnp.zeros_like(gh)
@@ -163,38 +170,50 @@
         left_ref[:, wide * m : wide * (m + 1)] = blocks[2 * source + (x ^ (m % 2))]
 
 
-def project(first, last, sides, plan, spare, at_ref, left_ref, square_ref, *refs):
-    refs = list(refs)
-    out_ref = refs.pop()
-    count = 1 + max(at for pieces in plan for at, _ in pieces)
-    base = refs[count] if len(refs) > count else None
-    pieces = [
-        [refs[at][...] if part is None else refs[at][part] for at, part in side] for side in plan
-    ]
-    wide = (pieces[0] + pieces[1])[0].shape[0]
+def product(left_ref, first, last, slots, pieces):
+    weight = jnp.concatenate(
+        [ref[...] if part is None else ref[part] for ref, part in pieces], axis=0
+    )
+    wide = weight.shape[0] // len(slots)
+    left = jnp.concatenate(
+        [left_ref[first:last, wide * m : wide * (m + 1)] for m in slots], axis=1
+    )
+    return jnp.dot(left, weight, preferred_element_type=jnp.float32)
+
+
+def project_early(sides, plan, left_ref, *refs):
+    outs = refs[-4:]
+    count = outs[0].shape[0]
     for i, slots in enumerate(sides):
-        weight = jnp.concatenate(pieces[i], axis=0)
-        left = jnp.concatenate(
-            [left_ref[first:last, wide * m : wide * (m + 1)] for m in slots], axis=1
-        )
-        total = jnp.dot(left, weight, preferred_element_type=jnp.float32)
-        out_ref[i] = total if base is None else total + base[i, first:last]
-    if base is not None:
-        tail = 1 - at_ref[0]
-        lane = lax.broadcasted_iota(jnp.int32, (last - first, LANES), 1)
-        cut = spare // LANES * LANES
-        out_ref[tail, :, cut : cut + LANES] = jnp.where(
-            lane == spare % LANES, square_ref[first:last], out_ref[tail, :, cut : cut + LANES]
-        )
-
-
-def finish(depth, spare, at_ref, own_ref, got_ref, out_ref):
-    half = own_ref.shape[2]
-    first, last = at_ref[0], 1 - at_ref[0]
-    right = own_ref[last] + got_ref[last]
-    scale = lax.rsqrt(right[:, spare : spare + 1] / depth + norm_epsilon)
-    out_ref[:, half:depth] = (right[:, : depth - half] * scale).astype(jnp.bfloat16)
-    out_ref[:, 0:half] = ((own_ref[first] + got_ref[first]) * scale).astype(jnp.bfloat16)
+        pieces = [(refs[place], part) for place, part in plan[i]]
+        total = product(left_ref, 0, 2 * count, slots, pieces)
+        outs[2 * i][...] = total[:count]
+        outs[2 * i + 1][...] = total[count:]
+
+
+def project_late(first, last, slots, left_ref, base_ref, *refs):
+    out_ref = refs[-1]
+    pieces = [(ref, None) for ref in refs[:-1]]
+    total = base_ref[...] + product(left_ref, first, last, slots, pieces)
+    out_ref[...] = total.astype(out_ref.dtype)
+
+
+def finish(depth, at_ref, square_ref, near_ref, mine_ref, got_mine_ref, rest_ref, got_rest_ref, out_ref):
+    count, half = mine_ref.shape
+    square = square_ref[0:count, 0:1] + near_ref[:, 0:1]
+    scale = lax.rsqrt(square / depth + norm_epsilon)
+    mine = ((mine_ref[...] + got_mine_ref[...].astype(jnp.float32)) * scale).astype(jnp.bfloat16)
+    rest = ((rest_ref[...] + got_rest_ref[...].astype(jnp.float32)) * scale).astype(jnp.bfloat16)
+
+    @pl.when(at_ref[0] == 0)
+    def _():
+        out_ref[:, 0:half] = mine
+        out_ref[:, half:depth] = rest[:, : depth - half]
+
+    @pl.when(at_ref[0] != 0)
+    def _():
+        out_ref[:, 0:half] = rest
+        out_ref[:, half:depth] = mine[:, : depth - half]
 
 
 def fast(query_tokens, key_tokens, value_tokens, norm_gain, out_weight):
@@ -206,7 +225,6 @@
     shard = out_weight.shape[-1] // depth
     tall = round_up(shard, 16)
     cols = round_up(depth, 2 * LANES) // 2
-    spare = depth - cols
     swap = [(0, 1), (1, 0)]
 
     def flip(x, mask):
@@ -260,54 +278,65 @@
     )
     total = own + across(other, "band")
     sent = total.astype(bf16)
-    prefix = total
-    step = 0
-    while 1 << step < peers:
-        got = flip(sent, 1 << step)
-        prefix = prefix + jnp.where((at[2] & (1 << step)) != 0, got.astype(f32), 0.0)
-        total = total + got.astype(f32)
-        sent = total.astype(bf16)
-        step += 1
+    running, scanned = total, []
+    while 1 << len(scanned) < peers:
+        step = len(scanned)
+        scanned.append(flip(sent, 1 << step))
+        running = running + scanned[-1].astype(f32)
+        sent = running.astype(bf16)
     left, square = call(
         functools.partial(read_states, half, shard, peers),
         (shape((2 * count, peers * tall), bf16), shape((2 * count, LANES), f32)),
-        (at, queries, partner, prefix, norm_gain.reshape(1, depth)),
+        (at, queries, partner, norm_gain.reshape(1, depth), total, *scanned),
         scratch=[
             pltpu.VMEM((2 * count, wide), bf16),
             pltpu.VMEM((1, wide), f32),
             pltpu.VMEM((2 * count, wide), bf16),
             pltpu.VMEM((peers, 2 * count, tall), bf16),
+            pltpu.VMEM((HD + 8, wide), f32),
         ],
         smem=1,
         flops=8 * count * LANES * wide,
     )
 
-    def partial_sums(first, last, slots, base):
-        arrays, plan = [], []
-        for chosen, held in zip(slots, (mine, rest)):
-            plan.append([])
-            for m in chosen:
-                array, part = held[m] if isinstance(held[m], tuple) else (held[m], None)
-                if not any(array is a for a in arrays):
-                    arrays.append(array)
-                plan[-1].append(([array is a for a in arrays].index(True), part))
-        return call(
-            functools.partial(project, first, last, slots, plan, spare),
-            shape((2, last - first, cols), f32),
-            (at, left, square, *arrays, *base),
-            smem=1,
-            flops=2 * (last - first) * cols * tall * sum(map(len, plan)),
-        )
-
+    near_square = across(square[count:], "band")
     late = ((peers - 3,), (peers - 3, peers - 1))
     soon = tuple(tuple(m for m in range(peers) if m not in side) for side in late)
-    base = partial_sums(0, 2 * count, soon, ())
-    other = partial_sums(count, 2 * count, late, (base,))
-    own = partial_sums(0, count, late, (base,))
+    arrays, plan = [], []
+    for chosen, held in zip(soon, (mine, rest)):
+        plan.append([])
+        for m in chosen:
+            array, part = held[m] if isinstance(held[m], tuple) else (held[m], None)
+            if not any(array is a for a in arrays):
+                arrays.append(array)
+            plan[-1].append(([array is a for a in arrays].index(True), part))
+    base = call(
+        functools.partial(project_early, soon, plan),
+        (shape((count, cols), f32),) * 4,
+        (left, *arrays),
+        flops=4 * count * cols * tall * sum(map(len, plan)),
+    )
+
+    def finished(side, held):
+        first = 2 * side
+        sums = []
+        for which, rows_from, dtype in (("other", count, bf16), ("own", 0, f32)):
+            sums.append(
+                call(
+                    functools.partial(project_late, rows_from, rows_from + count, late[side]),
+                    shape((count, cols), dtype),
+                    (left, base[first + (which == "other")], *[held[m] for m in late[side]]),
+                    flops=2 * count * cols * tall * len(late[side]),
+                )
+            )
+        return sums[1], across(sums[0], "band")
+
+    from_rest = finished(1, rest)
+    from_mine = finished(0, mine)
     out = call(
-        functools.partial(finish, depth, spare),
+        functools.partial(finish, depth),
         shape((count, depth), bf16),
-        (at, own, across(other, "band")),
+        (at, square, near_square, *from_mine, *from_rest),
         smem=1,
     )
     return out.reshape(frames, rows, width, depth)

time: 66.9 us -> 64.7 us (0.967)
  Pallas kernels: 10.4 us -> 8.45 us
  other arithmetic: 1.29 us -> 0.17 us
  waiting for transfers between devices: 26.8 us -> 27.9 us
  local copies, waits for them, and re-layouts: 3 us -> 2.27 us
    pallas_call x7 -> x9, Pallas kernels: 10.4 us -> 8.45 us  [call(): pl.pallas_call(kernel, out_shape=out, in_specs=[scalar] * smem + [whole]...]
    ppermute x7, waiting for transfers between devices: 4.99 us -> 6.51 us  [flip(): return lax.ppermute(x, 'tm', [(i, i ^ mask) for i in range(peers)])]
    ppermute x7 -> x9, waiting for transfers between devices: 2.88 us -> 1.57 us  [across(): return lax.ppermute(x, axis, swap)]
    add x1 -> x0, other arithmetic: 1.13 us -> none  [fast(): prefix = prefix + jnp.where(at[2] & 1 << step != 0, got.astype(f32), 0.0)]
    squeeze x1, local copies, waits for them, and re-layouts: 0.75 us -> 0.03 us  [fast(): last = beside[0] if k == 1 else mine[m - 1]]
    ppermute x7 -> x9, starting transfers between devices: 6.71 us -> 7.27 us  [across(): return lax.ppermute(x, axis, swap)]
    unnamed x18 -> x10, local copies, waits for them, and re-layouts: 2.25 us -> 2.23 us
  transfers between devices with their start and end apart: 19 -> 21, of which waited for: 6 -> 8; matrix products, arithmetic and copies ran while one was open for 3% -> 0% of each run, Pallas kernels for 10% -> 9%
where the time goes in v2:
time: 64.7 us; the launch traced here: 64.5 us
  waiting for transfers between devices  27.9 us (43%)
  starting transfers between devices  25.6 us (40%)
  Pallas kernels  8.45 us (13%)
  local copies, waits for them, and re-layouts  2.27 us (4%)
    ppermute x3, waiting for transfers between devices, fast(): mine[m] = lax.ppermute(mine[m - 2], 'tm', onward)  19.6 us
    ppermute x7, starting transfers between devices, flip(): return lax.ppermute(x, 'tm', [(i, i ^ mask) for i in range(peers)])  10.1 us
    pallas_call x9, Pallas kernels, call(): pl.pallas_call(kernel, out_shape=out, in_specs=[scalar] * smem + [whole]...  8.45 us
    ppermute x9, starting transfers between devices, across(): return lax.ppermute(x, axis, swap)  7.27 us
    ppermute x7, waiting for transfers between devices, flip(): return lax.ppermute(x, 'tm', [(i, i ^ mask) for i in range(peers)])  6.51 us
    ppermute x2, starting transfers between devices, fast(): mine[m + 1] = lax.ppermute(last, 'tm', onward)  4.22 us
    ppermute x3, starting transfers between devices, fast(): mine[m] = lax.ppermute(mine[m - 2], 'tm', onward)  3.98 us
    unnamed x10, local copies, waits for them, and re-layouts  2.23 us
  transfers between devices with their start and end apart: 21, of which 8 were waited for; matrix products, arithmetic and copies ran while one was open for 0% of the time, Pallas kernels for 9%

profile of v2, /device:TPU:0, one launch (start us, length us, event | category | flops | bytes accessed | tf_op | source)
XLA Modules:
  0.0 64.5 jit_solution(12021511308804465477)
XLA Ops:
  0.1 1.1 %copy-done.1 = bf16[1,4,32,2240]{3,2,1,0:T(8,128)(2,1)S(1)} copy-done((bf16[1,4,32,2240]{3,2,1,0:T(8,128)(2,1)S(1)}, bf16[1,4,32,2240]{3,2,1,0:T(8,128)(2,1)}, u32[]{:S(2)}) %copy-start.1) | copy-done | bytes 573464
  1.2 1.1 %copy-done.2 = bf16[1,4,32,2240]{3,2,1,0:T(8,128)(2,1)S(1)} copy-done((bf16[1,4,32,2240]{3,2,1,0:T(8,128)(2,1)S(1)}, bf16[1,4,32,2240]{3,2,1,0:T(8,128)(2,1)}, u32[]{:S(2)}) %copy-start.2) | copy-done | bytes 573464
  2.3 1.0 %shard_map.55 = (f32[40,1152]{1,0:T(8,128)S(1)}, f32[40,1152]{1,0:T(8,128)S(1)}) custom-call(s32[3]{0:T(128)S(1)} %pad_add_fusion.at_ref, bf16[128,2240]{1,0:T(8,128)(2,1)S(1)} %bitcast.10, bf16[128,2240]{1,0:T(8,128)(2,1)S(1)} %bitcast.11), custom_call_target="tpu_custom_call" | custom-call | flops 73400320 | bytes 1515532 | tf_op jit(solution)/shard_map/pallas_call | solution.py:27
  3.3 0.6 collective-permute-start.1
  3.9 1.1 %collective-permute-done.1 = f32[40,1152]{1,0:T(8,128)S(1)} collective-permute-done((f32[40,1152]{1,0:T(8,128)S(1)}, f32[40,1152]{1,0:T(8,128)S(1)}, u32[]{:S(2)}, u32[]{:S(2)}) %collective-permute-start.1) | collective-permute-done | bytes 184352 | tf_op jit(solution)/shard_map/ppermute | solution.py:234
  5.0 2.9 %collective-permute-start.2 = (bf16[40,1152]{1,0:T(8,128)(2,1)S(1)}, bf16[40,1152]{1,0:T(8,128)(2,1)S(1)}, u32[]{:S(2)}, u32[]{:S(2)}) collective-permute-start(bf16[40,1152]{1,0:T(8,128)(2,1)S(1)} %get-tuple-element.25), channel_id=1, source_target_pairs={{0,2},{2,0},{4,6},{6,4},{8,10},{10,8},{12,14},{14,12},{1,3},{3,1},... | collective-permute-start | bytes 276488 | tf_op jit(solution)/shard_map/ppermute | solution.py:231
  7.9 1.0 %shard_map.57 = (bf16[144,1152]{1,0:T(8,128)(2,1)S(1)}, bf16[2,144,1152]{2,1,0:T(8,128)(2,1)S(1)}) custom-call(s32[3]{0:T(128)S(1)} %pad_add_fusion.at_ref, bf16[1,1,313600]{2,1,0:T(2,128)(2,1)S(1)} %copy-done), custom_call_target="tpu_custom_call" | custom-call | bytes 1622540 | tf_op jit(solution)/shard_map/pallas_call | solution.py:27
  8.9 1.6 %collective-permute-start.7 = (bf16[144,1152]{1,0:T(8,128)(2,1)S(1)}, bf16[144,1152]{1,0:T(8,128)(2,1)S(1)}, u32[]{:S(2)}, u32[]{:S(2)}) collective-permute-start(bf16[144,1152]{1,0:T(8,128)(2,1)S(1)} %get-tuple-element.19.refs_0_), channel_id=1, source_target_pairs={{0,4},{2,6},{4,12},{6,14},{12,8},{14,10},{8,0},{10,2},{1,5},{3,7},... | collective-permute-start | bytes 995336 | tf_op jit(solution)/shard_map/ppermute | solution.py:259
  10.5 0.5 collective-permute-start.6
  11.1 2.7 %collective-permute-start.3 = (bf16[40,1152]{1,0:T(8,128)(2,1)S(1)}, bf16[40,1152]{1,0:T(8,128)(2,1)S(1)}, u32[]{:S(2)}, u32[]{:S(2)}) collective-permute-start(bf16[40,1152]{1,0:T(8,128)(2,1)S(1)} %fusion), channel_id=1, source_target_pairs={{0,4},{2,6},{4,0},{6,2},{8,12},{10,14},{12,8},{14,10},{1,5},{3,7},... | collective-permute-start | bytes 276488 | tf_op jit(solution)/shard_map/ppermute | solution.py:231
  13.7 5.8 %collective-permute-done.7.refs_2_ = bf16[144,1152]{1,0:T(8,128)(2,1)S(1)} collective-permute-done((bf16[144,1152]{1,0:T(8,128)(2,1)S(1)}, bf16[144,1152]{1,0:T(8,128)(2,1)S(1)}, u32[]{:S(2)}, u32[]{:S(2)}) %collective-permute-start.7) | collective-permute-done | bytes 331808 | tf_op jit(solution)/shard_map/ppermute | solution.py:259
  19.5 1.6 %collective-permute-start.9 = (bf16[144,1152]{1,0:T(8,128)(2,1)S(1)}, bf16[144,1152]{1,0:T(8,128)(2,1)S(1)}, u32[]{:S(2)}, u32[]{:S(2)}) collective-permute-start(bf16[144,1152]{1,0:T(8,128)(2,1)S(1)} %collective-permute-done.7.refs_2_), channel_id=1, source_target_pairs={{0,4},{2,6},{4,12},{6,14},{12,8},{14,10},{8,0},{10,2},{1,5},{3,7},... | collective-permute-start | bytes 995336 | tf_op jit(solution)/shard_map/ppermute | solution.py:259
  21.1 1.5 %collective-permute-start.12 = (bf16[144,1152]{1,0:T(8,128)(2,1)S(1)}, bf16[144,1152]{1,0:T(8,128)(2,1)S(1)}, u32[]{:S(2)}, u32[]{:S(2)}) collective-permute-start(bf16[144,1152]{1,0:T(8,128)(2,1)S(1)} %collective-permute-done.7.refs_2_), channel_id=1, source_target_pairs={{0,16},{16,0},{1,17},{17,1},{2,18},{18,2},{3,19},{19,3},{4,20},{20... | collective-permute-start | bytes 995336 | tf_op jit(solution)/shard_map/ppermute | solution.py:234
  22.6 1.4 %collective-permute-start.4 = (bf16[40,1152]{1,0:T(8,128)(2,1)S(1)}, bf16[40,1152]{1,0:T(8,128)(2,1)S(1)}, u32[]{:S(2)}, u32[]{:S(2)}) collective-permute-start(bf16[40,1152]{1,0:T(8,128)(2,1)S(1)} %add_convert_fusion), channel_id=1, source_target_pairs={{0,8},{2,10},{4,12},{6,14},{8,0},{10,2},{12,4},{14,6},{1,9},{3,11}... | collective-permute-start | bytes 276488 | tf_op jit(solution)/shard_map/ppermute | solution.py:231
  24.0 8.3 %collective-permute-done.9.refs_4_ = bf16[144,1152]{1,0:T(8,128)(2,1)S(1)} collective-permute-done((bf16[144,1152]{1,0:T(8,128)(2,1)S(1)}, bf16[144,1152]{1,0:T(8,128)(2,1)S(1)}, u32[]{:S(2)}, u32[]{:S(2)}) %collective-permute-start.9) | collective-permute-done | bytes 331808 | tf_op jit(solution)/shard_map/ppermute | solution.py:259
  32.4 0.8 %collective-permute-start.10 = (bf16[144,1152]{1,0:T(8,128)(2,1)S(1)}, bf16[144,1152]{1,0:T(8,128)(2,1)S(1)}, u32[]{:S(2)}, u32[]{:S(2)}) collective-permute-start(bf16[144,1152]{1,0:T(8,128)(2,1)S(1)} %collective-permute-done.9.refs_4_), channel_id=1, source_target_pairs={{0,4},{2,6},{4,12},{6,14},{12,8},{14,10},{8,0},{10,2},{1,5},{3,7},... | collective-permute-start | bytes 995336 | tf_op jit(solution)/shard_map/ppermute | solution.py:259
  33.2 3.4 %collective-permute-start.8 = (bf16[144,1152]{1,0:T(8,128)(2,1)S(1)}, bf16[144,1152]{1,0:T(8,128)(2,1)S(1)}, u32[]{:S(2)}, u32[]{:S(2)}) collective-permute-start(bf16[144,1152]{1,0:T(8,128)(2,1)S(1)} %slice_bitcast_fusion), channel_id=1, source_target_pairs={{0,4},{2,6},{4,12},{6,14},{12,8},{14,10},{8,0},{10,2},{1,5},{3,7},... | collective-permute-start | bytes 995336 | tf_op jit(solution)/shard_map/ppermute | solution.py:263
  36.6 1.5 %collective-permute-start.14 = (bf16[144,1152]{1,0:T(8,128)(2,1)S(1)}, bf16[144,1152]{1,0:T(8,128)(2,1)S(1)}, u32[]{:S(2)}, u32[]{:S(2)}) collective-permute-start(bf16[144,1152]{1,0:T(8,128)(2,1)S(1)} %collective-permute-done.9.refs_4_), channel_id=1, source_target_pairs={{0,16},{16,0},{1,17},{17,1},{2,18},{18,2},{3,19},{19,3},{4,20},{20... | collective-permute-start | bytes 995336 | tf_op jit(solution)/shard_map/ppermute | solution.py:234
  38.2 5.5 %collective-permute-done.10.refs_5_ = bf16[144,1152]{1,0:T(8,128)(2,1)S(1)} collective-permute-done((bf16[144,1152]{1,0:T(8,128)(2,1)S(1)}, bf16[144,1152]{1,0:T(8,128)(2,1)S(1)}, u32[]{:S(2)}, u32[]{:S(2)}) %collective-permute-start.10) | collective-permute-done | bytes 331808 | tf_op jit(solution)/shard_map/ppermute | solution.py:259
  43.6 0.8 %collective-permute-start.11 = (bf16[144,1152]{1,0:T(8,128)(2,1)S(1)}, bf16[144,1152]{1,0:T(8,128)(2,1)S(1)}, u32[]{:S(2)}, u32[]{:S(2)}) collective-permute-start(bf16[144,1152]{1,0:T(8,128)(2,1)S(1)} %collective-permute-done.10.refs_5_), channel_id=1, source_target_pairs={{0,2},{2,0},{4,6},{6,4},{8,10},{10,8},{12,14},{14,12},{1,3},{3,1},... | collective-permute-start | bytes 995336 | tf_op jit(solution)/shard_map/ppermute | solution.py:231
  44.4 1.3 %collective-permute-start.13 = (bf16[144,1152]{1,0:T(8,128)(2,1)S(1)}, bf16[144,1152]{1,0:T(8,128)(2,1)S(1)}, u32[]{:S(2)}, u32[]{:S(2)}) collective-permute-start(bf16[144,1152]{1,0:T(8,128)(2,1)S(1)} %collective-permute-done.12.refs_8_), channel_id=1, source_target_pairs={{0,2},{2,0},{4,6},{6,4},{8,10},{10,8},{12,14},{14,12},{1,3},{3,1},... | collective-permute-start | bytes 995336 | tf_op jit(solution)/shard_map/ppermute | solution.py:231
  45.7 1.5 %collective-permute-start.15 = (bf16[144,1152]{1,0:T(8,128)(2,1)S(1)}, bf16[144,1152]{1,0:T(8,128)(2,1)S(1)}, u32[]{:S(2)}, u32[]{:S(2)}) collective-permute-start(bf16[144,1152]{1,0:T(8,128)(2,1)S(1)} %collective-permute-done.10.refs_5_), channel_id=1, source_target_pairs={{0,16},{16,0},{1,17},{17,1},{2,18},{18,2},{3,19},{19,3},{4,20},{20... | collective-permute-start | bytes 995336 | tf_op jit(solution)/shard_map/ppermute | solution.py:234
  47.5 0.8 %collective-permute-start.16 = (bf16[144,1152]{1,0:T(8,128)(2,1)S(1)}, bf16[144,1152]{1,0:T(8,128)(2,1)S(1)}, u32[]{:S(2)}, u32[]{:S(2)}) collective-permute-start(bf16[144,1152]{1,0:T(8,128)(2,1)S(1)} %collective-permute-done.8.refs_3_), channel_id=1, source_target_pairs={{0,4},{2,6},{4,12},{6,14},{12,8},{14,10},{8,0},{10,2},{1,5},{3,7},... | collective-permute-start | bytes 995336 | tf_op jit(solution)/shard_map/ppermute | solution.py:263
  48.3 0.5 collective-permute-start.18
  48.8 4.9 %collective-permute-done.11.refs_6_ = bf16[144,1152]{1,0:T(8,128)(2,1)S(1)} collective-permute-done((bf16[144,1152]{1,0:T(8,128)(2,1)S(1)}, bf16[144,1152]{1,0:T(8,128)(2,1)S(1)}, u32[]{:S(2)}, u32[]{:S(2)}) %collective-permute-start.11) | collective-permute-done | bytes 331808 | tf_op jit(solution)/shard_map/ppermute | solution.py:231
  53.7 1.5 %collective-permute-start.19 = (bf16[144,1152]{1,0:T(8,128)(2,1)S(1)}, bf16[144,1152]{1,0:T(8,128)(2,1)S(1)}, u32[]{:S(2)}, u32[]{:S(2)}) collective-permute-start(bf16[144,1152]{1,0:T(8,128)(2,1)S(1)} %collective-permute-done.11.refs_6_), channel_id=1, source_target_pairs={{0,16},{16,0},{1,17},{17,1},{2,18},{18,2},{3,19},{19,3},{4,20},{20... | collective-permute-start | bytes 995336 | tf_op jit(solution)/shard_map/ppermute | solution.py:234
  55.2 2.0 %shard_map.56 = (bf16[256,1152]{1,0:T(8,128)(2,1)S(1)}, f32[256,128]{1,0:T(8,128)S(1)}) custom-call(s32[3]{0:T(128)S(1)} %pad_add_fusion.at_ref, bf16[128,2240]{1,0:T(8,128)(2,1)S(1)} %bitcast.12, bf16[128,2240]{1,0:T(8,128)(2,1)S(1)} %bitcast.13, f32[1,2240]{1,0:T(1,128)S(1)} %reshape.20.g_ref, f32[40,1152]{1,0:T(8,128)S(1)} %get-tuple-element.26.total_ref, ...), custom_call_target="tpu_custom_call" | custom-call | flops 150994944 | bytes 2337548 | tf_op jit(solution)/shard_map/pallas_call | solution.py:27
  57.2 1.6 %shard_map.58 = (f32[128,1152]{1,0:T(8,128)S(1)}, f32[128,1152]{1,0:T(8,128)S(1)}, f32[128,1152]{1,0:T(8,128)S(1)}, f32[128,1152]{1,0:T(8,128)S(1)}) custom-call(bf16[256,1152]{1,0:T(8,128)(2,1)S(1)} %get-tuple-element.18.left_ref, bf16[144,1152]{1,0:T(8,128)(2,1)S(1)} %get-tuple-element.19.refs_0_, ...), custom_call_target="tpu_custom_call" | custom-call | flops 1104150528 | bytes 7593984 | tf_op jit(solution)/shard_map/pallas_call | solution.py:27
  59.2 1.6 %collective-permute-done.18.refs_0_ = bf16[144,1152]{1,0:T(8,128)(2,1)S(1)} collective-permute-done((bf16[144,1152]{1,0:T(8,128)(2,1)S(1)}, bf16[144,1152]{1,0:T(8,128)(2,1)S(1)}, u32[]{:S(2)}, u32[]{:S(2)}) %collective-permute-start.18) | collective-permute-done | bytes 331808 | tf_op jit(solution)/shard_map/ppermute | solution.py:231
  61.3 0.5 collective-permute-start.5
  62.4 0.5 collective-permute-done.5.near_ref
  62.9 1.6 %shard_map.63 = bf16[128,2240]{1,0:T(8,128)(2,1)} custom-call(s32[3]{0:T(128)S(1)} %pad_add_fusion.at_ref, f32[256,128]{1,0:T(8,128)S(1)} %get-tuple-element.17.square_ref, f32[128,128]{1,0:T(8,128)S(1)} %collective-permute-done.5.near_ref, f32[128,1152]{1,0:T(8,128)S(1)} %shard_map.59.mine_ref, bf16[128,1152]{1,0:T(8,128)(2,1)S(1)} %collective-permute-done.17.got_mine_ref, ...), custom_call_target="tpu_custom_call" | custom-call | bytes 2539532 | tf_op jit(solution)/shard_map/pallas_call | solution.py:27
  (36 shorter events, 2.0 us)
Async XLA Ops:
  0.0 7.9 %copy-start = (bf16[1,1,313600]{2,1,0:T(2,128)(2,1)S(1)}, bf16[1,1,313600]{2,1,0:T(2,128)(2,1)}, u32[]{:S(2)}) copy-start(bf16[1,1,313600]{2,1,0:T(2,128)(2,1)} %w_ref.1) | copy-start | bytes 1881604
  0.1 1.2 %copy-start.1 = (bf16[1,4,32,2240]{3,2,1,0:T(8,128)(2,1)S(1)}, bf16[1,4,32,2240]{3,2,1,0:T(8,128)(2,1)}, u32[]{:S(2)}) copy-start(bf16[1,4,32,2240]{3,2,1,0:T(8,128)(2,1)} %param.6) | copy-start | bytes 1720324
  1.2 1.1 %copy-start.2 = (bf16[1,4,32,2240]{3,2,1,0:T(8,128)(2,1)S(1)}, bf16[1,4,32,2240]{3,2,1,0:T(8,128)(2,1)}, u32[]{:S(2)}) copy-start(bf16[1,4,32,2240]{3,2,1,0:T(8,128)(2,1)} %param.7) | copy-start | bytes 1720324
  3.3 10.4 %copy-start.3 = (bf16[1,4,32,2240]{3,2,1,0:T(8,128)(2,1)S(1)}, bf16[1,4,32,2240]{3,2,1,0:T(8,128)(2,1)}, u32[]{:S(2)}) copy-start(bf16[1,4,32,2240]{3,2,1,0:T(8,128)(2,1)} %param.5) | copy-start | bytes 1720324
  3.3 1.6 %collective-permute-start.1 = (f32[40,1152]{1,0:T(8,128)S(1)}, f32[40,1152]{1,0:T(8,128)S(1)}, u32[]{:S(2)}, u32[]{:S(2)}) collective-permute-start(f32[40,1152]{1,0:T(8,128)S(1)} %get-tuple-element.16), channel_id=1, source_target_pairs={{0,1},{1,0},{2,3},{3,2},{4,5},{5,4},{6,7},{7,6},{8,9},{9,8},{10,11... | collective-permute-start | bytes 552968 | tf_op jit(solution)/shard_map/ppermute | solution.py:234
  5.0 50.2 %copy-start.4 = (f32[2240]{0:T(1024)S(1)}, f32[2240]{0:T(1024)}, u32[]{:S(2)}) copy-start(f32[2240]{0:T(1024)} %param.8) | copy-start | bytes 26884
  5.0 6.0 %collective-permute-start.2 = (bf16[40,1152]{1,0:T(8,128)(2,1)S(1)}, bf16[40,1152]{1,0:T(8,128)(2,1)S(1)}, u32[]{:S(2)}, u32[]{:S(2)}) collective-permute-start(bf16[40,1152]{1,0:T(8,128)(2,1)S(1)} %get-tuple-element.25), channel_id=1, source_target_pairs={{0,2},{2,0},{4,6},{6,4},{8,10},{10,8},{12,14},{14,12},{1,3},{3,1},... | collective-permute-start | bytes 276488 | tf_op jit(solution)/shard_map/ppermute | solution.py:231
  8.9 10.6 %collective-permute-start.7 = (bf16[144,1152]{1,0:T(8,128)(2,1)S(1)}, bf16[144,1152]{1,0:T(8,128)(2,1)S(1)}, u32[]{:S(2)}, u32[]{:S(2)}) collective-permute-start(bf16[144,1152]{1,0:T(8,128)(2,1)S(1)} %get-tuple-element.19.refs_0_), channel_id=1, source_target_pairs={{0,4},{2,6},{4,12},{6,14},{12,8},{14,10},{8,0},{10,2},{1,5},{3,7},... | collective-permute-start | bytes 995336 | tf_op jit(solution)/shard_map/ppermute | solution.py:259
  10.5 22.7 %collective-permute-start.6 = (bf16[2,144,1152]{2,1,0:T(8,128)(2,1)S(1)}, bf16[2,144,1152]{2,1,0:T(8,128)(2,1)S(1)}, u32[]{:S(2)}, u32[]{:S(2)}) collective-permute-start(bf16[2,144,1152]{2,1,0:T(8,128)(2,1)S(1)} %get-tuple-element.20.refs_7_), channel_id=1, source_target_pairs={{0,2},{2,0},{4,6},{6,4},{8,10},{10,8},{12,14},{14,12},{1,3},{3,1},... | collective-permute-start | bytes 1990664 | tf_op jit(solution)/shard_map/ppermute | solution.py:231
  11.1 11.5 %collective-permute-start.3 = (bf16[40,1152]{1,0:T(8,128)(2,1)S(1)}, bf16[40,1152]{1,0:T(8,128)(2,1)S(1)}, u32[]{:S(2)}, u32[]{:S(2)}) collective-permute-start(bf16[40,1152]{1,0:T(8,128)(2,1)S(1)} %fusion), channel_id=1, source_target_pairs={{0,4},{2,6},{4,0},{6,2},{8,12},{10,14},{12,8},{14,10},{1,5},{3,7},... | collective-permute-start | bytes 276488 | tf_op jit(solution)/shard_map/ppermute | solution.py:231
  13.7 32.0 %collective-permute-start = (bf16[1,4,32,2240]{3,2,1,0:T(8,128)(2,1)S(1)}, bf16[1,4,32,2240]{3,2,1,0:T(8,128)(2,1)S(1)}, u32[]{:S(2)}, u32[]{:S(2)}) collective-permute-start(bf16[1,4,32,2240]{3,2,1,0:T(8,128)(2,1)S(1)} %copy-done.3), channel_id=1, source_target_pairs={{0,1},{1,0},{2,3},{3,2},{4,5},{5,4},{6,7},{7,6},{8,9},{9,8},{10,11... | collective-permute-start | bytes 1720328 | tf_op jit(solution)/shard_map/ppermute | solution.py:234
  19.5 12.9 %collective-permute-start.9 = (bf16[144,1152]{1,0:T(8,128)(2,1)S(1)}, bf16[144,1152]{1,0:T(8,128)(2,1)S(1)}, u32[]{:S(2)}, u32[]{:S(2)}) collective-permute-start(bf16[144,1152]{1,0:T(8,128)(2,1)S(1)} %collective-permute-done.7.refs_2_), channel_id=1, source_target_pairs={{0,4},{2,6},{4,12},{6,14},{12,8},{14,10},{8,0},{10,2},{1,5},{3,7},... | collective-permute-start | bytes 995336 | tf_op jit(solution)/shard_map/ppermute | solution.py:259
  21.1 23.4 %collective-permute-start.12 = (bf16[144,1152]{1,0:T(8,128)(2,1)S(1)}, bf16[144,1152]{1,0:T(8,128)(2,1)S(1)}, u32[]{:S(2)}, u32[]{:S(2)}) collective-permute-start(bf16[144,1152]{1,0:T(8,128)(2,1)S(1)} %collective-permute-done.7.refs_2_), channel_id=1, source_target_pairs={{0,16},{16,0},{1,17},{17,1},{2,18},{18,2},{3,19},{19,3},{4,20},{20... | collective-permute-start | bytes 995336 | tf_op jit(solution)/shard_map/ppermute | solution.py:234
  22.6 14.0 %collective-permute-start.4 = (bf16[40,1152]{1,0:T(8,128)(2,1)S(1)}, bf16[40,1152]{1,0:T(8,128)(2,1)S(1)}, u32[]{:S(2)}, u32[]{:S(2)}) collective-permute-start(bf16[40,1152]{1,0:T(8,128)(2,1)S(1)} %add_convert_fusion), channel_id=1, source_target_pairs={{0,8},{2,10},{4,12},{6,14},{8,0},{10,2},{12,4},{14,6},{1,9},{3,11}... | collective-permute-start | bytes 276488 | tf_op jit(solution)/shard_map/ppermute | solution.py:231
  32.4 11.3 %collective-permute-start.10 = (bf16[144,1152]{1,0:T(8,128)(2,1)S(1)}, bf16[144,1152]{1,0:T(8,128)(2,1)S(1)}, u32[]{:S(2)}, u32[]{:S(2)}) collective-permute-start(bf16[144,1152]{1,0:T(8,128)(2,1)S(1)} %collective-permute-done.9.refs_4_), channel_id=1, source_target_pairs={{0,4},{2,6},{4,12},{6,14},{12,8},{14,10},{8,0},{10,2},{1,5},{3,7},... | collective-permute-start | bytes 995336 | tf_op jit(solution)/shard_map/ppermute | solution.py:259
  33.2 14.3 %collective-permute-start.8 = (bf16[144,1152]{1,0:T(8,128)(2,1)S(1)}, bf16[144,1152]{1,0:T(8,128)(2,1)S(1)}, u32[]{:S(2)}, u32[]{:S(2)}) collective-permute-start(bf16[144,1152]{1,0:T(8,128)(2,1)S(1)} %slice_bitcast_fusion), channel_id=1, source_target_pairs={{0,4},{2,6},{4,12},{6,14},{12,8},{14,10},{8,0},{10,2},{1,5},{3,7},... | collective-permute-start | bytes 995336 | tf_op jit(solution)/shard_map/ppermute | solution.py:263
  36.6 11.6 %collective-permute-start.14 = (bf16[144,1152]{1,0:T(8,128)(2,1)S(1)}, bf16[144,1152]{1,0:T(8,128)(2,1)S(1)}, u32[]{:S(2)}, u32[]{:S(2)}) collective-permute-start(bf16[144,1152]{1,0:T(8,128)(2,1)S(1)} %collective-permute-done.9.refs_4_), channel_id=1, source_target_pairs={{0,16},{16,0},{1,17},{17,1},{2,18},{18,2},{3,19},{19,3},{4,20},{20... | collective-permute-start | bytes 995336 | tf_op jit(solution)/shard_map/ppermute | solution.py:234
  43.6 10.0 %collective-permute-start.11 = (bf16[144,1152]{1,0:T(8,128)(2,1)S(1)}, bf16[144,1152]{1,0:T(8,128)(2,1)S(1)}, u32[]{:S(2)}, u32[]{:S(2)}) collective-permute-start(bf16[144,1152]{1,0:T(8,128)(2,1)S(1)} %collective-permute-done.10.refs_5_), channel_id=1, source_target_pairs={{0,2},{2,0},{4,6},{6,4},{8,10},{10,8},{12,14},{14,12},{1,3},{3,1},... | collective-permute-start | bytes 995336 | tf_op jit(solution)/shard_map/ppermute | solution.py:231
  44.4 12.8 %collective-permute-start.13 = (bf16[144,1152]{1,0:T(8,128)(2,1)S(1)}, bf16[144,1152]{1,0:T(8,128)(2,1)S(1)}, u32[]{:S(2)}, u32[]{:S(2)}) collective-permute-start(bf16[144,1152]{1,0:T(8,128)(2,1)S(1)} %collective-permute-done.12.refs_8_), channel_id=1, source_target_pairs={{0,2},{2,0},{4,6},{6,4},{8,10},{10,8},{12,14},{14,12},{1,3},{3,1},... | collective-permute-start | bytes 995336 | tf_op jit(solution)/shard_map/ppermute | solution.py:231
  45.7 11.5 %collective-permute-start.15 = (bf16[144,1152]{1,0:T(8,128)(2,1)S(1)}, bf16[144,1152]{1,0:T(8,128)(2,1)S(1)}, u32[]{:S(2)}, u32[]{:S(2)}) collective-permute-start(bf16[144,1152]{1,0:T(8,128)(2,1)S(1)} %collective-permute-done.10.refs_5_), channel_id=1, source_target_pairs={{0,16},{16,0},{1,17},{17,1},{2,18},{18,2},{3,19},{19,3},{4,20},{20... | collective-permute-start | bytes 995336 | tf_op jit(solution)/shard_map/ppermute | solution.py:234
  47.5 11.3 %collective-permute-start.16 = (bf16[144,1152]{1,0:T(8,128)(2,1)S(1)}, bf16[144,1152]{1,0:T(8,128)(2,1)S(1)}, u32[]{:S(2)}, u32[]{:S(2)}) collective-permute-start(bf16[144,1152]{1,0:T(8,128)(2,1)S(1)} %collective-permute-done.8.refs_3_), channel_id=1, source_target_pairs={{0,4},{2,6},{4,12},{6,14},{12,8},{14,10},{8,0},{10,2},{1,5},{3,7},... | collective-permute-start | bytes 995336 | tf_op jit(solution)/shard_map/ppermute | solution.py:263
  48.3 12.5 %collective-permute-start.18 = (bf16[144,1152]{1,0:T(8,128)(2,1)S(1)}, bf16[144,1152]{1,0:T(8,128)(2,1)S(1)}, u32[]{:S(2)}, u32[]{:S(2)}) collective-permute-start(bf16[144,1152]{1,0:T(8,128)(2,1)S(1)} %collective-permute-done.14.refs_10_), channel_id=1, source_target_pairs={{0,2},{2,0},{4,6},{6,4},{8,10},{10,8},{12,14},{14,12},{1,3},{3,1},... | collective-permute-start | bytes 995336 | tf_op jit(solution)/shard_map/ppermute | solution.py:231
  53.7 7.1 %collective-permute-start.19 = (bf16[144,1152]{1,0:T(8,128)(2,1)S(1)}, bf16[144,1152]{1,0:T(8,128)(2,1)S(1)}, u32[]{:S(2)}, u32[]{:S(2)}) collective-permute-start(bf16[144,1152]{1,0:T(8,128)(2,1)S(1)} %collective-permute-done.11.refs_6_), channel_id=1, source_target_pairs={{0,16},{16,0},{1,17},{17,1},{2,18},{18,2},{3,19},{19,3},{4,20},{20... | collective-permute-start | bytes 995336 | tf_op jit(solution)/shard_map/ppermute | solution.py:234
  59.1 3.8 %collective-permute-start.17 = (bf16[128,1152]{1,0:T(8,128)(2,1)S(1)}, bf16[128,1152]{1,0:T(8,128)(2,1)S(1)}, u32[]{:S(2)}, u32[]{:S(2)}) collective-permute-start(bf16[128,1152]{1,0:T(8,128)(2,1)S(1)} %shard_map.60), channel_id=1, source_target_pairs={{0,1},{1,0},{2,3},{3,2},{4,5},{5,4},{6,7},{7,6},{8,9},{9,8},{10,11... | collective-permute-start | bytes 884744 | tf_op jit(solution)/shard_map/ppermute | solution.py:234
  61.2 1.7 %collective-permute-start.20 = (bf16[128,1152]{1,0:T(8,128)(2,1)S(1)}, bf16[128,1152]{1,0:T(8,128)(2,1)S(1)}, u32[]{:S(2)}, u32[]{:S(2)}) collective-permute-start(bf16[128,1152]{1,0:T(8,128)(2,1)S(1)} %shard_map.62), channel_id=1, source_target_pairs={{0,1},{1,0},{2,3},{3,2},{4,5},{5,4},{6,7},{7,6},{8,9},{9,8},{10,11... | collective-permute-start | bytes 884744 | tf_op jit(solution)/shard_map/ppermute | solution.py:234
  61.3 1.6 %collective-permute-start.5 = (f32[128,128]{1,0:T(8,128)S(1)}, f32[128,128]{1,0:T(8,128)S(1)}, u32[]{:S(2)}, u32[]{:S(2)}) collective-permute-start(f32[128,128]{1,0:T(8,128)S(1)} %slice.6), channel_id=1, source_target_pairs={{0,1},{1,0},{2,3},{3,2},{4,5},{5,4},{6,7},{7,6},{8,9},{9,8},{10,11... | collective-permute-start | bytes 196616 | tf_op jit(solution)/shard_map/ppermute | solution.py:234

commit v3 on v2

--- a/solution.py
+++ b/solution.py
@@ -20,15 +20,16 @@
     return -(-n // m) * m
 
 
-def call(kernel, out, args, scratch=(), flops=0, smem=0, mib=16):
+def call(kernel, out, args, scratch=(), flops=0, smem=0, mib=16, far_out=False):
     whole = pl.BlockSpec(memory_space=pltpu.VMEM)
     scalar = pl.BlockSpec(memory_space=pltpu.SMEM)
+    far = pl.BlockSpec(memory_space=pl.ANY)
     moved = sum(a.size * a.dtype.itemsize for a in jax.tree.leaves((args, out)))
     return pl.pallas_call(
         kernel,
         out_shape=out,
         in_specs=[scalar] * smem + [whole] * (len(args) - smem),
-        out_specs=jax.tree.map(lambda _: whole, out),
+        out_specs=jax.tree.map(lambda _: far if far_out else whole, out),
         scratch_shapes=list(scratch),
         compiler_params=pltpu.CompilerParams(vmem_limit_bytes=mib * 1024 * 1024),
         cost_estimate=pl.CostEstimate(flops=flops, bytes_accessed=moved, transcendentals=0),
@@ -51,7 +52,7 @@
     return jax.ShapeDtypeStruct(tuple(dims), dtype)
 
 
-def unpack_weight(rows, depth, at_ref, w_ref, mine_ref, both_ref, tall):
+def unpack_weight(rows, depth, at_ref, w_ref, mine_ref, rest_ref, tall):
     half = mine_ref.shape[1]
     tall[pl.ds(rows // 8 * 8, tall.shape[0] - rows // 8 * 8), :] = jnp.zeros(
         (tall.shape[0] - rows // 8 * 8, tall.shape[1]), jnp.float32
@@ -63,10 +64,8 @@
     for r in range(rows):
         tall[r : r + 1, 0:depth] = w_ref[0, :, depth * r : depth * (r + 1)].astype(jnp.float32)
     y = at_ref[0]
-    first = tall[:, pl.ds(pl.multiple_of(y * half, LANES), half)].astype(jnp.bfloat16)
-    mine_ref[...] = first
-    both_ref[0] = first
-    both_ref[1] = tall[:, pl.ds(pl.multiple_of((1 - y) * half, LANES), half)].astype(jnp.bfloat16)
+    for ref, side in ((mine_ref, y), (rest_ref, 1 - y)):
+        ref[...] = tall[:, pl.ds(pl.multiple_of(side * half, LANES), half)].astype(jnp.bfloat16)
 
 
 def head_mask():
@@ -198,22 +197,44 @@
     out_ref[...] = total.astype(out_ref.dtype)
 
 
-def finish(depth, at_ref, square_ref, near_ref, mine_ref, got_mine_ref, rest_ref, got_rest_ref, out_ref):
+def scaled(depth, square_ref, near_ref, own_ref, got_ref, out_ref):
+    square = square_ref[0 : own_ref.shape[0], 0:1] + near_ref[:, 0:1]
+    total = own_ref[...] + got_ref[...].astype(jnp.float32)
+    out_ref[...] = (total * lax.rsqrt(square / depth + norm_epsilon)).astype(jnp.bfloat16)
+
+
+def finish(
+    depth, at_ref, square_ref, near_ref, mine_ref, got_mine_ref, rest_ref, out_ref, wide, sems
+):
     count, half = mine_ref.shape
-    square = square_ref[0:count, 0:1] + near_ref[:, 0:1]
-    scale = lax.rsqrt(square / depth + norm_epsilon)
-    mine = ((mine_ref[...] + got_mine_ref[...].astype(jnp.float32)) * scale).astype(jnp.bfloat16)
-    rest = ((rest_ref[...] + got_rest_ref[...].astype(jnp.float32)) * scale).astype(jnp.bfloat16)
+    each = count // sems.shape[0]
+
+    def store(i):
+        rows = pl.ds(i * each, each)
+        return pltpu.make_async_copy(wide.at[rows], out_ref.at[rows], sems.at[i])
+
+    def fill(mine_first):
+        for i in range(sems.shape[0]):
+            rows = slice(i * each, (i + 1) * each)
+            square = square_ref[rows, 0:1] + near_ref[rows, 0:1]
+            total = mine_ref[rows, :] + got_mine_ref[rows, :].astype(jnp.float32)
+            mine = (total * lax.rsqrt(square / depth + norm_epsilon)).astype(jnp.bfloat16)
+            rest = rest_ref[rows, :]
+            left, right = (mine, rest) if mine_first else (rest, mine)
+            wide[rows, 0:half] = left
+            wide[rows, half:depth] = right[:, : depth - half]
+            store(i).start()
 
     @pl.when(at_ref[0] == 0)
     def _():
-        out_ref[:, 0:half] = mine
-        out_ref[:, half:depth] = rest[:, : depth - half]
+        fill(True)
 
     @pl.when(at_ref[0] != 0)
     def _():
-        out_ref[:, 0:half] = rest
-        out_ref[:, half:depth] = mine[:, : depth - half]
+        fill(False)
+
+    for i in range(sems.shape[0]):
+        store(i).wait()
 
 
 def fast(query_tokens, key_tokens, value_tokens, norm_gain, out_weight):
@@ -239,9 +260,9 @@
     bf16, f32 = jnp.bfloat16, jnp.float32
 
     mine, rest = {}, {}
-    mine[0], both = call(
+    mine[0], rest[0] = call(
         functools.partial(unpack_weight, shard, depth),
-        (shape((tall, cols), bf16), shape((2, tall, cols), bf16)),
+        (shape((tall, cols), bf16), shape((tall, cols), bf16)),
         (at, out_weight),
         scratch=[pltpu.VMEM((tall, 2 * cols), f32)],
         smem=1,
@@ -251,20 +272,19 @@
     onward = [
         (2 * a + x, 2 * b + x) for a, b in zip(order, order[1:] + order[:1]) for x in range(2)
     ]
-    beside = flip(both, 1)
-    rest[0] = (both, 1)
-    mine[1], rest[1] = (beside, 0), (beside, 1)
+    mine[1], rest[1] = flip(mine[0], 1), flip(rest[0], 1)
     for k in range(1, length):
         m = 2 * k
         mine[m] = lax.ppermute(mine[m - 2], "tm", onward)
         rest[m] = across(mine[m], "parts")
         if k < length - 1:
-            last = beside[0] if k == 1 else mine[m - 1]
-            mine[m + 1] = lax.ppermute(last, "tm", onward)
-            rest[m + 1] = flip(rest[m], 1)
+            mine[m + 1] = lax.ppermute(mine[m - 1], "tm", onward)
         else:
             mine[m + 1] = flip(mine[m], 1)
+        if k == length - 1:
             rest[m + 1] = across(mine[m + 1], "parts")
+        else:
+            rest[m + 1] = flip(rest[m], 1)
 
     queries = query_tokens.reshape(count, depth)
     partner = across(query_tokens, "band").reshape(count, depth)
@@ -333,11 +353,18 @@
 
     from_rest = finished(1, rest)
     from_mine = finished(0, mine)
+    rest_out = call(
+        functools.partial(scaled, depth),
+        shape((count, cols), bf16),
+        (square, near_square, *from_rest),
+    )
     out = call(
         functools.partial(finish, depth),
         shape((count, depth), bf16),
-        (at, square, near_square, *from_mine, *from_rest),
+        (at, square, near_square, *from_mine, rest_out),
+        scratch=[pltpu.VMEM((count, depth), bf16), pltpu.SemaphoreType.DMA((4,))],
         smem=1,
+        far_out=True,
     )
     return out.reshape(frames, rows, width, depth)
 
@@ -414,6 +441,7 @@
         and lax.axis_size("band") == 2
         and lax.axis_size("parts") == 2
         and peers > 2
+        and query_tokens.shape[1] * query_tokens.shape[2] % 64 == 0
         and peers & (peers - 1) == 0
         and out_weight.shape[-1] % depth == 0
         and depth % (2 * HD) == 0

time: 64.7 us -> 70.5 us (1.090)
  waiting for transfers between devices: 27.9 us -> 36.9 us
  starting transfers between devices: 25.6 us -> 21.2 us
  local copies, waits for them, and re-layouts: 2.27 us -> 3.45 us
    ppermute x7 -> x8, waiting for transfers between devices: 6.51 us -> 23.1 us  [flip(): return lax.ppermute(x, 'tm', [(i, i ^ mask) for i in range(peers)])]
    ppermute x3, waiting for transfers between devices: 19.6 us -> 13.2 us  [fast(): mine[m] = lax.ppermute(mine[m - 2], 'tm', onward)]
    ppermute x2, starting transfers between devices: 4.22 us -> 0.01 us  [fast(): mine[m + 1] = lax.ppermute(mine[m - 1], 'tm', onward)]
    ppermute x7 -> x8, starting transfers between devices: 10.1 us -> 12.5 us  [flip(): return lax.ppermute(x, 'tm', [(i, i ^ mask) for i in range(peers)])]
    ppermute x9, starting transfers between devices: 7.27 us -> 5.32 us  [across(): return lax.ppermute(x, axis, swap)]
    unnamed x10, local copies, waits for them, and re-layouts: 2.23 us -> 3.43 us
    ppermute x9, waiting for transfers between devices: 1.57 us -> 0.55 us  [across(): return lax.ppermute(x, axis, swap)]
    pallas_call x9 -> x10, Pallas kernels: 8.45 us -> 8.45 us  [call(): pl.pallas_call(kernel, out_shape=out, in_specs=[scalar] * smem + [whole]...]
  transfers between devices with their start and end apart: 21 -> 22, of which waited for: 8 -> 9; matrix products, arithmetic and copies ran while one was open for 0% -> 0% of each run, Pallas kernels for 9% -> 8%
where the time goes in v3:
time: 70.5 us; the launch traced here: 70.3 us
  waiting for transfers between devices  36.9 us (52%)
  starting transfers between devices  21.2 us (30%)
  Pallas kernels  8.45 us (12%)
  local copies, waits for them, and re-layouts  3.45 us (5%)
    ppermute x8, waiting for transfers between devices, flip(): return lax.ppermute(x, 'tm', [(i, i ^ mask) for i in range(peers)])  23.1 us
    ppermute x3, waiting for transfers between devices, fast(): mine[m] = lax.ppermute(mine[m - 2], 'tm', onward)  13.2 us
    ppermute x8, starting transfers between devices, flip(): return lax.ppermute(x, 'tm', [(i, i ^ mask) for i in range(peers)])  12.5 us
    pallas_call x10, Pallas kernels, call(): pl.pallas_call(kernel, out_shape=out, in_specs=[scalar] * smem + [whole]...  8.45 us
    ppermute x9, starting transfers between devices, across(): return lax.ppermute(x, axis, swap)  5.32 us
    ppermute x3, starting transfers between devices, fast(): mine[m] = lax.ppermute(mine[m - 2], 'tm', onward)  3.46 us
    unnamed x10, local copies, waits for them, and re-layouts  3.43 us
  transfers between devices with their start and end apart: 22, of which 9 were waited for; matrix products, arithmetic and copies ran while one was open for 0% of the time, Pallas kernels for 8%

profile of v3, /device:TPU:0, one launch (start us, length us, event | category | flops | bytes accessed | tf_op | source)
XLA Modules:
  0.0 70.3 jit_solution(1945987738989566999)
XLA Ops:
  0.1 1.1 %copy-done.1 = bf16[1,4,32,2240]{3,2,1,0:T(8,128)(2,1)S(1)} copy-done((bf16[1,4,32,2240]{3,2,1,0:T(8,128)(2,1)S(1)}, bf16[1,4,32,2240]{3,2,1,0:T(8,128)(2,1)}, u32[]{:S(2)}) %copy-start.1) | copy-done | bytes 573464
  1.1 1.1 %copy-done.2 = bf16[1,4,32,2240]{3,2,1,0:T(8,128)(2,1)S(1)} copy-done((bf16[1,4,32,2240]{3,2,1,0:T(8,128)(2,1)S(1)}, bf16[1,4,32,2240]{3,2,1,0:T(8,128)(2,1)}, u32[]{:S(2)}) %copy-start.2) | copy-done | bytes 573464
  2.2 1.0 %shard_map.55 = (f32[40,1152]{1,0:T(8,128)S(1)}, f32[40,1152]{1,0:T(8,128)S(1)}) custom-call(s32[3]{0:T(128)S(1)} %pad_add_fusion.at_ref, bf16[128,2240]{1,0:T(8,128)(2,1)S(1)} %bitcast.8, bf16[128,2240]{1,0:T(8,128)(2,1)S(1)} %bitcast.9), custom_call_target="tpu_custom_call" | custom-call | flops 73400320 | bytes 1515532 | tf_op jit(solution)/shard_map/pallas_call | solution.py:28
  3.2 0.6 collective-permute-start.1
  3.8 1.3 %copy-done = bf16[1,1,313600]{2,1,0:T(2,128)(2,1)S(1)} copy-done((bf16[1,1,313600]{2,1,0:T(2,128)(2,1)S(1)}, bf16[1,1,313600]{2,1,0:T(2,128)(2,1)}, u32[]{:S(2)}) %copy-start) | copy-done | bytes 627224
  5.1 1.0 %shard_map.57 = (bf16[144,1152]{1,0:T(8,128)(2,1)S(1)}, bf16[144,1152]{1,0:T(8,128)(2,1)S(1)}) custom-call(s32[3]{0:T(128)S(1)} %pad_add_fusion.at_ref, bf16[1,1,313600]{2,1,0:T(2,128)(2,1)S(1)} %copy-done), custom_call_target="tpu_custom_call" | custom-call | bytes 1290764 | tf_op jit(solution)/shard_map/pallas_call | solution.py:28
  6.1 2.6 %collective-permute-start.7 = (bf16[144,1152]{1,0:T(8,128)(2,1)S(1)}, bf16[144,1152]{1,0:T(8,128)(2,1)S(1)}, u32[]{:S(2)}, u32[]{:S(2)}) collective-permute-start(bf16[144,1152]{1,0:T(8,128)(2,1)S(1)} %get-tuple-element.19.refs_0_), channel_id=1, source_target_pairs={{0,4},{2,6},{4,12},{6,14},{12,8},{14,10},{8,0},{10,2},{1,5},{3,7},... | collective-permute-start | bytes 995336 | tf_op jit(solution)/shard_map/ppermute | solution.py:278
  8.7 1.6 %collective-permute-start.2 = (bf16[40,1152]{1,0:T(8,128)(2,1)S(1)}, bf16[40,1152]{1,0:T(8,128)(2,1)S(1)}, u32[]{:S(2)}, u32[]{:S(2)}) collective-permute-start(bf16[40,1152]{1,0:T(8,128)(2,1)S(1)} %get-tuple-element.25), channel_id=1, source_target_pairs={{0,2},{2,0},{4,6},{6,4},{8,10},{10,8},{12,14},{14,12},{1,3},{3,1},... | collective-permute-start | bytes 276488 | tf_op jit(solution)/shard_map/ppermute | solution.py:252
  10.3 7.9 %collective-permute-done.7.refs_2_ = bf16[144,1152]{1,0:T(8,128)(2,1)S(1)} collective-permute-done((bf16[144,1152]{1,0:T(8,128)(2,1)S(1)}, bf16[144,1152]{1,0:T(8,128)(2,1)S(1)}, u32[]{:S(2)}, u32[]{:S(2)}) %collective-permute-start.7) | collective-permute-done | bytes 331808 | tf_op jit(solution)/shard_map/ppermute | solution.py:278
  18.2 0.8 %collective-permute-start.9 = (bf16[144,1152]{1,0:T(8,128)(2,1)S(1)}, bf16[144,1152]{1,0:T(8,128)(2,1)S(1)}, u32[]{:S(2)}, u32[]{:S(2)}) collective-permute-start(bf16[144,1152]{1,0:T(8,128)(2,1)S(1)} %collective-permute-done.7.refs_2_), channel_id=1, source_target_pairs={{0,4},{2,6},{4,12},{6,14},{12,8},{14,10},{8,0},{10,2},{1,5},{3,7},... | collective-permute-start | bytes 995336 | tf_op jit(solution)/shard_map/ppermute | solution.py:278
  19.0 3.4 %collective-permute-start.3 = (bf16[40,1152]{1,0:T(8,128)(2,1)S(1)}, bf16[40,1152]{1,0:T(8,128)(2,1)S(1)}, u32[]{:S(2)}, u32[]{:S(2)}) collective-permute-start(bf16[40,1152]{1,0:T(8,128)(2,1)S(1)} %fusion), channel_id=1, source_target_pairs={{0,4},{2,6},{4,0},{6,2},{8,12},{10,14},{12,8},{14,10},{1,5},{3,7},... | collective-permute-start | bytes 276488 | tf_op jit(solution)/shard_map/ppermute | solution.py:252
  22.5 1.5 %collective-permute-start.6 = (bf16[144,1152]{1,0:T(8,128)(2,1)S(1)}, bf16[144,1152]{1,0:T(8,128)(2,1)S(1)}, u32[]{:S(2)}, u32[]{:S(2)}) collective-permute-start(bf16[144,1152]{1,0:T(8,128)(2,1)S(1)} %get-tuple-element.19.refs_0_), channel_id=1, source_target_pairs={{0,2},{2,0},{4,6},{6,4},{8,10},{10,8},{12,14},{14,12},{1,3},{3,1},... | collective-permute-start | bytes 995336 | tf_op jit(solution)/shard_map/ppermute | solution.py:252
  24.0 0.5 collective-permute-start.12
  24.5 6.2 %collective-permute-done.3.refs_1_ = bf16[40,1152]{1,0:T(8,128)(2,1)S(1)} collective-permute-done((bf16[40,1152]{1,0:T(8,128)(2,1)S(1)}, bf16[40,1152]{1,0:T(8,128)(2,1)S(1)}, u32[]{:S(2)}, u32[]{:S(2)}) %collective-permute-start.3) | collective-permute-done | bytes 92192 | tf_op jit(solution)/shard_map/ppermute | solution.py:252
  30.7 1.3 %collective-permute-start.13 = (bf16[144,1152]{1,0:T(8,128)(2,1)S(1)}, bf16[144,1152]{1,0:T(8,128)(2,1)S(1)}, u32[]{:S(2)}, u32[]{:S(2)}) collective-permute-start(bf16[144,1152]{1,0:T(8,128)(2,1)S(1)} %collective-permute-done.7.refs_2_), channel_id=1, source_target_pairs={{0,16},{16,0},{1,17},{17,1},{2,18},{18,2},{3,19},{19,3},{4,20},{20... | collective-permute-start | bytes 995336 | tf_op jit(solution)/shard_map/ppermute | solution.py:255
  32.0 1.1 %collective-permute-done.6.refs_1_ = bf16[144,1152]{1,0:T(8,128)(2,1)S(1)} collective-permute-done((bf16[144,1152]{1,0:T(8,128)(2,1)S(1)}, bf16[144,1152]{1,0:T(8,128)(2,1)S(1)}, u32[]{:S(2)}, u32[]{:S(2)}) %collective-permute-start.6) | collective-permute-done | bytes 331808 | tf_op jit(solution)/shard_map/ppermute | solution.py:252
  33.1 1.8 %collective-permute-start.4 = (bf16[40,1152]{1,0:T(8,128)(2,1)S(1)}, bf16[40,1152]{1,0:T(8,128)(2,1)S(1)}, u32[]{:S(2)}, u32[]{:S(2)}) collective-permute-start(bf16[40,1152]{1,0:T(8,128)(2,1)S(1)} %add_convert_fusion), channel_id=1, source_target_pairs={{0,8},{2,10},{4,12},{6,14},{8,0},{10,2},{12,4},{14,6},{1,9},{3,11}... | collective-permute-start | bytes 276488 | tf_op jit(solution)/shard_map/ppermute | solution.py:252
  35.0 3.4 %collective-permute-done.12.refs_8_ = bf16[144,1152]{1,0:T(8,128)(2,1)S(1)} collective-permute-done((bf16[144,1152]{1,0:T(8,128)(2,1)S(1)}, bf16[144,1152]{1,0:T(8,128)(2,1)S(1)}, u32[]{:S(2)}, u32[]{:S(2)}) %collective-permute-start.12) | collective-permute-done | bytes 331808 | tf_op jit(solution)/shard_map/ppermute | solution.py:252
  38.4 1.5 %collective-permute-start.15 = (bf16[144,1152]{1,0:T(8,128)(2,1)S(1)}, bf16[144,1152]{1,0:T(8,128)(2,1)S(1)}, u32[]{:S(2)}, u32[]{:S(2)}) collective-permute-start(bf16[144,1152]{1,0:T(8,128)(2,1)S(1)} %collective-permute-done.9.refs_4_), channel_id=1, source_target_pairs={{0,16},{16,0},{1,17},{17,1},{2,18},{18,2},{3,19},{19,3},{4,20},{20... | collective-permute-start | bytes 995336 | tf_op jit(solution)/shard_map/ppermute | solution.py:255
  39.9 5.4 %collective-permute-done.10.refs_5_ = bf16[144,1152]{1,0:T(8,128)(2,1)S(1)} collective-permute-done((bf16[144,1152]{1,0:T(8,128)(2,1)S(1)}, bf16[144,1152]{1,0:T(8,128)(2,1)S(1)}, u32[]{:S(2)}, u32[]{:S(2)}) %collective-permute-start.10) | collective-permute-done | bytes 331808 | tf_op jit(solution)/shard_map/ppermute | solution.py:278
  45.2 1.5 %collective-permute-start.11 = (bf16[144,1152]{1,0:T(8,128)(2,1)S(1)}, bf16[144,1152]{1,0:T(8,128)(2,1)S(1)}, u32[]{:S(2)}, u32[]{:S(2)}) collective-permute-start(bf16[144,1152]{1,0:T(8,128)(2,1)S(1)} %collective-permute-done.10.refs_5_), channel_id=1, source_target_pairs={{0,2},{2,0},{4,6},{6,4},{8,10},{10,8},{12,14},{14,12},{1,3},{3,1},... | collective-permute-start | bytes 995336 | tf_op jit(solution)/shard_map/ppermute | solution.py:252
  46.8 1.0 %collective-permute-start.14 = (bf16[144,1152]{1,0:T(8,128)(2,1)S(1)}, bf16[144,1152]{1,0:T(8,128)(2,1)S(1)}, u32[]{:S(2)}, u32[]{:S(2)}) collective-permute-start(bf16[144,1152]{1,0:T(8,128)(2,1)S(1)} %collective-permute-done.13.refs_9_), channel_id=1, source_target_pairs={{0,2},{2,0},{4,6},{6,4},{8,10},{10,8},{12,14},{14,12},{1,3},{3,1},... | collective-permute-start | bytes 995336 | tf_op jit(solution)/shard_map/ppermute | solution.py:252
  48.2 1.1 %collective-permute-start.19 = (bf16[144,1152]{1,0:T(8,128)(2,1)S(1)}, bf16[144,1152]{1,0:T(8,128)(2,1)S(1)}, u32[]{:S(2)}, u32[]{:S(2)}) collective-permute-start(bf16[144,1152]{1,0:T(8,128)(2,1)S(1)} %collective-permute-done.15.refs_11_), channel_id=1, source_target_pairs={{0,2},{2,0},{4,6},{6,4},{8,10},{10,8},{12,14},{14,12},{1,3},{3,1},... | collective-permute-start | bytes 995336 | tf_op jit(solution)/shard_map/ppermute | solution.py:252
  49.4 6.6 %collective-permute-done.11.refs_6_ = bf16[144,1152]{1,0:T(8,128)(2,1)S(1)} collective-permute-done((bf16[144,1152]{1,0:T(8,128)(2,1)S(1)}, bf16[144,1152]{1,0:T(8,128)(2,1)S(1)}, u32[]{:S(2)}, u32[]{:S(2)}) %collective-permute-start.11) | collective-permute-done | bytes 331808 | tf_op jit(solution)/shard_map/ppermute | solution.py:252
  55.9 0.7 %collective-permute-start.20 = (bf16[144,1152]{1,0:T(8,128)(2,1)S(1)}, bf16[144,1152]{1,0:T(8,128)(2,1)S(1)}, u32[]{:S(2)}, u32[]{:S(2)}) collective-permute-start(bf16[144,1152]{1,0:T(8,128)(2,1)S(1)} %collective-permute-done.11.refs_6_), channel_id=1, source_target_pairs={{0,16},{16,0},{1,17},{17,1},{2,18},{18,2},{3,19},{19,3},{4,20},{20... | collective-permute-start | bytes 995336 | tf_op jit(solution)/shard_map/ppermute | solution.py:255
  56.7 2.0 %shard_map.56 = (bf16[256,1152]{1,0:T(8,128)(2,1)S(1)}, f32[256,128]{1,0:T(8,128)S(1)}) custom-call(s32[3]{0:T(128)S(1)} %pad_add_fusion.at_ref, bf16[128,2240]{1,0:T(8,128)(2,1)S(1)} %bitcast.10, bf16[128,2240]{1,0:T(8,128)(2,1)S(1)} %bitcast.11, f32[1,2240]{1,0:T(1,128)S(1)} %reshape.20.g_ref, f32[40,1152]{1,0:T(8,128)S(1)} %get-tuple-element.26.total_ref, ...), custom_call_target="tpu_custom_call" | custom-call | flops 150994944 | bytes 2337548 | tf_op jit(solution)/shard_map/pallas_call | solution.py:28
  58.7 3.8 %collective-permute-done.14.refs_10_ = bf16[144,1152]{1,0:T(8,128)(2,1)S(1)} collective-permute-done((bf16[144,1152]{1,0:T(8,128)(2,1)S(1)}, bf16[144,1152]{1,0:T(8,128)(2,1)S(1)}, u32[]{:S(2)}, u32[]{:S(2)}) %collective-permute-start.14) | collective-permute-done | bytes 331808 | tf_op jit(solution)/shard_map/ppermute | solution.py:252
  62.5 1.5 %shard_map.58 = (f32[128,1152]{1,0:T(8,128)S(1)}, f32[128,1152]{1,0:T(8,128)S(1)}, f32[128,1152]{1,0:T(8,128)S(1)}, f32[128,1152]{1,0:T(8,128)S(1)}) custom-call(bf16[256,1152]{1,0:T(8,128)(2,1)S(1)} %get-tuple-element.18.left_ref, bf16[144,1152]{1,0:T(8,128)(2,1)S(1)} %get-tuple-element.19.refs_0_, bf16[144,1152]{1,0:T(8,128)(2,1)S(1)} %collective-permute-done.6.refs_1_, ...), custom_call_target="tpu_custom_call" | custom-call | flops 1104150528 | bytes 7262208 | tf_op jit(solution)/shard_map/pallas_call | solution.py:28
  64.1 2.0 %collective-permute-done.19.refs_0_ = bf16[144,1152]{1,0:T(8,128)(2,1)S(1)} collective-permute-done((bf16[144,1152]{1,0:T(8,128)(2,1)S(1)}, bf16[144,1152]{1,0:T(8,128)(2,1)S(1)}, u32[]{:S(2)}, u32[]{:S(2)}) %collective-permute-start.19) | collective-permute-done | bytes 331808 | tf_op jit(solution)/shard_map/ppermute | solution.py:252
  66.8 0.5 collective-permute-start.18
  68.2 0.5 collective-permute-done.5.near_ref
  68.8 1.5 %shard_map.64 = bf16[128,2240]{1,0:T(8,128)(2,1)} custom-call(s32[3]{0:T(128)S(1)} %pad_add_fusion.at_ref, f32[256,128]{1,0:T(8,128)S(1)} %get-tuple-element.17.square_ref, f32[128,128]{1,0:T(8,128)S(1)} %collective-permute-done.5.near_ref, f32[128,1152]{1,0:T(8,128)S(1)} %shard_map.59.mine_ref, bf16[128,1152]{1,0:T(8,128)(2,1)S(1)} %collective-permute-done.18.got_mine_ref, ...), custom_call_target="tpu_custom_call" | custom-call | bytes 1949708 | tf_op jit(solution)/shard_map/pallas_call | solution.py:28
  (38 shorter events, 2.4 us)
Async XLA Ops:
  0.1 1.1 %copy-start.1 = (bf16[1,4,32,2240]{3,2,1,0:T(8,128)(2,1)S(1)}, bf16[1,4,32,2240]{3,2,1,0:T(8,128)(2,1)}, u32[]{:S(2)}) copy-start(bf16[1,4,32,2240]{3,2,1,0:T(8,128)(2,1)} %param.6) | copy-start | bytes 1720324
  1.1 1.1 %copy-start.2 = (bf16[1,4,32,2240]{3,2,1,0:T(8,128)(2,1)S(1)}, bf16[1,4,32,2240]{3,2,1,0:T(8,128)(2,1)}, u32[]{:S(2)}) copy-start(bf16[1,4,32,2240]{3,2,1,0:T(8,128)(2,1)} %param.7) | copy-start | bytes 1720324
  2.2 21.8 %copy-start.3 = (bf16[1,4,32,2240]{3,2,1,0:T(8,128)(2,1)S(1)}, bf16[1,4,32,2240]{3,2,1,0:T(8,128)(2,1)}, u32[]{:S(2)}) copy-start(bf16[1,4,32,2240]{3,2,1,0:T(8,128)(2,1)} %param.5) | copy-start | bytes 1720324
  3.2 5.4 %collective-permute-start.1 = (f32[40,1152]{1,0:T(8,128)S(1)}, f32[40,1152]{1,0:T(8,128)S(1)}, u32[]{:S(2)}, u32[]{:S(2)}) collective-permute-start(f32[40,1152]{1,0:T(8,128)S(1)} %get-tuple-element.16), channel_id=1, source_target_pairs={{0,1},{1,0},{2,3},{3,2},{4,5},{5,4},{6,7},{7,6},{8,9},{9,8},{10,11... | collective-permute-start | bytes 552968 | tf_op jit(solution)/shard_map/ppermute | solution.py:255
  3.8 1.3 %copy-start = (bf16[1,1,313600]{2,1,0:T(2,128)(2,1)S(1)}, bf16[1,1,313600]{2,1,0:T(2,128)(2,1)}, u32[]{:S(2)}) copy-start(bf16[1,1,313600]{2,1,0:T(2,128)(2,1)} %w_ref.1) | copy-start | bytes 1881604
  5.1 51.6 %copy-start.4 = (f32[2240]{0:T(1024)S(1)}, f32[2240]{0:T(1024)}, u32[]{:S(2)}) copy-start(f32[2240]{0:T(1024)} %param.8) | copy-start | bytes 26884
  6.1 12.1 %collective-permute-start.7 = (bf16[144,1152]{1,0:T(8,128)(2,1)S(1)}, bf16[144,1152]{1,0:T(8,128)(2,1)S(1)}, u32[]{:S(2)}, u32[]{:S(2)}) collective-permute-start(bf16[144,1152]{1,0:T(8,128)(2,1)S(1)} %get-tuple-element.19.refs_0_), channel_id=1, source_target_pairs={{0,4},{2,6},{4,12},{6,14},{12,8},{14,10},{8,0},{10,2},{1,5},{3,7},... | collective-permute-start | bytes 995336 | tf_op jit(solution)/shard_map/ppermute | solution.py:278
  8.7 10.3 %collective-permute-start.2 = (bf16[40,1152]{1,0:T(8,128)(2,1)S(1)}, bf16[40,1152]{1,0:T(8,128)(2,1)S(1)}, u32[]{:S(2)}, u32[]{:S(2)}) collective-permute-start(bf16[40,1152]{1,0:T(8,128)(2,1)S(1)} %get-tuple-element.25), channel_id=1, source_target_pairs={{0,2},{2,0},{4,6},{6,4},{8,10},{10,8},{12,14},{14,12},{1,3},{3,1},... | collective-permute-start | bytes 276488 | tf_op jit(solution)/shard_map/ppermute | solution.py:252
  18.2 13.8 %collective-permute-start.9 = (bf16[144,1152]{1,0:T(8,128)(2,1)S(1)}, bf16[144,1152]{1,0:T(8,128)(2,1)S(1)}, u32[]{:S(2)}, u32[]{:S(2)}) collective-permute-start(bf16[144,1152]{1,0:T(8,128)(2,1)S(1)} %collective-permute-done.7.refs_2_), channel_id=1, source_target_pairs={{0,4},{2,6},{4,12},{6,14},{12,8},{14,10},{8,0},{10,2},{1,5},{3,7},... | collective-permute-start | bytes 995336 | tf_op jit(solution)/shard_map/ppermute | solution.py:278
  19.0 11.6 %collective-permute-start.3 = (bf16[40,1152]{1,0:T(8,128)(2,1)S(1)}, bf16[40,1152]{1,0:T(8,128)(2,1)S(1)}, u32[]{:S(2)}, u32[]{:S(2)}) collective-permute-start(bf16[40,1152]{1,0:T(8,128)(2,1)S(1)} %fusion), channel_id=1, source_target_pairs={{0,4},{2,6},{4,0},{6,2},{8,12},{10,14},{12,8},{14,10},{1,5},{3,7},... | collective-permute-start | bytes 276488 | tf_op jit(solution)/shard_map/ppermute | solution.py:252
  22.5 10.7 %collective-permute-start.6 = (bf16[144,1152]{1,0:T(8,128)(2,1)S(1)}, bf16[144,1152]{1,0:T(8,128)(2,1)S(1)}, u32[]{:S(2)}, u32[]{:S(2)}) collective-permute-start(bf16[144,1152]{1,0:T(8,128)(2,1)S(1)} %get-tuple-element.19.refs_0_), channel_id=1, source_target_pairs={{0,2},{2,0},{4,6},{6,4},{8,10},{10,8},{12,14},{14,12},{1,3},{3,1},... | collective-permute-start | bytes 995336 | tf_op jit(solution)/shard_map/ppermute | solution.py:252
  24.0 23.8 %collective-permute-start = (bf16[1,4,32,2240]{3,2,1,0:T(8,128)(2,1)S(1)}, bf16[1,4,32,2240]{3,2,1,0:T(8,128)(2,1)S(1)}, u32[]{:S(2)}, u32[]{:S(2)}) collective-permute-start(bf16[1,4,32,2240]{3,2,1,0:T(8,128)(2,1)S(1)} %copy-done.3), channel_id=1, source_target_pairs={{0,1},{1,0},{2,3},{3,2},{4,5},{5,4},{6,7},{7,6},{8,9},{9,8},{10,11... | collective-permute-start | bytes 1720328 | tf_op jit(solution)/shard_map/ppermute | solution.py:255
  24.0 14.4 %collective-permute-start.12 = (bf16[144,1152]{1,0:T(8,128)(2,1)S(1)}, bf16[144,1152]{1,0:T(8,128)(2,1)S(1)}, u32[]{:S(2)}, u32[]{:S(2)}) collective-permute-start(bf16[144,1152]{1,0:T(8,128)(2,1)S(1)} %get-tuple-element.20.refs_7_), channel_id=1, source_target_pairs={{0,2},{2,0},{4,6},{6,4},{8,10},{10,8},{12,14},{14,12},{1,3},{3,1},... | collective-permute-start | bytes 995336 | tf_op jit(solution)/shard_map/ppermute | solution.py:252
  30.7 16.1 %collective-permute-start.13 = (bf16[144,1152]{1,0:T(8,128)(2,1)S(1)}, bf16[144,1152]{1,0:T(8,128)(2,1)S(1)}, u32[]{:S(2)}, u32[]{:S(2)}) collective-permute-start(bf16[144,1152]{1,0:T(8,128)(2,1)S(1)} %collective-permute-done.7.refs_2_), channel_id=1, source_target_pairs={{0,16},{16,0},{1,17},{17,1},{2,18},{18,2},{3,19},{19,3},{4,20},{20... | collective-permute-start | bytes 995336 | tf_op jit(solution)/shard_map/ppermute | solution.py:255
  31.9 13.3 %collective-permute-start.10 = (bf16[144,1152]{1,0:T(8,128)(2,1)S(1)}, bf16[144,1152]{1,0:T(8,128)(2,1)S(1)}, u32[]{:S(2)}, u32[]{:S(2)}) collective-permute-start(bf16[144,1152]{1,0:T(8,128)(2,1)S(1)} %collective-permute-done.9.refs_4_), channel_id=1, source_target_pairs={{0,4},{2,6},{4,12},{6,14},{12,8},{14,10},{8,0},{10,2},{1,5},{3,7},... | collective-permute-start | bytes 995336 | tf_op jit(solution)/shard_map/ppermute | solution.py:278
  33.1 13.6 %collective-permute-start.4 = (bf16[40,1152]{1,0:T(8,128)(2,1)S(1)}, bf16[40,1152]{1,0:T(8,128)(2,1)S(1)}, u32[]{:S(2)}, u32[]{:S(2)}) collective-permute-start(bf16[40,1152]{1,0:T(8,128)(2,1)S(1)} %add_convert_fusion), channel_id=1, source_target_pairs={{0,8},{2,10},{4,12},{6,14},{8,0},{10,2},{12,4},{14,6},{1,9},{3,11}... | collective-permute-start | bytes 276488 | tf_op jit(solution)/shard_map/ppermute | solution.py:252
  38.4 9.9 %collective-permute-start.15 = (bf16[144,1152]{1,0:T(8,128)(2,1)S(1)}, bf16[144,1152]{1,0:T(8,128)(2,1)S(1)}, u32[]{:S(2)}, u32[]{:S(2)}) collective-permute-start(bf16[144,1152]{1,0:T(8,128)(2,1)S(1)} %collective-permute-done.9.refs_4_), channel_id=1, source_target_pairs={{0,16},{16,0},{1,17},{17,1},{2,18},{18,2},{3,19},{19,3},{4,20},{20... | collective-permute-start | bytes 995336 | tf_op jit(solution)/shard_map/ppermute | solution.py:255
  45.2 10.7 %collective-permute-start.11 = (bf16[144,1152]{1,0:T(8,128)(2,1)S(1)}, bf16[144,1152]{1,0:T(8,128)(2,1)S(1)}, u32[]{:S(2)}, u32[]{:S(2)}) collective-permute-start(bf16[144,1152]{1,0:T(8,128)(2,1)S(1)} %collective-permute-done.10.refs_5_), channel_id=1, source_target_pairs={{0,2},{2,0},{4,6},{6,4},{8,10},{10,8},{12,14},{14,12},{1,3},{3,1},... | collective-permute-start | bytes 995336 | tf_op jit(solution)/shard_map/ppermute | solution.py:252
  46.7 9.9 %collective-permute-start.8 = (bf16[144,1152]{1,0:T(8,128)(2,1)S(1)}, bf16[144,1152]{1,0:T(8,128)(2,1)S(1)}, u32[]{:S(2)}, u32[]{:S(2)}) collective-permute-start(bf16[144,1152]{1,0:T(8,128)(2,1)S(1)} %collective-permute-done.6.refs_1_), channel_id=1, source_target_pairs={{0,4},{2,6},{4,12},{6,14},{12,8},{14,10},{8,0},{10,2},{1,5},{3,7},... | collective-permute-start | bytes 995336 | tf_op jit(solution)/shard_map/ppermute | solution.py:281
  46.8 15.8 %collective-permute-start.14 = (bf16[144,1152]{1,0:T(8,128)(2,1)S(1)}, bf16[144,1152]{1,0:T(8,128)(2,1)S(1)}, u32[]{:S(2)}, u32[]{:S(2)}) collective-permute-start(bf16[144,1152]{1,0:T(8,128)(2,1)S(1)} %collective-permute-done.13.refs_9_), channel_id=1, source_target_pairs={{0,2},{2,0},{4,6},{6,4},{8,10},{10,8},{12,14},{14,12},{1,3},{3,1},... | collective-permute-start | bytes 995336 | tf_op jit(solution)/shard_map/ppermute | solution.py:252
  47.7 14.8 %collective-permute-start.16 = (bf16[144,1152]{1,0:T(8,128)(2,1)S(1)}, bf16[144,1152]{1,0:T(8,128)(2,1)S(1)}, u32[]{:S(2)}, u32[]{:S(2)}) collective-permute-start(bf16[144,1152]{1,0:T(8,128)(2,1)S(1)} %collective-permute-done.10.refs_5_), channel_id=1, source_target_pairs={{0,16},{16,0},{1,17},{17,1},{2,18},{18,2},{3,19},{19,3},{4,20},{20... | collective-permute-start | bytes 995336 | tf_op jit(solution)/shard_map/ppermute | solution.py:255
  48.2 17.8 %collective-permute-start.19 = (bf16[144,1152]{1,0:T(8,128)(2,1)S(1)}, bf16[144,1152]{1,0:T(8,128)(2,1)S(1)}, u32[]{:S(2)}, u32[]{:S(2)}) collective-permute-start(bf16[144,1152]{1,0:T(8,128)(2,1)S(1)} %collective-permute-done.15.refs_11_), channel_id=1, source_target_pairs={{0,2},{2,0},{4,6},{6,4},{8,10},{10,8},{12,14},{14,12},{1,3},{3,1},... | collective-permute-start | bytes 995336 | tf_op jit(solution)/shard_map/ppermute | solution.py:252
  55.9 10.2 %collective-permute-start.20 = (bf16[144,1152]{1,0:T(8,128)(2,1)S(1)}, bf16[144,1152]{1,0:T(8,128)(2,1)S(1)}, u32[]{:S(2)}, u32[]{:S(2)}) collective-permute-start(bf16[144,1152]{1,0:T(8,128)(2,1)S(1)} %collective-permute-done.11.refs_6_), channel_id=1, source_target_pairs={{0,16},{16,0},{1,17},{17,1},{2,18},{18,2},{3,19},{19,3},{4,20},{20... | collective-permute-start | bytes 995336 | tf_op jit(solution)/shard_map/ppermute | solution.py:255
  56.7 9.9 %collective-permute-start.17 = (bf16[144,1152]{1,0:T(8,128)(2,1)S(1)}, bf16[144,1152]{1,0:T(8,128)(2,1)S(1)}, u32[]{:S(2)}, u32[]{:S(2)}) collective-permute-start(bf16[144,1152]{1,0:T(8,128)(2,1)S(1)} %collective-permute-done.8.refs_3_), channel_id=1, source_target_pairs={{0,4},{2,6},{4,12},{6,14},{12,8},{14,10},{8,0},{10,2},{1,5},{3,7},... | collective-permute-start | bytes 995336 | tf_op jit(solution)/shard_map/ppermute | solution.py:281
  66.5 2.2 %collective-permute-start.21 = (bf16[128,1152]{1,0:T(8,128)(2,1)S(1)}, bf16[128,1152]{1,0:T(8,128)(2,1)S(1)}, u32[]{:S(2)}, u32[]{:S(2)}) collective-permute-start(bf16[128,1152]{1,0:T(8,128)(2,1)S(1)} %shard_map.62), channel_id=1, source_target_pairs={{0,1},{1,0},{2,3},{3,2},{4,5},{5,4},{6,7},{7,6},{8,9},{9,8},{10,11... | collective-permute-start | bytes 884744 | tf_op jit(solution)/shard_map/ppermute | solution.py:255
  66.8 2.0 %collective-permute-start.18 = (bf16[128,1152]{1,0:T(8,128)(2,1)S(1)}, bf16[128,1152]{1,0:T(8,128)(2,1)S(1)}, u32[]{:S(2)}, u32[]{:S(2)}) collective-permute-start(bf16[128,1152]{1,0:T(8,128)(2,1)S(1)} %shard_map.60), channel_id=1, source_target_pairs={{0,1},{1,0},{2,3},{3,2},{4,5},{5,4},{6,7},{7,6},{8,9},{9,8},{10,11... | collective-permute-start | bytes 884744 | tf_op jit(solution)/shard_map/ppermute | solution.py:255
  67.4 1.3 %collective-permute-start.5 = (f32[128,128]{1,0:T(8,128)S(1)}, f32[128,128]{1,0:T(8,128)S(1)}, u32[]{:S(2)}, u32[]{:S(2)}) collective-permute-start(f32[128,128]{1,0:T(8,128)S(1)} %slice.3), channel_id=1, source_target_pairs={{0,1},{1,0},{2,3},{3,2},{4,5},{5,4},{6,7},{7,6},{8,9},{9,8},{10,11... | collective-permute-start | bytes 196616 | tf_op jit(solution)/shard_map/ppermute | solution.py:255

commit v4 on v3

--- a/solution.py
+++ b/solution.py
@@ -20,16 +20,15 @@
     return -(-n // m) * m
 
 
-def call(kernel, out, args, scratch=(), flops=0, smem=0, mib=16, far_out=False):
+def call(kernel, out, args, scratch=(), flops=0, smem=0, mib=16):
     whole = pl.BlockSpec(memory_space=pltpu.VMEM)
     scalar = pl.BlockSpec(memory_space=pltpu.SMEM)
-    far = pl.BlockSpec(memory_space=pl.ANY)
     moved = sum(a.size * a.dtype.itemsize for a in jax.tree.leaves((args, out)))
     return pl.pallas_call(
         kernel,
         out_shape=out,
         in_specs=[scalar] * smem + [whole] * (len(args) - smem),
-        out_specs=jax.tree.map(lambda _: far if far_out else whole, out),
+        out_specs=jax.tree.map(lambda _: whole, out),
         scratch_shapes=list(scratch),
         compiler_params=pltpu.CompilerParams(vmem_limit_bytes=mib * 1024 * 1024),
         cost_estimate=pl.CostEstimate(flops=flops, bytes_accessed=moved, transcendentals=0),
@@ -203,38 +202,21 @@
     out_ref[...] = (total * lax.rsqrt(square / depth + norm_epsilon)).astype(jnp.bfloat16)
 
 
-def finish(
-    depth, at_ref, square_ref, near_ref, mine_ref, got_mine_ref, rest_ref, out_ref, wide, sems
-):
+def finish(depth, at_ref, square_ref, near_ref, mine_ref, got_mine_ref, rest_ref, out_ref):
     count, half = mine_ref.shape
-    each = count // sems.shape[0]
-
-    def store(i):
-        rows = pl.ds(i * each, each)
-        return pltpu.make_async_copy(wide.at[rows], out_ref.at[rows], sems.at[i])
-
-    def fill(mine_first):
-        for i in range(sems.shape[0]):
-            rows = slice(i * each, (i + 1) * each)
-            square = square_ref[rows, 0:1] + near_ref[rows, 0:1]
-            total = mine_ref[rows, :] + got_mine_ref[rows, :].astype(jnp.float32)
-            mine = (total * lax.rsqrt(square / depth + norm_epsilon)).astype(jnp.bfloat16)
-            rest = rest_ref[rows, :]
-            left, right = (mine, rest) if mine_first else (rest, mine)
-            wide[rows, 0:half] = left
-            wide[rows, half:depth] = right[:, : depth - half]
-            store(i).start()
+    square = square_ref[0:count, 0:1] + near_ref[:, 0:1]
+    total = mine_ref[...] + got_mine_ref[...].astype(jnp.float32)
+    mine = (total * lax.rsqrt(square / depth + norm_epsilon)).astype(jnp.bfloat16)
 
     @pl.when(at_ref[0] == 0)
     def _():
-        fill(True)
+        out_ref[:, 0:half] = mine
+        out_ref[:, half:depth] = rest_ref[:, : depth - half]
 
     @pl.when(at_ref[0] != 0)
     def _():
-        fill(False)
-
-    for i in range(sems.shape[0]):
-        store(i).wait()
+        out_ref[:, 0:half] = rest_ref[...]
+        out_ref[:, half:depth] = mine[:, : depth - half]
 
 
 def fast(query_tokens, key_tokens, value_tokens, norm_gain, out_weight):
@@ -362,9 +344,7 @@
         functools.partial(finish, depth),
         shape((count, depth), bf16),
         (at, square, near_square, *from_mine, rest_out),
-        scratch=[pltpu.VMEM((count, depth), bf16), pltpu.SemaphoreType.DMA((4,))],
         smem=1,
-        far_out=True,
     )
     return out.reshape(frames, rows, width, depth)
 
@@ -441,7 +421,6 @@
         and lax.axis_size("band") == 2
         and lax.axis_size("parts") == 2
         and peers > 2
-        and query_tokens.shape[1] * query_tokens.shape[2] % 64 == 0
         and peers & (peers - 1) == 0
         and out_weight.shape[-1] % depth == 0
         and depth % (2 * HD) == 0

time: 70.5 us -> 70.6 us (level)
  no operation moved by 1% of the time
where the time goes in v4:
time: 70.6 us; the launch traced here: 70.4 us
  waiting for transfers between devices  36.9 us (52%)
  starting transfers between devices  21.2 us (30%)
  Pallas kernels  8.49 us (12%)
  local copies, waits for them, and re-layouts  3.45 us (5%)
    ppermute x8, waiting for transfers between devices, flip(): return lax.ppermute(x, 'tm', [(i, i ^ mask) for i in range(peers)])  23.1 us
    ppermute x3, waiting for transfers between devices, fast(): mine[m] = lax.ppermute(mine[m - 2], 'tm', onward)  13.2 us
    ppermute x8, starting transfers between devices, flip(): return lax.ppermute(x, 'tm', [(i, i ^ mask) for i in range(peers)])  12.5 us
    pallas_call x10, Pallas kernels, call(): pl.pallas_call(kernel, out_shape=out, in_specs=[scalar] * smem + [whole]...  8.49 us
    ppermute x9, starting transfers between devices, across(): return lax.ppermute(x, axis, swap)  5.32 us
    ppermute x3, starting transfers between devices, fast(): mine[m] = lax.ppermute(mine[m - 2], 'tm', onward)  3.46 us
    unnamed x10, local copies, waits for them, and re-layouts  3.43 us
  transfers between devices with their start and end apart: 22, of which 9 were waited for; matrix products, arithmetic and copies ran while one was open for 0% of the time, Pallas kernels for 8%

profile of v4, /device:TPU:0, one launch (start us, length us, event | category | flops | bytes accessed | tf_op | source)
XLA Modules:
  0.0 70.4 jit_solution(195816417166374276)
XLA Ops:
  0.1 1.1 %copy-done.1 = bf16[1,4,32,2240]{3,2,1,0:T(8,128)(2,1)S(1)} copy-done((bf16[1,4,32,2240]{3,2,1,0:T(8,128)(2,1)S(1)}, bf16[1,4,32,2240]{3,2,1,0:T(8,128)(2,1)}, u32[]{:S(2)}) %copy-start.1) | copy-done | bytes 573464
  1.1 1.1 %copy-done.2 = bf16[1,4,32,2240]{3,2,1,0:T(8,128)(2,1)S(1)} copy-done((bf16[1,4,32,2240]{3,2,1,0:T(8,128)(2,1)S(1)}, bf16[1,4,32,2240]{3,2,1,0:T(8,128)(2,1)}, u32[]{:S(2)}) %copy-start.2) | copy-done | bytes 573464
  2.2 1.0 %shard_map.55 = (f32[40,1152]{1,0:T(8,128)S(1)}, f32[40,1152]{1,0:T(8,128)S(1)}) custom-call(s32[3]{0:T(128)S(1)} %pad_add_fusion.at_ref, bf16[128,2240]{1,0:T(8,128)(2,1)S(1)} %bitcast.8, bf16[128,2240]{1,0:T(8,128)(2,1)S(1)} %bitcast.9), custom_call_target="tpu_custom_call" | custom-call | flops 73400320 | bytes 1515532 | tf_op jit(solution)/shard_map/pallas_call | solution.py:27
  3.2 0.6 collective-permute-start.1
  3.8 1.3 %copy-done = bf16[1,1,313600]{2,1,0:T(2,128)(2,1)S(1)} copy-done((bf16[1,1,313600]{2,1,0:T(2,128)(2,1)S(1)}, bf16[1,1,313600]{2,1,0:T(2,128)(2,1)}, u32[]{:S(2)}) %copy-start) | copy-done | bytes 627224
  5.1 1.0 %shard_map.57 = (bf16[144,1152]{1,0:T(8,128)(2,1)S(1)}, bf16[144,1152]{1,0:T(8,128)(2,1)S(1)}) custom-call(s32[3]{0:T(128)S(1)} %pad_add_fusion.at_ref, bf16[1,1,313600]{2,1,0:T(2,128)(2,1)S(1)} %copy-done), custom_call_target="tpu_custom_call" | custom-call | bytes 1290764 | tf_op jit(solution)/shard_map/pallas_call | solution.py:27
  6.1 2.6 %collective-permute-start.7 = (bf16[144,1152]{1,0:T(8,128)(2,1)S(1)}, bf16[144,1152]{1,0:T(8,128)(2,1)S(1)}, u32[]{:S(2)}, u32[]{:S(2)}) collective-permute-start(bf16[144,1152]{1,0:T(8,128)(2,1)S(1)} %get-tuple-element.19.refs_0_), channel_id=1, source_target_pairs={{0,4},{2,6},{4,12},{6,14},{12,8},{14,10},{8,0},{10,2},{1,5},{3,7},... | collective-permute-start | bytes 995336 | tf_op jit(solution)/shard_map/ppermute | solution.py:260
  8.7 1.6 %collective-permute-start.2 = (bf16[40,1152]{1,0:T(8,128)(2,1)S(1)}, bf16[40,1152]{1,0:T(8,128)(2,1)S(1)}, u32[]{:S(2)}, u32[]{:S(2)}) collective-permute-start(bf16[40,1152]{1,0:T(8,128)(2,1)S(1)} %get-tuple-element.25), channel_id=1, source_target_pairs={{0,2},{2,0},{4,6},{6,4},{8,10},{10,8},{12,14},{14,12},{1,3},{3,1},... | collective-permute-start | bytes 276488 | tf_op jit(solution)/shard_map/ppermute | solution.py:234
  10.3 7.9 %collective-permute-done.7.refs_2_ = bf16[144,1152]{1,0:T(8,128)(2,1)S(1)} collective-permute-done((bf16[144,1152]{1,0:T(8,128)(2,1)S(1)}, bf16[144,1152]{1,0:T(8,128)(2,1)S(1)}, u32[]{:S(2)}, u32[]{:S(2)}) %collective-permute-start.7) | collective-permute-done | bytes 331808 | tf_op jit(solution)/shard_map/ppermute | solution.py:260
  18.2 0.8 %collective-permute-start.9 = (bf16[144,1152]{1,0:T(8,128)(2,1)S(1)}, bf16[144,1152]{1,0:T(8,128)(2,1)S(1)}, u32[]{:S(2)}, u32[]{:S(2)}) collective-permute-start(bf16[144,1152]{1,0:T(8,128)(2,1)S(1)} %collective-permute-done.7.refs_2_), channel_id=1, source_target_pairs={{0,4},{2,6},{4,12},{6,14},{12,8},{14,10},{8,0},{10,2},{1,5},{3,7},... | collective-permute-start | bytes 995336 | tf_op jit(solution)/shard_map/ppermute | solution.py:260
  19.0 3.4 %collective-permute-start.3 = (bf16[40,1152]{1,0:T(8,128)(2,1)S(1)}, bf16[40,1152]{1,0:T(8,128)(2,1)S(1)}, u32[]{:S(2)}, u32[]{:S(2)}) collective-permute-start(bf16[40,1152]{1,0:T(8,128)(2,1)S(1)} %fusion), channel_id=1, source_target_pairs={{0,4},{2,6},{4,0},{6,2},{8,12},{10,14},{12,8},{14,10},{1,5},{3,7},... | collective-permute-start | bytes 276488 | tf_op jit(solution)/shard_map/ppermute | solution.py:234
  22.5 1.5 %collective-permute-start.6 = (bf16[144,1152]{1,0:T(8,128)(2,1)S(1)}, bf16[144,1152]{1,0:T(8,128)(2,1)S(1)}, u32[]{:S(2)}, u32[]{:S(2)}) collective-permute-start(bf16[144,1152]{1,0:T(8,128)(2,1)S(1)} %get-tuple-element.19.refs_0_), channel_id=1, source_target_pairs={{0,2},{2,0},{4,6},{6,4},{8,10},{10,8},{12,14},{14,12},{1,3},{3,1},... | collective-permute-start | bytes 995336 | tf_op jit(solution)/shard_map/ppermute | solution.py:234
  24.0 0.5 collective-permute-start.12
  24.5 6.2 %collective-permute-done.3.refs_1_ = bf16[40,1152]{1,0:T(8,128)(2,1)S(1)} collective-permute-done((bf16[40,1152]{1,0:T(8,128)(2,1)S(1)}, bf16[40,1152]{1,0:T(8,128)(2,1)S(1)}, u32[]{:S(2)}, u32[]{:S(2)}) %collective-permute-start.3) | collective-permute-done | bytes 92192 | tf_op jit(solution)/shard_map/ppermute | solution.py:234
  30.7 1.3 %collective-permute-start.13 = (bf16[144,1152]{1,0:T(8,128)(2,1)S(1)}, bf16[144,1152]{1,0:T(8,128)(2,1)S(1)}, u32[]{:S(2)}, u32[]{:S(2)}) collective-permute-start(bf16[144,1152]{1,0:T(8,128)(2,1)S(1)} %collective-permute-done.7.refs_2_), channel_id=1, source_target_pairs={{0,16},{16,0},{1,17},{17,1},{2,18},{18,2},{3,19},{19,3},{4,20},{20... | collective-permute-start | bytes 995336 | tf_op jit(solution)/shard_map/ppermute | solution.py:237
  32.0 1.1 %collective-permute-done.6.refs_1_ = bf16[144,1152]{1,0:T(8,128)(2,1)S(1)} collective-permute-done((bf16[144,1152]{1,0:T(8,128)(2,1)S(1)}, bf16[144,1152]{1,0:T(8,128)(2,1)S(1)}, u32[]{:S(2)}, u32[]{:S(2)}) %collective-permute-start.6) | collective-permute-done | bytes 331808 | tf_op jit(solution)/shard_map/ppermute | solution.py:234
  33.1 1.8 %collective-permute-start.4 = (bf16[40,1152]{1,0:T(8,128)(2,1)S(1)}, bf16[40,1152]{1,0:T(8,128)(2,1)S(1)}, u32[]{:S(2)}, u32[]{:S(2)}) collective-permute-start(bf16[40,1152]{1,0:T(8,128)(2,1)S(1)} %add_convert_fusion), channel_id=1, source_target_pairs={{0,8},{2,10},{4,12},{6,14},{8,0},{10,2},{12,4},{14,6},{1,9},{3,11}... | collective-permute-start | bytes 276488 | tf_op jit(solution)/shard_map/ppermute | solution.py:234
  35.0 3.4 %collective-permute-done.12.refs_8_ = bf16[144,1152]{1,0:T(8,128)(2,1)S(1)} collective-permute-done((bf16[144,1152]{1,0:T(8,128)(2,1)S(1)}, bf16[144,1152]{1,0:T(8,128)(2,1)S(1)}, u32[]{:S(2)}, u32[]{:S(2)}) %collective-permute-start.12) | collective-permute-done | bytes 331808 | tf_op jit(solution)/shard_map/ppermute | solution.py:234
  38.4 1.5 %collective-permute-start.15 = (bf16[144,1152]{1,0:T(8,128)(2,1)S(1)}, bf16[144,1152]{1,0:T(8,128)(2,1)S(1)}, u32[]{:S(2)}, u32[]{:S(2)}) collective-permute-start(bf16[144,1152]{1,0:T(8,128)(2,1)S(1)} %collective-permute-done.9.refs_4_), channel_id=1, source_target_pairs={{0,16},{16,0},{1,17},{17,1},{2,18},{18,2},{3,19},{19,3},{4,20},{20... | collective-permute-start | bytes 995336 | tf_op jit(solution)/shard_map/ppermute | solution.py:237
  39.9 5.4 %collective-permute-done.10.refs_5_ = bf16[144,1152]{1,0:T(8,128)(2,1)S(1)} collective-permute-done((bf16[144,1152]{1,0:T(8,128)(2,1)S(1)}, bf16[144,1152]{1,0:T(8,128)(2,1)S(1)}, u32[]{:S(2)}, u32[]{:S(2)}) %collective-permute-start.10) | collective-permute-done | bytes 331808 | tf_op jit(solution)/shard_map/ppermute | solution.py:260
  45.2 1.5 %collective-permute-start.11 = (bf16[144,1152]{1,0:T(8,128)(2,1)S(1)}, bf16[144,1152]{1,0:T(8,128)(2,1)S(1)}, u32[]{:S(2)}, u32[]{:S(2)}) collective-permute-start(bf16[144,1152]{1,0:T(8,128)(2,1)S(1)} %collective-permute-done.10.refs_5_), channel_id=1, source_target_pairs={{0,2},{2,0},{4,6},{6,4},{8,10},{10,8},{12,14},{14,12},{1,3},{3,1},... | collective-permute-start | bytes 995336 | tf_op jit(solution)/shard_map/ppermute | solution.py:234
  46.8 1.0 %collective-permute-start.14 = (bf16[144,1152]{1,0:T(8,128)(2,1)S(1)}, bf16[144,1152]{1,0:T(8,128)(2,1)S(1)}, u32[]{:S(2)}, u32[]{:S(2)}) collective-permute-start(bf16[144,1152]{1,0:T(8,128)(2,1)S(1)} %collective-permute-done.13.refs_9_), channel_id=1, source_target_pairs={{0,2},{2,0},{4,6},{6,4},{8,10},{10,8},{12,14},{14,12},{1,3},{3,1},... | collective-permute-start | bytes 995336 | tf_op jit(solution)/shard_map/ppermute | solution.py:234
  48.2 1.1 %collective-permute-start.19 = (bf16[144,1152]{1,0:T(8,128)(2,1)S(1)}, bf16[144,1152]{1,0:T(8,128)(2,1)S(1)}, u32[]{:S(2)}, u32[]{:S(2)}) collective-permute-start(bf16[144,1152]{1,0:T(8,128)(2,1)S(1)} %collective-permute-done.15.refs_11_), channel_id=1, source_target_pairs={{0,2},{2,0},{4,6},{6,4},{8,10},{10,8},{12,14},{14,12},{1,3},{3,1},... | collective-permute-start | bytes 995336 | tf_op jit(solution)/shard_map/ppermute | solution.py:234
  49.4 6.6 %collective-permute-done.11.refs_6_ = bf16[144,1152]{1,0:T(8,128)(2,1)S(1)} collective-permute-done((bf16[144,1152]{1,0:T(8,128)(2,1)S(1)}, bf16[144,1152]{1,0:T(8,128)(2,1)S(1)}, u32[]{:S(2)}, u32[]{:S(2)}) %collective-permute-start.11) | collective-permute-done | bytes 331808 | tf_op jit(solution)/shard_map/ppermute | solution.py:234
  55.9 0.7 %collective-permute-start.20 = (bf16[144,1152]{1,0:T(8,128)(2,1)S(1)}, bf16[144,1152]{1,0:T(8,128)(2,1)S(1)}, u32[]{:S(2)}, u32[]{:S(2)}) collective-permute-start(bf16[144,1152]{1,0:T(8,128)(2,1)S(1)} %collective-permute-done.11.refs_6_), channel_id=1, source_target_pairs={{0,16},{16,0},{1,17},{17,1},{2,18},{18,2},{3,19},{19,3},{4,20},{20... | collective-permute-start | bytes 995336 | tf_op jit(solution)/shard_map/ppermute | solution.py:237
  56.7 2.0 %shard_map.56 = (bf16[256,1152]{1,0:T(8,128)(2,1)S(1)}, f32[256,128]{1,0:T(8,128)S(1)}) custom-call(s32[3]{0:T(128)S(1)} %pad_add_fusion.at_ref, bf16[128,2240]{1,0:T(8,128)(2,1)S(1)} %bitcast.10, bf16[128,2240]{1,0:T(8,128)(2,1)S(1)} %bitcast.11, f32[1,2240]{1,0:T(1,128)S(1)} %reshape.20.g_ref, f32[40,1152]{1,0:T(8,128)S(1)} %get-tuple-element.26.total_ref, ...), custom_call_target="tpu_custom_call" | custom-call | flops 150994944 | bytes 2337548 | tf_op jit(solution)/shard_map/pallas_call | solution.py:27
  58.7 3.8 %collective-permute-done.14.refs_10_ = bf16[144,1152]{1,0:T(8,128)(2,1)S(1)} collective-permute-done((bf16[144,1152]{1,0:T(8,128)(2,1)S(1)}, bf16[144,1152]{1,0:T(8,128)(2,1)S(1)}, u32[]{:S(2)}, u32[]{:S(2)}) %collective-permute-start.14) | collective-permute-done | bytes 331808 | tf_op jit(solution)/shard_map/ppermute | solution.py:234
  62.5 1.5 %shard_map.58 = (f32[128,1152]{1,0:T(8,128)S(1)}, f32[128,1152]{1,0:T(8,128)S(1)}, f32[128,1152]{1,0:T(8,128)S(1)}, f32[128,1152]{1,0:T(8,128)S(1)}) custom-call(bf16[256,1152]{1,0:T(8,128)(2,1)S(1)} %get-tuple-element.18.left_ref, bf16[144,1152]{1,0:T(8,128)(2,1)S(1)} %get-tuple-element.19.refs_0_, bf16[144,1152]{1,0:T(8,128)(2,1)S(1)} %collective-permute-done.6.refs_1_, ...), custom_call_target="tpu_custom_call" | custom-call | flops 1104150528 | bytes 7262208 | tf_op jit(solution)/shard_map/pallas_call | solution.py:27
  64.1 2.0 %collective-permute-done.19.refs_0_ = bf16[144,1152]{1,0:T(8,128)(2,1)S(1)} collective-permute-done((bf16[144,1152]{1,0:T(8,128)(2,1)S(1)}, bf16[144,1152]{1,0:T(8,128)(2,1)S(1)}, u32[]{:S(2)}, u32[]{:S(2)}) %collective-permute-start.19) | collective-permute-done | bytes 331808 | tf_op jit(solution)/shard_map/ppermute | solution.py:234
  66.8 0.5 collective-permute-start.18
  68.2 0.5 collective-permute-done.5.near_ref
  68.8 1.5 %shard_map.64 = bf16[128,2240]{1,0:T(8,128)(2,1)} custom-call(s32[3]{0:T(128)S(1)} %pad_add_fusion.at_ref, f32[256,128]{1,0:T(8,128)S(1)} %get-tuple-element.17.square_ref, f32[128,128]{1,0:T(8,128)S(1)} %collective-permute-done.5.near_ref, f32[128,1152]{1,0:T(8,128)S(1)} %shard_map.59.mine_ref, bf16[128,1152]{1,0:T(8,128)(2,1)S(1)} %collective-permute-done.18.got_mine_ref, ...), custom_call_target="tpu_custom_call" | custom-call | bytes 1949708 | tf_op jit(solution)/shard_map/pallas_call | solution.py:27
  (38 shorter events, 2.4 us)
Async XLA Ops:
  0.1 1.1 %copy-start.1 = (bf16[1,4,32,2240]{3,2,1,0:T(8,128)(2,1)S(1)}, bf16[1,4,32,2240]{3,2,1,0:T(8,128)(2,1)}, u32[]{:S(2)}) copy-start(bf16[1,4,32,2240]{3,2,1,0:T(8,128)(2,1)} %param.6) | copy-start | bytes 1720324
  1.1 1.1 %copy-start.2 = (bf16[1,4,32,2240]{3,2,1,0:T(8,128)(2,1)S(1)}, bf16[1,4,32,2240]{3,2,1,0:T(8,128)(2,1)}, u32[]{:S(2)}) copy-start(bf16[1,4,32,2240]{3,2,1,0:T(8,128)(2,1)} %param.7) | copy-start | bytes 1720324
  2.2 21.8 %copy-start.3 = (bf16[1,4,32,2240]{3,2,1,0:T(8,128)(2,1)S(1)}, bf16[1,4,32,2240]{3,2,1,0:T(8,128)(2,1)}, u32[]{:S(2)}) copy-start(bf16[1,4,32,2240]{3,2,1,0:T(8,128)(2,1)} %param.5) | copy-start | bytes 1720324
  3.2 5.4 %collective-permute-start.1 = (f32[40,1152]{1,0:T(8,128)S(1)}, f32[40,1152]{1,0:T(8,128)S(1)}, u32[]{:S(2)}, u32[]{:S(2)}) collective-permute-start(f32[40,1152]{1,0:T(8,128)S(1)} %get-tuple-element.16), channel_id=1, source_target_pairs={{0,1},{1,0},{2,3},{3,2},{4,5},{5,4},{6,7},{7,6},{8,9},{9,8},{10,11... | collective-permute-start | bytes 552968 | tf_op jit(solution)/shard_map/ppermute | solution.py:237
  3.8 1.3 %copy-start = (bf16[1,1,313600]{2,1,0:T(2,128)(2,1)S(1)}, bf16[1,1,313600]{2,1,0:T(2,128)(2,1)}, u32[]{:S(2)}) copy-start(bf16[1,1,313600]{2,1,0:T(2,128)(2,1)} %w_ref.1) | copy-start | bytes 1881604
  5.1 51.6 %copy-start.4 = (f32[2240]{0:T(1024)S(1)}, f32[2240]{0:T(1024)}, u32[]{:S(2)}) copy-start(f32[2240]{0:T(1024)} %param.8) | copy-start | bytes 26884
  6.1 12.1 %collective-permute-start.7 = (bf16[144,1152]{1,0:T(8,128)(2,1)S(1)}, bf16[144,1152]{1,0:T(8,128)(2,1)S(1)}, u32[]{:S(2)}, u32[]{:S(2)}) collective-permute-start(bf16[144,1152]{1,0:T(8,128)(2,1)S(1)} %get-tuple-element.19.refs_0_), channel_id=1, source_target_pairs={{0,4},{2,6},{4,12},{6,14},{12,8},{14,10},{8,0},{10,2},{1,5},{3,7},... | collective-permute-start | bytes 995336 | tf_op jit(solution)/shard_map/ppermute | solution.py:260
  8.7 10.3 %collective-permute-start.2 = (bf16[40,1152]{1,0:T(8,128)(2,1)S(1)}, bf16[40,1152]{1,0:T(8,128)(2,1)S(1)}, u32[]{:S(2)}, u32[]{:S(2)}) collective-permute-start(bf16[40,1152]{1,0:T(8,128)(2,1)S(1)} %get-tuple-element.25), channel_id=1, source_target_pairs={{0,2},{2,0},{4,6},{6,4},{8,10},{10,8},{12,14},{14,12},{1,3},{3,1},... | collective-permute-start | bytes 276488 | tf_op jit(solution)/shard_map/ppermute | solution.py:234
  18.2 13.8 %collective-permute-start.9 = (bf16[144,1152]{1,0:T(8,128)(2,1)S(1)}, bf16[144,1152]{1,0:T(8,128)(2,1)S(1)}, u32[]{:S(2)}, u32[]{:S(2)}) collective-permute-start(bf16[144,1152]{1,0:T(8,128)(2,1)S(1)} %collective-permute-done.7.refs_2_), channel_id=1, source_target_pairs={{0,4},{2,6},{4,12},{6,14},{12,8},{14,10},{8,0},{10,2},{1,5},{3,7},... | collective-permute-start | bytes 995336 | tf_op jit(solution)/shard_map/ppermute | solution.py:260
  19.0 11.6 %collective-permute-start.3 = (bf16[40,1152]{1,0:T(8,128)(2,1)S(1)}, bf16[40,1152]{1,0:T(8,128)(2,1)S(1)}, u32[]{:S(2)}, u32[]{:S(2)}) collective-permute-start(bf16[40,1152]{1,0:T(8,128)(2,1)S(1)} %fusion), channel_id=1, source_target_pairs={{0,4},{2,6},{4,0},{6,2},{8,12},{10,14},{12,8},{14,10},{1,5},{3,7},... | collective-permute-start | bytes 276488 | tf_op jit(solution)/shard_map/ppermute | solution.py:234
  22.5 10.7 %collective-permute-start.6 = (bf16[144,1152]{1,0:T(8,128)(2,1)S(1)}, bf16[144,1152]{1,0:T(8,128)(2,1)S(1)}, u32[]{:S(2)}, u32[]{:S(2)}) collective-permute-start(bf16[144,1152]{1,0:T(8,128)(2,1)S(1)} %get-tuple-element.19.refs_0_), channel_id=1, source_target_pairs={{0,2},{2,0},{4,6},{6,4},{8,10},{10,8},{12,14},{14,12},{1,3},{3,1},... | collective-permute-start | bytes 995336 | tf_op jit(solution)/shard_map/ppermute | solution.py:234
  24.0 23.8 %collective-permute-start = (bf16[1,4,32,2240]{3,2,1,0:T(8,128)(2,1)S(1)}, bf16[1,4,32,2240]{3,2,1,0:T(8,128)(2,1)S(1)}, u32[]{:S(2)}, u32[]{:S(2)}) collective-permute-start(bf16[1,4,32,2240]{3,2,1,0:T(8,128)(2,1)S(1)} %copy-done.3), channel_id=1, source_target_pairs={{0,1},{1,0},{2,3},{3,2},{4,5},{5,4},{6,7},{7,6},{8,9},{9,8},{10,11... | collective-permute-start | bytes 1720328 | tf_op jit(solution)/shard_map/ppermute | solution.py:237
  24.0 14.4 %collective-permute-start.12 = (bf16[144,1152]{1,0:T(8,128)(2,1)S(1)}, bf16[144,1152]{1,0:T(8,128)(2,1)S(1)}, u32[]{:S(2)}, u32[]{:S(2)}) collective-permute-start(bf16[144,1152]{1,0:T(8,128)(2,1)S(1)} %get-tuple-element.20.refs_7_), channel_id=1, source_target_pairs={{0,2},{2,0},{4,6},{6,4},{8,10},{10,8},{12,14},{14,12},{1,3},{3,1},... | collective-permute-start | bytes 995336 | tf_op jit(solution)/shard_map/ppermute | solution.py:234
  30.7 16.1 %collective-permute-start.13 = (bf16[144,1152]{1,0:T(8,128)(2,1)S(1)}, bf16[144,1152]{1,0:T(8,128)(2,1)S(1)}, u32[]{:S(2)}, u32[]{:S(2)}) collective-permute-start(bf16[144,1152]{1,0:T(8,128)(2,1)S(1)} %collective-permute-done.7.refs_2_), channel_id=1, source_target_pairs={{0,16},{16,0},{1,17},{17,1},{2,18},{18,2},{3,19},{19,3},{4,20},{20... | collective-permute-start | bytes 995336 | tf_op jit(solution)/shard_map/ppermute | solution.py:237
  31.9 13.3 %collective-permute-start.10 = (bf16[144,1152]{1,0:T(8,128)(2,1)S(1)}, bf16[144,1152]{1,0:T(8,128)(2,1)S(1)}, u32[]{:S(2)}, u32[]{:S(2)}) collective-permute-start(bf16[144,1152]{1,0:T(8,128)(2,1)S(1)} %collective-permute-done.9.refs_4_), channel_id=1, source_target_pairs={{0,4},{2,6},{4,12},{6,14},{12,8},{14,10},{8,0},{10,2},{1,5},{3,7},... | collective-permute-start | bytes 995336 | tf_op jit(solution)/shard_map/ppermute | solution.py:260
  33.1 13.6 %collective-permute-start.4 = (bf16[40,1152]{1,0:T(8,128)(2,1)S(1)}, bf16[40,1152]{1,0:T(8,128)(2,1)S(1)}, u32[]{:S(2)}, u32[]{:S(2)}) collective-permute-start(bf16[40,1152]{1,0:T(8,128)(2,1)S(1)} %add_convert_fusion), channel_id=1, source_target_pairs={{0,8},{2,10},{4,12},{6,14},{8,0},{10,2},{12,4},{14,6},{1,9},{3,11}... | collective-permute-start | bytes 276488 | tf_op jit(solution)/shard_map/ppermute | solution.py:234
  38.4 9.9 %collective-permute-start.15 = (bf16[144,1152]{1,0:T(8,128)(2,1)S(1)}, bf16[144,1152]{1,0:T(8,128)(2,1)S(1)}, u32[]{:S(2)}, u32[]{:S(2)}) collective-permute-start(bf16[144,1152]{1,0:T(8,128)(2,1)S(1)} %collective-permute-done.9.refs_4_), channel_id=1, source_target_pairs={{0,16},{16,0},{1,17},{17,1},{2,18},{18,2},{3,19},{19,3},{4,20},{20... | collective-permute-start | bytes 995336 | tf_op jit(solution)/shard_map/ppermute | solution.py:237
  45.2 10.7 %collective-permute-start.11 = (bf16[144,1152]{1,0:T(8,128)(2,1)S(1)}, bf16[144,1152]{1,0:T(8,128)(2,1)S(1)}, u32[]{:S(2)}, u32[]{:S(2)}) collective-permute-start(bf16[144,1152]{1,0:T(8,128)(2,1)S(1)} %collective-permute-done.10.refs_5_), channel_id=1, source_target_pairs={{0,2},{2,0},{4,6},{6,4},{8,10},{10,8},{12,14},{14,12},{1,3},{3,1},... | collective-permute-start | bytes 995336 | tf_op jit(solution)/shard_map/ppermute | solution.py:234
  46.7 9.9 %collective-permute-start.8 = (bf16[144,1152]{1,0:T(8,128)(2,1)S(1)}, bf16[144,1152]{1,0:T(8,128)(2,1)S(1)}, u32[]{:S(2)}, u32[]{:S(2)}) collective-permute-start(bf16[144,1152]{1,0:T(8,128)(2,1)S(1)} %collective-permute-done.6.refs_1_), channel_id=1, source_target_pairs={{0,4},{2,6},{4,12},{6,14},{12,8},{14,10},{8,0},{10,2},{1,5},{3,7},... | collective-permute-start | bytes 995336 | tf_op jit(solution)/shard_map/ppermute | solution.py:263
  46.8 15.8 %collective-permute-start.14 = (bf16[144,1152]{1,0:T(8,128)(2,1)S(1)}, bf16[144,1152]{1,0:T(8,128)(2,1)S(1)}, u32[]{:S(2)}, u32[]{:S(2)}) collective-permute-start(bf16[144,1152]{1,0:T(8,128)(2,1)S(1)} %collective-permute-done.13.refs_9_), channel_id=1, source_target_pairs={{0,2},{2,0},{4,6},{6,4},{8,10},{10,8},{12,14},{14,12},{1,3},{3,1},... | collective-permute-start | bytes 995336 | tf_op jit(solution)/shard_map/ppermute | solution.py:234
  47.7 14.8 %collective-permute-start.16 = (bf16[144,1152]{1,0:T(8,128)(2,1)S(1)}, bf16[144,1152]{1,0:T(8,128)(2,1)S(1)}, u32[]{:S(2)}, u32[]{:S(2)}) collective-permute-start(bf16[144,1152]{1,0:T(8,128)(2,1)S(1)} %collective-permute-done.10.refs_5_), channel_id=1, source_target_pairs={{0,16},{16,0},{1,17},{17,1},{2,18},{18,2},{3,19},{19,3},{4,20},{20... | collective-permute-start | bytes 995336 | tf_op jit(solution)/shard_map/ppermute | solution.py:237
  48.2 17.8 %collective-permute-start.19 = (bf16[144,1152]{1,0:T(8,128)(2,1)S(1)}, bf16[144,1152]{1,0:T(8,128)(2,1)S(1)}, u32[]{:S(2)}, u32[]{:S(2)}) collective-permute-start(bf16[144,1152]{1,0:T(8,128)(2,1)S(1)} %collective-permute-done.15.refs_11_), channel_id=1, source_target_pairs={{0,2},{2,0},{4,6},{6,4},{8,10},{10,8},{12,14},{14,12},{1,3},{3,1},... | collective-permute-start | bytes 995336 | tf_op jit(solution)/shard_map/ppermute | solution.py:234
  55.9 10.2 %collective-permute-start.20 = (bf16[144,1152]{1,0:T(8,128)(2,1)S(1)}, bf16[144,1152]{1,0:T(8,128)(2,1)S(1)}, u32[]{:S(2)}, u32[]{:S(2)}) collective-permute-start(bf16[144,1152]{1,0:T(8,128)(2,1)S(1)} %collective-permute-done.11.refs_6_), channel_id=1, source_target_pairs={{0,16},{16,0},{1,17},{17,1},{2,18},{18,2},{3,19},{19,3},{4,20},{20... | collective-permute-start | bytes 995336 | tf_op jit(solution)/shard_map/ppermute | solution.py:237
  56.7 9.9 %collective-permute-start.17 = (bf16[144,1152]{1,0:T(8,128)(2,1)S(1)}, bf16[144,1152]{1,0:T(8,128)(2,1)S(1)}, u32[]{:S(2)}, u32[]{:S(2)}) collective-permute-start(bf16[144,1152]{1,0:T(8,128)(2,1)S(1)} %collective-permute-done.8.refs_3_), channel_id=1, source_target_pairs={{0,4},{2,6},{4,12},{6,14},{12,8},{14,10},{8,0},{10,2},{1,5},{3,7},... | collective-permute-start | bytes 995336 | tf_op jit(solution)/shard_map/ppermute | solution.py:263
  66.5 2.2 %collective-permute-start.21 = (bf16[128,1152]{1,0:T(8,128)(2,1)S(1)}, bf16[128,1152]{1,0:T(8,128)(2,1)S(1)}, u32[]{:S(2)}, u32[]{:S(2)}) collective-permute-start(bf16[128,1152]{1,0:T(8,128)(2,1)S(1)} %shard_map.62), channel_id=1, source_target_pairs={{0,1},{1,0},{2,3},{3,2},{4,5},{5,4},{6,7},{7,6},{8,9},{9,8},{10,11... | collective-permute-start | bytes 884744 | tf_op jit(solution)/shard_map/ppermute | solution.py:237
  66.8 2.0 %collective-permute-start.18 = (bf16[128,1152]{1,0:T(8,128)(2,1)S(1)}, bf16[128,1152]{1,0:T(8,128)(2,1)S(1)}, u32[]{:S(2)}, u32[]{:S(2)}) collective-permute-start(bf16[128,1152]{1,0:T(8,128)(2,1)S(1)} %shard_map.60), channel_id=1, source_target_pairs={{0,1},{1,0},{2,3},{3,2},{4,5},{5,4},{6,7},{7,6},{8,9},{9,8},{10,11... | collective-permute-start | bytes 884744 | tf_op jit(solution)/shard_map/ppermute | solution.py:237
  67.4 1.3 %collective-permute-start.5 = (f32[128,128]{1,0:T(8,128)S(1)}, f32[128,128]{1,0:T(8,128)S(1)}, u32[]{:S(2)}, u32[]{:S(2)}) collective-permute-start(f32[128,128]{1,0:T(8,128)S(1)} %slice.3), channel_id=1, source_target_pairs={{0,1},{1,0},{2,3},{3,2},{4,5},{5,4},{6,7},{7,6},{8,9},{9,8},{10,11... | collective-permute-start | bytes 196616 | tf_op jit(solution)/shard_map/ppermute | solution.py:237
